TPU v7x, 32 devices: a whole 2x2x4 slice. The times are simulated.
32 devices in a mesh: img: 2 (over x), row: 4 (over y, core), col: 4 (over z).
Axes of the slice: x: 2, y: 2, z: 4, core: 2. Of those that a mesh axis runs over, the one named last changes fastest.
Arguments:
- latent: bfloat16 [8, 4, 64, 64], P('img', None, 'row', 'col'), may hold values from -6 to 6
- cotangent: bfloat16 [8, 8, 64, 64], P('img', None, 'row', 'col'), may hold values from -6 to 6
- cond: float32 [8, 4, 1152], P('img'), may hold values from -6 to 6
- canvas_kind: int32 [8], P('img'), may hold values from 0 to 1
- w_patch: bfloat16 [16, 1152], P('img'), may hold values from -1.5 to 1.5
- w_qkv: bfloat16 [1152, 3456], P('img'), may hold values from -0.1875 to 0.1875
- w_proj: bfloat16 [1152, 1152], P('img'), may hold values from -1.5 to 1.5
- w_up: bfloat16 [1152, 4608], P('img'), may hold values from -0.1875 to 0.1875
- w_down: bfloat16 [4608, 1152], P('img'), may hold values from -0.09375 to 0.09375
- w_ada: bfloat16 [1152, 6912], P('img'), may hold values from -0.1875 to 0.1875
- w_final_ada: bfloat16 [1152, 2304], P('img'), may hold values from -0.1875 to 0.1875
- w_out: bfloat16 [1152, 32], P('img'), may hold values from -0.1875 to 0.1875
Outputs:
- latent_out: float32 [8, 8, 64, 64], P('img', None, 'row', 'col')
- latent_grad: float32 [8, 4, 64, 64], P('img', None, 'row', 'col')
- cond_grad: float32 [8, 4, 1152], P('img')
- g_patch: float32 [16, 1152], P('img')
- g_qkv: float32 [1152, 3456], P('img')
- g_proj: float32 [1152, 1152], P('img')
- g_up: float32 [1152, 4608], P('img')
- g_down: float32 [4608, 1152], P('img')
- g_ada: float32 [1152, 6912], P('img')
- g_final_ada: float32 [1152, 2304], P('img')
- g_out: float32 [1152, 32], P('img')
Inputs may be any that keep to these rules, and one draw needn't show every extreme that they name: Canvas n holds one image of 64 x 64 latent pixels when canvas_kind[n] is 0, and four images of 32 x 32 latent pixels in its quadrants when it is 1; tokens attend only within their image, and only cond[n, 0] is used by a canvas of one image.
All inputs are finite; a program needn't handle non-finite values.
Results may differ from a plain program's by a relative error of at most 0.019.
Values may be sent and summed in bfloat16 or wider, within the bound.
No kernel may reach another device: no remote copies, remote signals or barrier semaphores. Data moves between devices by JAX's collectives and lax.ppermute only.
A program may use at most 248 MiB of HBM per device.

v0:
```python
import math

import jax
import jax.numpy as jnp
from jax import lax
from jax.sharding import PartitionSpec as P

HEADS = 16
MB = 2


def shifted(block, axis, distance):
    devices = range(lax.axis_size(axis))
    route = [((i - distance) % len(devices), i) for i in devices]
    return lax.ppermute(block, axis, route)


def layer_norm(value):
    center = value - jnp.mean(value, -1, keepdims=True)
    spread = jnp.mean(center * center, -1, keepdims=True)
    return center * lax.rsqrt(spread + 1e-06)


def modulate(value, shift, scale):
    return layer_norm(value) * (1.0 + scale[:, None, :]) + shift[:, None, :]


def gelu_tanh(value):
    return jax.nn.gelu(value, approximate=True)


def swish(value):
    return value * jax.nn.sigmoid(value)


def sincos(coord, count):
    freqs = 1.0 / 10000.0 ** (jnp.arange(count, dtype=jnp.float32) / count)
    angle = coord.astype(jnp.float32)[..., None] * freqs
    return jnp.concatenate([jnp.sin(angle), jnp.cos(angle)], axis=-1)


def transposed(left, right):
    return lax.dot_general(
        left, right, (((0,), (0,)), ((), ())), preferred_element_type=jnp.float32
    )


def against(left, weight):
    return lax.dot_general(
        left, weight, (((1,), (1,)), ((), ())), preferred_element_type=jnp.float32
    )


def group_heads(value, groups):
    count, length, heads, depth = value.shape
    return value.reshape(count, length, groups, heads // groups, depth).transpose(2, 0, 1, 3, 4)


def join_heads(value):
    groups, count, length, inner, depth = value.shape
    return value.transpose(1, 2, 0, 3, 4).reshape(count, length, groups * inner * depth)


def local(
    latent,
    cotangent,
    cond,
    canvas_kind,
    w_patch,
    w_qkv,
    w_proj,
    w_up,
    w_down,
    w_ada,
    w_final_ada,
    w_out,
):
    local_n, chans, tile_r, tile_c = latent.shape
    out_ch = cotangent.shape[1]
    width = cond.shape[2]
    rows_n = lax.axis_size("row")
    cols_n = lax.axis_size("col")
    row_at = lax.axis_index("row")
    col_at = lax.axis_index("col")
    patch_r = tile_r // 2
    patch_c = tile_c // 2
    tile_tok = patch_r * patch_c
    canvas_tok = tile_tok * rows_n * cols_n
    half = patch_r * rows_n // 2
    heads = HEADS
    head_dim = width // heads
    groups = heads // math.gcd(heads, 4)
    factor = head_dim ** (-0.5)
    per_batch = local_n // MB
    highest = lax.Precision.HIGHEST
    stacked = jnp.concatenate([latent, cotangent], axis=1)
    upper = shifted(stacked[:, :, -1:, :], "row", 1)
    framed = jnp.concatenate([upper, stacked[:, :, :-1, :]], axis=2)
    beside = shifted(framed[:, :, :, -1:], "col", 1)
    framed = jnp.concatenate([beside, framed[:, :, :, :-1]], axis=3)

    def to_tokens(tile):
        depth = tile.shape[1]
        shaped = tile.reshape(local_n, depth, patch_r, 2, patch_c, 2).transpose(0, 2, 4, 1, 3, 5)
        return shaped.reshape(local_n, tile_tok, depth * 4)

    def to_tile(tokens):
        depth = tokens.shape[2] // 4
        shaped = tokens.reshape(local_n, patch_r, patch_c, depth, 2, 2).transpose(0, 3, 1, 4, 2, 5)
        return shaped.reshape(local_n, depth, tile_r, tile_c)

    patches = to_tokens(framed[:, :chans])
    cot_tokens = to_tokens(framed[:, chans:])
    quad = row_at * 2 // rows_n * 2 + col_at * 2 // cols_n
    slot = canvas_kind * quad
    picker = (slot[:, None] == jnp.arange(4, dtype=jnp.int32)[None, :]).astype(jnp.float32)
    cond_sel = jnp.einsum("ns,nsd->nd", picker, cond, precision=highest)
    silu_all = swish(cond_sel).astype(jnp.bfloat16)
    prow = row_at * patch_r + jnp.arange(patch_r, dtype=jnp.int32)
    pcol = col_at * patch_c + jnp.arange(patch_c, dtype=jnp.int32)
    kind_grid = canvas_kind[:, None, None]
    lrow = prow[None, :, None] - kind_grid * (prow[None, :, None] // half) * half
    lcol = pcol[None, None, :] - kind_grid * (pcol[None, None, :] // half) * half
    lrow = jnp.broadcast_to(lrow, (local_n, patch_r, patch_c))
    lcol = jnp.broadcast_to(lcol, (local_n, patch_r, patch_c))
    positions = jnp.concatenate(
        [sincos(lcol, width // 4), sincos(lrow, width // 4)], axis=-1
    ).reshape(local_n, tile_tok, width)
    gindex = jnp.arange(canvas_tok, dtype=jnp.int32)
    source = gindex // tile_tok
    key_quad = source // cols_n * 2 // rows_n * 2 + source % cols_n * 2 // cols_n
    allowed = canvas_kind[:, None] * key_quad[None, :] == slot[:, None]
    totals = tuple(
        (
            jnp.zeros(item.shape, jnp.float32)
            for item in (w_patch, w_qkv, w_proj, w_up, w_down, w_ada, w_final_ada, w_out)
        )
    )
    outputs = []
    latent_parts = []
    cond_parts = []
    for part in range(MB):
        first = part * per_batch
        wp = lax.all_gather(w_patch, "img", axis=0, tiled=True)
        wq = lax.all_gather(w_qkv, "img", axis=0, tiled=True)
        wpr = lax.all_gather(w_proj, "img", axis=0, tiled=True)
        wu = lax.all_gather(w_up, "img", axis=0, tiled=True)
        wd = lax.all_gather(w_down, "img", axis=0, tiled=True)
        wa = lax.all_gather(w_ada, "img", axis=0, tiled=True)
        wf = lax.all_gather(w_final_ada, "img", axis=0, tiled=True)
        wout = lax.all_gather(w_out, "img", axis=0, tiled=True)
        span = slice(first, first + per_batch)
        rows = per_batch * tile_tok
        silu_b = silu_all[span]
        mods = jnp.dot(silu_b, wa, preferred_element_type=jnp.float32)
        fmods = jnp.dot(silu_b, wf, preferred_element_type=jnp.float32)
        shift1, scale1, gate1, shift2, scale2, gate2 = jnp.split(mods, 6, axis=-1)
        shiftf, scalef = jnp.split(fmods, 2, axis=-1)
        pieces = patches[span].reshape(rows, chans * 4)
        x0 = (
            jnp.dot(pieces, wp, preferred_element_type=jnp.float32).reshape(
                per_batch, tile_tok, width
            )
            + positions[span]
        )
        a1 = modulate(x0, shift1, scale1).astype(jnp.bfloat16)
        qkv = jnp.dot(a1.reshape(rows, width), wq, preferred_element_type=jnp.float32).astype(
            jnp.bfloat16
        )
        qkv = qkv.reshape(per_batch, tile_tok, 3 * width)
        keys = lax.all_gather(qkv[..., width : 2 * width], ("row", "col"), axis=1, tiled=True)
        values = lax.all_gather(qkv[..., 2 * width :], ("row", "col"), axis=1, tiled=True)
        qgroups = group_heads(
            qkv[..., :width].reshape(per_batch, tile_tok, heads, head_dim), groups
        )
        kgroups = group_heads(keys.reshape(per_batch, canvas_tok, heads, head_dim), groups)
        vgroups = group_heads(values.reshape(per_batch, canvas_tok, heads, head_dim), groups)
        mask = allowed[span][:, None, None, :]

        def scores(qpart, kpart):
            raw = (
                jnp.einsum("nqhd,nkhd->nhqk", qpart, kpart, preferred_element_type=jnp.float32)
                * factor
            )
            return jnp.where(mask, raw, -1e30)

        def attend(items):
            qpart, kpart, vpart = items
            logits = scores(qpart, kpart)
            top = jnp.max(logits, -1, keepdims=True)
            expd = jnp.exp(logits - top)
            total = jnp.sum(expd, -1, keepdims=True)
            prob = (expd / total).astype(jnp.bfloat16)
            out = jnp.einsum("nhqk,nkhd->nqhd", prob, vpart, preferred_element_type=jnp.float32)
            return (out, top + jnp.log(total))

        att_groups, lse_groups = lax.map(attend, (qgroups, kgroups, vgroups))
        att = join_heads(att_groups).astype(jnp.bfloat16).reshape(rows, width)
        proj = jnp.dot(att, wpr, preferred_element_type=jnp.float32).reshape(
            per_batch, tile_tok, width
        )
        x1 = x0 + gate1[:, None, :] * proj
        a2 = modulate(x1, shift2, scale2).astype(jnp.bfloat16).reshape(rows, width)
        pre = jnp.dot(a2, wu, preferred_element_type=jnp.float32)
        hid = gelu_tanh(pre).astype(jnp.bfloat16)
        down = jnp.dot(hid, wd, preferred_element_type=jnp.float32).reshape(
            per_batch, tile_tok, width
        )
        x2 = x1 + gate2[:, None, :] * down
        af = modulate(x2, shiftf, scalef).astype(jnp.bfloat16).reshape(rows, width)
        outp = jnp.dot(af, wout, preferred_element_type=jnp.float32)
        dout = cot_tokens[span].reshape(rows, out_ch * 4)
        g_out = transposed(af, dout)
        daf = against(dout, wout).reshape(per_batch, tile_tok, width)
        _, pull = jax.vjp(modulate, x2, shiftf, scalef)
        dx2, dshiftf, dscalef = pull(daf)
        dgate2 = jnp.sum(dx2 * down, axis=1)
        ddown = (gate2[:, None, :] * dx2).astype(jnp.bfloat16).reshape(rows, width)
        g_down = transposed(hid, ddown)
        dhid = against(ddown, wd)
        _, pull = jax.vjp(gelu_tanh, pre)
        dpre = pull(dhid)[0].astype(jnp.bfloat16)
        g_up = transposed(a2, dpre)
        da2 = against(dpre, wu).reshape(per_batch, tile_tok, width)
        _, pull = jax.vjp(modulate, x1, shift2, scale2)
        dx1_norm, dshift2, dscale2 = pull(da2)
        dx1 = dx2 + dx1_norm
        dgate1 = jnp.sum(dx1 * proj, axis=1)
        dproj = (gate1[:, None, :] * dx1).astype(jnp.bfloat16).reshape(rows, width)
        g_proj = transposed(att, dproj)
        datt = (
            against(dproj, wpr).astype(jnp.bfloat16).reshape(per_batch, tile_tok, heads, head_dim)
        )
        dgroups = group_heads(datt, groups)

        def attend_back(items):
            qpart, kpart, vpart, dpart, lse = items
            prob = jnp.exp(scores(qpart, kpart) - lse)
            dprob = jnp.einsum("nqhd,nkhd->nhqk", dpart, vpart, preferred_element_type=jnp.float32)
            delta = jnp.sum(dprob * prob, -1, keepdims=True)
            dscore = (prob * (dprob - delta)).astype(jnp.bfloat16)
            dq = (
                jnp.einsum("nhqk,nkhd->nqhd", dscore, kpart, preferred_element_type=jnp.float32)
                * factor
            )
            dk = (
                jnp.einsum("nhqk,nqhd->nkhd", dscore, qpart, preferred_element_type=jnp.float32)
                * factor
            )
            dv = jnp.einsum(
                "nhqk,nqhd->nkhd",
                prob.astype(jnp.bfloat16),
                dpart,
                preferred_element_type=jnp.float32,
            )
            return (dq, dk, dv)

        dq_groups, dk_groups, dv_groups = lax.map(
            attend_back, (qgroups, kgroups, vgroups, dgroups, lse_groups)
        )
        dquery = join_heads(dq_groups)
        dkey = lax.psum_scatter(
            join_heads(dk_groups).astype(jnp.bfloat16),
            ("row", "col"),
            scatter_dimension=1,
            tiled=True,
        ).astype(jnp.float32)
        dvalue = lax.psum_scatter(
            join_heads(dv_groups).astype(jnp.bfloat16),
            ("row", "col"),
            scatter_dimension=1,
            tiled=True,
        ).astype(jnp.float32)
        dqkv = jnp.concatenate([dquery, dkey, dvalue], axis=-1)
        dqkv = dqkv.astype(jnp.bfloat16).reshape(rows, 3 * width)
        g_qkv = transposed(a1.reshape(rows, width), dqkv)
        da1 = against(dqkv, wq).reshape(per_batch, tile_tok, width)
        _, pull = jax.vjp(modulate, x0, shift1, scale1)
        dx0_norm, dshift1, dscale1 = pull(da1)
        dtok = (dx1 + dx0_norm).astype(jnp.bfloat16).reshape(rows, width)
        g_patch = transposed(pieces, dtok)
        dpatch = against(dtok, wp).reshape(per_batch, tile_tok, chans * 4)
        dmods = jnp.concatenate([dshift1, dscale1, dgate1, dshift2, dscale2, dgate2], axis=-1)
        dfmods = jnp.concatenate([dshiftf, dscalef], axis=-1)
        silu_float = silu_b.astype(jnp.float32)
        g_ada = jnp.dot(jnp.transpose(silu_float), dmods, precision=highest)
        g_fada = jnp.dot(jnp.transpose(silu_float), dfmods, precision=highest)
        dsilu = jnp.dot(dmods, jnp.transpose(wa.astype(jnp.float32)), precision=highest)
        dsilu = dsilu + jnp.dot(dfmods, jnp.transpose(wf.astype(jnp.float32)), precision=highest)
        _, pull = jax.vjp(swish, cond_sel[span])
        dcond_sel = pull(dsilu)[0]
        dcond = picker[span][:, :, None] * dcond_sel[:, None, :]
        grads = (g_patch, g_qkv, g_proj, g_up, g_down, g_ada, g_fada, g_out)
        grads, outp, dpatch, dcond = (
            grads,
            outp.reshape(per_batch, tile_tok, out_ch * 4),
            dpatch,
            dcond,
        )
        grads = (
            lax.psum_scatter(
                grads[0].astype(jnp.bfloat16), "img", scatter_dimension=0, tiled=True
            ).astype(jnp.float32),
            lax.psum_scatter(
                grads[1].astype(jnp.bfloat16), "img", scatter_dimension=0, tiled=True
            ).astype(jnp.float32),
            lax.psum_scatter(
                grads[2].astype(jnp.bfloat16), "img", scatter_dimension=0, tiled=True
            ).astype(jnp.float32),
            lax.psum_scatter(
                grads[3].astype(jnp.bfloat16), "img", scatter_dimension=0, tiled=True
            ).astype(jnp.float32),
            lax.psum_scatter(
                grads[4].astype(jnp.bfloat16), "img", scatter_dimension=0, tiled=True
            ).astype(jnp.float32),
            lax.psum_scatter(
                grads[5].astype(jnp.bfloat16), "img", scatter_dimension=0, tiled=True
            ).astype(jnp.float32),
            lax.psum_scatter(
                grads[6].astype(jnp.bfloat16), "img", scatter_dimension=0, tiled=True
            ).astype(jnp.float32),
            lax.psum_scatter(
                grads[7].astype(jnp.bfloat16), "img", scatter_dimension=0, tiled=True
            ).astype(jnp.float32),
        )
        totals = tuple((total + grad for total, grad in zip(totals, grads)))
        outputs.append(outp)
        latent_parts.append(dpatch)
        cond_parts.append(dcond)
    cond_local = jnp.concatenate(cond_parts, axis=0)
    summed = (
        lax.psum(totals[0].astype(jnp.bfloat16), ("row", "col")).astype(jnp.float32),
        lax.psum(totals[1].astype(jnp.bfloat16), ("row", "col")).astype(jnp.float32),
        lax.psum(totals[2].astype(jnp.bfloat16), ("row", "col")).astype(jnp.float32),
        lax.psum(totals[3].astype(jnp.bfloat16), ("row", "col")).astype(jnp.float32),
        lax.psum(totals[4].astype(jnp.bfloat16), ("row", "col")).astype(jnp.float32),
        lax.psum(totals[5].astype(jnp.bfloat16), ("row", "col")).astype(jnp.float32),
        lax.psum(totals[6].astype(jnp.bfloat16), ("row", "col")).astype(jnp.float32),
        lax.psum(totals[7].astype(jnp.bfloat16), ("row", "col")).astype(jnp.float32),
        lax.psum(cond_local.astype(jnp.bfloat16), ("row", "col")).astype(jnp.float32),
    )
    out_tile = to_tile(jnp.concatenate(outputs, axis=0))
    grad_tile = to_tile(jnp.concatenate(latent_parts, axis=0))
    joined = jnp.concatenate([out_tile, grad_tile], axis=1)
    right_rim = shifted(joined[:, :, :, :1], "col", -1)
    joined = jnp.concatenate([joined[:, :, :, 1:], right_rim], axis=3)
    lower_rim = shifted(joined[:, :, :1, :], "row", -1)
    joined = jnp.concatenate([joined[:, :, 1:, :], lower_rim], axis=2)
    latent_out = joined[:, :out_ch]
    latent_grad = joined[:, out_ch:]
    return (
        latent_out,
        latent_grad,
        summed[8],
        summed[0],
        summed[1],
        summed[2],
        summed[3],
        summed[4],
        summed[5],
        summed[6],
        summed[7],
    )


def solution(mesh):
    return jax.shard_map(
        local,
        mesh=mesh,
        in_specs=(
            P("img", None, "row", "col"),
            P("img", None, "row", "col"),
            P("img", None, None),
            P("img"),
            P("img", None),
            P("img", None),
            P("img", None),
            P("img", None),
            P("img", None),
            P("img", None),
            P("img", None),
            P("img", None),
        ),
        out_specs=(
            P("img", None, "row", "col"),
            P("img", None, "row", "col"),
            P("img", None, None),
            P("img", None),
            P("img", None),
            P("img", None),
            P("img", None),
            P("img", None),
            P("img", None),
            P("img", None),
            P("img", None),
        ),
        check_vma=False,
    )
```

profile of v0, /device:TPU:0, one launch (start us, length us, event | category | flops | bytes accessed | tf_op | source)
XLA Modules:
  0.0 3237.4 jit_solution(13200590915424139758)
XLA Ops:
  23.0 178.6 %all-gather.12.cloned.1.call-done = bf16[1152,6912]{1,0:T(8,128)(2,1)} async-done(((bf16[576,6912]{1,0:T(8,128)(2,1)}), bf16[1152,6912]{1,0:T(8,128)(2,1)}) %all-gather.12.cloned.1.call-update) | async-done | bytes 15925264 | tf_op jit(solution)/shard_map/all_gather | solution.py:149
  201.6 7.7 fusion.195
  209.5 92.8 %all-gather.14.cloned.1.call-done = bf16[1152,3456]{1,0:T(8,128)(2,1)} async-done(((bf16[576,3456]{1,0:T(8,128)(2,1)}), bf16[1152,3456]{1,0:T(8,128)(2,1)}) %all-gather.14.cloned.1.call-update) | async-done | bytes 7962640 | tf_op jit(solution)/shard_map/all_gather | solution.py:145
  312.5 9.2 fusion.189
  335.4 38.6 %all-gather.26.cloned.1.call-done = bf16[1152,2304]{1,0:T(8,128)(2,1)} async-done(((bf16[576,2304]{1,0:T(8,128)(2,1)}), bf16[1152,2304]{1,0:T(8,128)(2,1)}) %all-gather.26.cloned.1.call-update) | async-done | bytes 5308432 | tf_op jit(solution)/shard_map/all_gather | solution.py:150
  381.1 48.6 %all-gather.18.cloned.1.call-done = bf16[2,1024,1152]{2,0,1:T(2,128)(2,1)} async-done(((bf16[2,64,1152]{2,0,1:T(2,128)(2,1)}), bf16[2,1024,1152]{2,0,1:T(2,128)(2,1)}) %all-gather.18.cloned.1.call-update) | async-done | bytes 4718608 | tf_op jit(solution)/shard_map/all_gather | solution.py:171
  429.7 12.4 copy.87
  447.3 36.6 %all-gather.16.cloned.1.call-done = bf16[2,1024,1152]{2,0,1:T(2,128)(2,1)} async-done(((bf16[2,64,1152]{2,0,1:T(2,128)(2,1)}), bf16[2,1024,1152]{2,0,1:T(2,128)(2,1)}) %all-gather.16.cloned.1.call-update) | async-done | bytes 4718608 | tf_op jit(solution)/shard_map/all_gather | solution.py:172
  484.0 12.4 copy.85
  501.7 18.1 while.52
  521.4 16.8 all-gather.30.cloned.1.call-done
  538.2 12.4 copy.97
  555.8 36.8 %all-gather.28.cloned.1.call-done = bf16[2,1024,1152]{2,0,1:T(2,128)(2,1)} async-done(((bf16[2,64,1152]{2,0,1:T(2,128)(2,1)}), bf16[2,1024,1152]{2,0,1:T(2,128)(2,1)}) %all-gather.28.cloned.1.call-update) | async-done | bytes 4718608 | tf_op jit(solution)/shard_map/all_gather | solution.py:172
  592.6 12.5 copy.95
  610.5 18.2 while.53
  638.9 125.7 %all-gather.22.cloned.1.call-done = bf16[1152,4608]{1,0:T(8,128)(2,1)} async-done(((bf16[576,4608]{1,0:T(8,128)(2,1)}), bf16[1152,4608]{1,0:T(8,128)(2,1)}) %all-gather.22.cloned.1.call-update) | async-done | bytes 10616848 | tf_op jit(solution)/shard_map/all_gather | solution.py:147
  764.7 7.2 fusion.216
  771.8 125.2 %all-gather.24.cloned.1.call-done = bf16[4608,1152]{1,0:T(8,128)(2,1)} async-done(((bf16[2304,1152]{1,0:T(8,128)(2,1)}), bf16[4608,1152]{1,0:T(8,128)(2,1)}) %all-gather.24.cloned.1.call-update) | async-done | bytes 10616848 | tf_op jit(solution)/shard_map/all_gather | solution.py:148
  917.7 9.7 fusion.135
  945.2 46.8 %while.55 = (s32[]{:T(128)}, bf16[4,2,64,4,72]{4,2,3,1,0:T(8,128)(2,1)S(1)}, bf16[4,2,1024,4,72]{2,4,3,0,1:T(8,128)(2,1)}, bf16[4,2,1024,4,72]{2,4,3,0,1:T(8,128...) while((s32[]{:T(128)}, ...), condition=%wide.region_37.38_spmd, body=%wide.region_35.37_spmd.sunk | while | flops 382832128 | bytes 90854664 | solution.py:258
  992.0 6.8 copy.120
  1000.9 8.9 fusion.128
  1030.5 44.6 %while.54 = (s32[]{:T(128)}, bf16[4,2,64,4,72]{4,2,3,1,0:T(8,128)(2,1)S(1)}, bf16[4,2,1024,4,72]{2,4,3,0,1:T(8,128)(2,1)}, bf16[4,2,1024,4,72]{2,4,3,0,1:T(8,128...) while((s32[]{:T(128)}, ...), condition=%wide.region_26.27_spmd, body=%wide.region_24.26_spmd.sunk | while | flops 382832128 | bytes 90854664 | solution.py:258
  1102.1 51.6 %reduce-scatter.29.cloned.1.call-done = bf16[2,64,1152]{2,1,0:T(8,128)(2,1)} async-done(((bf16[2,1024,1152]{2,1,0:T(8,128)(2,1)}), bf16[2,64,1152]{2,1,0:T(8,128)(2,1)}) %reduce-scatter.29.cloned.1.call-update) | async-done | bytes 294928 | tf_op jit(solution)/shard_map/reduce_scatter | solution.py:268
  1162.1 70.8 %reduce-scatter.23.cloned.1.call-done = bf16[2,64,1152]{2,1,0:T(8,128)(2,1)} async-done(((bf16[2,1024,1152]{2,1,0:T(8,128)(2,1)}), bf16[2,64,1152]{2,1,0:T(8,128)(2,1)}) %reduce-scatter.23.cloned.1.call-update) | async-done | bytes 294928 | tf_op jit(solution)/shard_map/reduce_scatter | solution.py:262
  1233.9 78.1 %reduce-scatter.25.cloned.1.call-done = bf16[2,64,1152]{2,1,0:T(8,128)(2,1)} async-done(((bf16[2,1024,1152]{2,1,0:T(8,128)(2,1)}), bf16[2,64,1152]{2,1,0:T(8,128)(2,1)}) %reduce-scatter.25.cloned.1.call-update) | async-done | bytes 294928 | tf_op jit(solution)/shard_map/reduce_scatter | solution.py:268
  1344.4 6.9 convolution_convert_fusion.2
  1378.6 15.5 convolution_convert_fusion.1
  1394.9 15.5 convolution_convert_fusion
  1423.7 15.2 fusion.223
  1438.9 6.9 fusion.154
  1445.8 15.3 fusion.222
  1467.8 45.5 %reduce-scatter.51.cloned.1.call-done = bf16[576,2304]{1,0:T(8,128)(2,1)} async-done(((bf16[1152,2304]{1,0:T(8,128)(2,1)}), bf16[576,2304]{1,0:T(8,128)(2,1)}) %reduce-scatter.51.cloned.1.call-update) | async-done | bytes 2654224 | tf_op jit(solution)/shard_map/reduce_scatter | solution.py:319
  1513.3 69.4 %reduce-scatter.53.cloned.1.call-done = bf16[576,2304]{1,0:T(8,128)(2,1)} async-done(((bf16[1152,2304]{1,0:T(8,128)(2,1)}), bf16[576,2304]{1,0:T(8,128)(2,1)}) %reduce-scatter.53.cloned.1.call-update) | async-done | bytes 2654224 | tf_op jit(solution)/shard_map/reduce_scatter | solution.py:319
  1587.4 121.0 %reduce-scatter.43.cloned.1.call-done = bf16[2304,1152]{1,0:T(8,128)(2,1)} async-done(((bf16[4608,1152]{1,0:T(8,128)(2,1)}), bf16[2304,1152]{1,0:T(8,128)(2,1)}) %reduce-scatter.43.cloned.1.call-update) | async-done | bytes 5308432 | tf_op jit(solution)/shard_map/reduce_scatter | solution.py:313
  1708.4 125.7 %reduce-scatter.45.cloned.1.call-done = bf16[2304,1152]{1,0:T(8,128)(2,1)} async-done(((bf16[4608,1152]{1,0:T(8,128)(2,1)}), bf16[2304,1152]{1,0:T(8,128)(2,1)}) %reduce-scatter.45.cloned.1.call-update) | async-done | bytes 5308432 | tf_op jit(solution)/shard_map/reduce_scatter | solution.py:313
  1834.1 7.8 add_convert_fusion.1
  1841.9 118.3 %reduce-scatter.41.cloned.1.call-done = bf16[576,4608]{1,0:T(8,128)(2,1)} async-done(((bf16[1152,4608]{1,0:T(8,128)(2,1)}), bf16[576,4608]{1,0:T(8,128)(2,1)}) %reduce-scatter.41.cloned.1.call-update) | async-done | bytes 5308432 | tf_op jit(solution)/shard_map/reduce_scatter | solution.py:310
  1960.2 126.3 %reduce-scatter.39.cloned.1.call-done = bf16[576,4608]{1,0:T(8,128)(2,1)} async-done(((bf16[1152,4608]{1,0:T(8,128)(2,1)}), bf16[576,4608]{1,0:T(8,128)(2,1)}) %reduce-scatter.39.cloned.1.call-update) | async-done | bytes 5308432 | tf_op jit(solution)/shard_map/reduce_scatter | solution.py:310
  2086.5 7.8 add_convert_fusion.2
  2094.3 89.2 %reduce-scatter.31.cloned.1.call-done = bf16[576,3456]{1,0:T(8,128)(2,1)} async-done(((bf16[1152,3456]{1,0:T(8,128)(2,1)}), bf16[576,3456]{1,0:T(8,128)(2,1)}) %reduce-scatter.31.cloned.1.call-update) | async-done | bytes 3981328 | tf_op jit(solution)/shard_map/reduce_scatter | solution.py:304
  2183.4 97.5 %reduce-scatter.33.cloned.1.call-done = bf16[576,3456]{1,0:T(8,128)(2,1)} async-done(((bf16[1152,3456]{1,0:T(8,128)(2,1)}), bf16[576,3456]{1,0:T(8,128)(2,1)}) %reduce-scatter.33.cloned.1.call-update) | async-done | bytes 3981328 | tf_op jit(solution)/shard_map/reduce_scatter | solution.py:304
  2287.1 176.2 %reduce-scatter.47.cloned.1.call-done = bf16[576,6912]{1,0:T(8,128)(2,1)} async-done(((bf16[1152,6912]{1,0:T(8,128)(2,1)}), bf16[576,6912]{1,0:T(8,128)(2,1)}) %reduce-scatter.47.cloned.1.call-update) | async-done | bytes 7962640 | tf_op jit(solution)/shard_map/reduce_scatter | solution.py:316
  2463.3 183.0 %reduce-scatter.49.cloned.1.call-done = bf16[576,6912]{1,0:T(8,128)(2,1)} async-done(((bf16[1152,6912]{1,0:T(8,128)(2,1)}), bf16[576,6912]{1,0:T(8,128)(2,1)}) %reduce-scatter.49.cloned.1.call-update) | async-done | bytes 7962640 | tf_op jit(solution)/shard_map/reduce_scatter | solution.py:316
  2646.3 9.1 add_convert_fusion
  2668.2 71.9 %all-reduce.9.cloned.1.call-done = (bf16[4,4,1152]{2,1,0:T(4,128)(2,1)}, bf16[8,1152]{1,0:T(8,128)(2,1)}, bf16[576,32]{0,1:T(8,128)(2,1)}) async-done(((bf16[4,4,1152]{2,1,0:T(4,128)(2,1)}, bf16[8,1152]{1,0:T(8,128)(2,1)}, bf16[576,32]{0,1:T(8,128)(2,1)}), (bf16[4,4,1152]{2,1,0:T(4,128)(2,1)}, bf16[8,1152]{1,0:T(8,128)(2,1)}, bf16[576,32]{0,1:T(8,128)(2,1)})) %all-reduce.9.cloned.1.call-update) | async-done | bytes 92176 | tf_op jit(solution)/shard_map/psum | solution.py:340
  2744.2 457.9 %all-reduce.11.cloned.1.call-done = (bf16[576,3456]{1,0:T(8,128)(2,1)}, bf16[576,1152]{1,0:T(8,128)(2,1)}, bf16[576,4608]{1,0:T(8,128)(2,1)}, bf16[2304,1152]{1,...) async-done(((bf16[576,3456]{1,0:T(8,128)(2,1)}, bf16[576,1152]{1,0:T(8,128)(2,1)}, bf16[576,4608]{1,0:T(8,128)(2,1)}, bf16[2304,1152]{1,0:T(8,128)(2,1)}, ...) | async-done | bytes 26542096 | tf_op jit(solution)/shard_map/psum | solution.py:333
  3223.3 7.1 convert_element_type.392
  (778 shorter events, 430.8 us)
Async XLA Ops:
  7.2 194.4 %all-gather.12.cloned.1.call-start = ((), (), s32[]{:S(2)}) async-start(), calls=%async_computation.18 | async-start | bytes 23887872 | tf_op jit(solution)/shard_map/all_gather | solution.py:149
  7.9 294.4 %all-gather.14.cloned.1.call-start = ((), (), s32[]{:S(2)}) async-start(), calls=%async_computation.19 | async-start | bytes 11943936 | tf_op jit(solution)/shard_map/all_gather | solution.py:145
  8.7 365.3 %all-gather.26.cloned.1.call-start = ((), (), s32[]{:S(2)}) async-start(), calls=%async_computation.25 | async-start | bytes 7962624 | tf_op jit(solution)/shard_map/all_gather | solution.py:150
  9.5 3.9 collective-permute-start
  10.1 419.7 %all-gather.18.cloned.1.call-start = ((), (), s32[]{:S(2)}) async-start(), calls=%async_computation.21 | async-start | bytes 5013504 | tf_op jit(solution)/shard_map/all_gather | solution.py:171
  11.2 366.3 %copy-start.68 = (bf16[4,1152]{1,0:T(4,128)(2,1)}, bf16[4,1152]{1,0:T(4,128)(2,1)S(1)}, u32[]{:S(2)}) copy-start(bf16[4,1152]{1,0:T(4,128)(2,1)S(1)} %fusion.150) | copy-start | bytes 27652
  13.6 7.7 collective-permute-start.1
  20.5 291.3 %copy-start.80 = (bf16[16,1152]{1,0:T(8,128)(2,1)}, bf16[16,1152]{1,0:T(8,128)(2,1)S(1)}, u32[]{:S(2)}) copy-start(bf16[16,1152]{1,0:T(8,128)(2,1)S(1)} %all_gather.44) | copy-start | bytes 110596
  21.7 187.5 %copy-start.72 = (bf16[2,8,8,4,2,2]{3,5,2,4,1,0:T(2,128)(2,1)}, bf16[2,8,8,4,2,2]{3,5,2,4,1,0:T(2,128)(2,1)S(1)}, u32[]{:S(2)}) copy-start(bf16[2,8,8,4,2,2]{3,5,2,4,1,0:T(2,128)(2,1)S(1)} %get-tuple-element.430) | copy-start | bytes 12292
  21.7 289.5 %copy-start.70 = (bf16[2,8,8,4,2,2]{3,5,2,4,1,0:T(2,128)(2,1)}, bf16[2,8,8,4,2,2]{3,5,2,4,1,0:T(2,128)(2,1)S(1)}, u32[]{:S(2)}) copy-start(bf16[2,8,8,4,2,2]{3,5,2,4,1,0:T(2,128)(2,1)S(1)} %get-tuple-element.431) | copy-start | bytes 12292
  22.7 613.7 %copy-start.5 = (f32[2,64,1152]{2,1,0:T(8,128)}, f32[2,64,1152]{2,1,0:T(8,128)S(1)}, u32[]{:S(2)}) copy-start(f32[2,64,1152]{2,1,0:T(8,128)S(1)} %get-tuple-element.469) | copy-start | bytes 1769476
  22.8 186.5 %copy-start.97 = (f32[2,64]{1,0:T(2,128)}, f32[2,64]{1,0:T(2,128)S(1)}, u32[]{:S(2)}) copy-start(f32[2,64]{1,0:T(2,128)S(1)} %broadcast_multiply_fusion.5) | copy-start | bytes 1540
  23.0 186.3 %copy-start.106 = (f32[2,64]{1,0:T(2,128)}, f32[2,64]{1,0:T(2,128)S(1)}, u32[]{:S(2)}) copy-start(f32[2,64]{1,0:T(2,128)S(1)} %multiply_reduce_fusion.21) | copy-start | bytes 1540
  23.0 186.3 %copy-start.102 = (f32[2,64]{1,0:T(2,128)}, f32[2,64]{1,0:T(2,128)S(1)}, u32[]{:S(2)}) copy-start(f32[2,64]{1,0:T(2,128)S(1)} %fusion.175) | copy-start | bytes 1540
  308.9 175.1 %all-gather.16.cloned.1.call-start = ((), (), s32[]{:S(2)}) async-start(), calls=%async_computation.20 | async-start | bytes 5013504 | tf_op jit(solution)/shard_map/all_gather | solution.py:172
  311.0 227.3 %all-gather.30.cloned.1.call-start = ((), (), s32[]{:S(2)}) async-start(), calls=%async_computation.27 | async-start | bytes 5013504 | tf_op jit(solution)/shard_map/all_gather | solution.py:171
  324.6 268.0 %all-gather.28.cloned.1.call-start = ((), (), s32[]{:S(2)}) async-start(), calls=%async_computation.26 | async-start | bytes 5013504 | tf_op jit(solution)/shard_map/all_gather | solution.py:172
  325.7 306.4 %all-gather.20.cloned.1.call-start = ((), (), s32[]{:S(2)}) async-start(), calls=%async_computation.22 | async-start | bytes 3981312 | tf_op jit(solution)/shard_map/all_gather | solution.py:146
  326.5 438.2 %all-gather.22.cloned.1.call-start = ((), (), s32[]{:S(2)}) async-start(), calls=%async_computation.23 | async-start | bytes 15925248 | tf_op jit(solution)/shard_map/all_gather | solution.py:147
  327.2 569.8 %all-gather.24.cloned.1.call-start = ((), (), s32[]{:S(2)}) async-start(), calls=%async_computation.24 | async-start | bytes 15925248 | tf_op jit(solution)/shard_map/all_gather | solution.py:148
  327.8 773.3 %reduce-scatter.27.cloned.1.call-start = ((), (), s32[]{:S(2)}) async-start(), calls=%async_computation.30 | async-start | bytes 5013504 | tf_op jit(solution)/shard_map/reduce_scatter | solution.py:262
  334.2 579.8 %copy-start.66 = (bf16[1152,32,1]{0,1,2:T(8,128)(2,1)}, bf16[1152,32,1]{0,1,2:T(8,128)(2,1)S(1)}, u32[]{:S(2)}) copy-start(bf16[1152,32,1]{0,1,2:T(8,128)(2,1)S(1)} %reshape.741) | copy-start | bytes 221188
  771.8 131.9 %copy-start.10 = (f32[2,64,1152]{2,1,0:T(8,128)S(1)}, f32[2,64,1152]{2,1,0:T(8,128)}, u32[]{:S(2)}) copy-start(f32[2,64,1152]{2,1,0:T(8,128)} %copy-done.9) | copy-start | bytes 1769476
  998.8 154.8 %reduce-scatter.29.cloned.1.call-start = ((), (), s32[]{:S(2)}) async-start(), calls=%async_computation.31 | async-start | bytes 5013504 | tf_op jit(solution)/shard_map/reduce_scatter | solution.py:268
  1024.8 208.2 %reduce-scatter.23.cloned.1.call-start = ((), (), s32[]{:S(2)}) async-start(), calls=%async_computation.28 | async-start | bytes 5013504 | tf_op jit(solution)/shard_map/reduce_scatter | solution.py:262
  1081.8 230.3 %reduce-scatter.25.cloned.1.call-start = ((), (), s32[]{:S(2)}) async-start(), calls=%async_computation.29 | async-start | bytes 5013504 | tf_op jit(solution)/shard_map/reduce_scatter | solution.py:268
  1088.5 323.8 %reduce-scatter.55.cloned.1.call-start = ((), (), s32[]{:S(2)}) async-start(), calls=%async_computation.44 | async-start | bytes 442368
  1091.4 322.0 %reduce-scatter.57.cloned.1.call-start = ((), (), s32[]{:S(2)}) async-start(), calls=%async_computation.45 | async-start | bytes 442368
  1092.8 322.3 %reduce-scatter.37.cloned.1.call-start = ((), (), s32[]{:S(2)}) async-start(), calls=%async_computation.35 | async-start | bytes 3981312 | tf_op jit(solution)/shard_map/reduce_scatter | solution.py:307
  1095.3 325.3 %reduce-scatter.35.cloned.1.call-start = ((), (), s32[]{:S(2)}) async-start(), calls=%async_computation.34 | async-start | bytes 3981312 | tf_op jit(solution)/shard_map/reduce_scatter | solution.py:307
  1100.9 365.2 %all-reduce.13.cloned.1.call-start = ((), (), s32[]{:S(2)}) async-start(), calls=%async_computation.48 | async-start | bytes 147456
  1160.9 152.1 %copy-start.6 = (f32[2,64,1152]{2,1,0:T(8,128)S(1)}, f32[2,64,1152]{2,1,0:T(8,128)}, u32[]{:S(2)}) copy-start(f32[2,64,1152]{2,1,0:T(8,128)} %copy-done.5) | copy-start | bytes 1769476
  1160.9 152.1 %copy-start.83 = (f32[2,1152]{1,0:T(2,128)S(1)}, f32[2,1152]{1,0:T(2,128)}, u32[]{:S(2)}) copy-start(f32[2,1152]{1,0:T(2,128)} %copy-done.82) | copy-start | bytes 27652
  1161.0 152.1 %copy-start.98 = (f32[2,64]{1,0:T(2,128)S(1)}, f32[2,64]{1,0:T(2,128)}, u32[]{:S(2)}) copy-start(f32[2,64]{1,0:T(2,128)} %copy-done.97) | copy-start | bytes 1540
  1321.8 191.6 %reduce-scatter.51.cloned.1.call-start = ((), (), s32[]{:S(2)}) async-start(), calls=%async_computation.42 | async-start | bytes 7962624 | tf_op jit(solution)/shard_map/reduce_scatter | solution.py:319
  1328.1 254.7 %reduce-scatter.53.cloned.1.call-start = ((), (), s32[]{:S(2)}) async-start(), calls=%async_computation.43 | async-start | bytes 7962624 | tf_op jit(solution)/shard_map/reduce_scatter | solution.py:319
  1334.5 373.9 %reduce-scatter.43.cloned.1.call-start = ((), (), s32[]{:S(2)}) async-start(), calls=%async_computation.38 | async-start | bytes 15925248 | tf_op jit(solution)/shard_map/reduce_scatter | solution.py:313
  1342.8 491.3 %reduce-scatter.45.cloned.1.call-start = ((), (), s32[]{:S(2)}) async-start(), calls=%async_computation.39 | async-start | bytes 15925248 | tf_op jit(solution)/shard_map/reduce_scatter | solution.py:313
  1351.3 608.9 %reduce-scatter.41.cloned.1.call-start = ((), (), s32[]{:S(2)}) async-start(), calls=%async_computation.37 | async-start | bytes 15925248 | tf_op jit(solution)/shard_map/reduce_scatter | solution.py:310
  1358.3 728.1 %reduce-scatter.39.cloned.1.call-start = ((), (), s32[]{:S(2)}) async-start(), calls=%async_computation.36 | async-start | bytes 15925248 | tf_op jit(solution)/shard_map/reduce_scatter | solution.py:310
  1365.4 818.0 %reduce-scatter.31.cloned.1.call-start = ((), (), s32[]{:S(2)}) async-start(), calls=%async_computation.32 | async-start | bytes 11943936 | tf_op jit(solution)/shard_map/reduce_scatter | solution.py:304
  1371.7 909.2 %reduce-scatter.33.cloned.1.call-start = ((), (), s32[]{:S(2)}) async-start(), calls=%async_computation.33 | async-start | bytes 11943936 | tf_op jit(solution)/shard_map/reduce_scatter | solution.py:304
  1378.5 1084.8 %reduce-scatter.47.cloned.1.call-start = ((), (), s32[]{:S(2)}) async-start(), calls=%async_computation.40 | async-start | bytes 23887872 | tf_op jit(solution)/shard_map/reduce_scatter | solution.py:316
  1394.1 1252.1 %reduce-scatter.49.cloned.1.call-start = ((), (), s32[]{:S(2)}) async-start(), calls=%async_computation.41 | async-start | bytes 23887872 | tf_op jit(solution)/shard_map/reduce_scatter | solution.py:316
  1410.4 1329.7 %all-reduce.9.cloned.1.call-start = ((), (), s32[]{:S(2)}) async-start(), calls=%async_computation.46 | async-start | bytes 192512 | tf_op jit(solution)/shard_map/psum | solution.py:340
  1467.5 1734.5 %all-reduce.11.cloned.1.call-start = ((), (), s32[]{:S(2)}) async-start(), calls=%async_computation.47 | async-start | bytes 53084160 | tf_op jit(solution)/shard_map/psum | solution.py:333
  2659.2 5.0 collective-permute-start.2
  2664.2 1.7 collective-permute-start.3
  (167 other events, 1235.7 us)
Sparse Core Ops, SparseCore 0:
  9.6 191.9 all-gather.11
  203.1 99.1 all-gather.13
  303.8 70.1 all-gather.25
  376.8 52.9 all-gather.17
  432.5 51.4 all-gather.15
  486.7 51.4 all-gather.29
  541.1 51.4 all-gather.27
  594.2 37.8 all-gather.19
  633.7 130.9 all-gather.21
  766.1 130.9 all-gather.23
  999.0 75.5 reduce-scatter.26
  1078.8 74.7 reduce-scatter.28
  1158.1 74.7 reduce-scatter.22
  1237.2 74.7 reduce-scatter.24
  1314.1 11.3 reduce-scatter.54
  1327.6 12.1 reduce-scatter.56
  1342.4 38.0 reduce-scatter.36
  1382.6 38.0 reduce-scatter.34
  1423.6 20.9 all-reduce.12
  1446.7 66.5 reduce-scatter.50
  1516.2 66.4 reduce-scatter.52
  1585.1 123.3 reduce-scatter.42
  1710.7 123.3 reduce-scatter.44
  1836.8 123.3 reduce-scatter.40
  1963.1 123.3 reduce-scatter.38
  2088.6 94.7 reduce-scatter.30
  2186.2 94.7 reduce-scatter.32
  2283.2 180.0 reduce-scatter.46
  2466.2 180.0 reduce-scatter.48
  2650.4 89.5 all-reduce.8
  2746.7 455.2 all-reduce.10
where the time goes:
time: 3250 us; the launch traced here: 3240 us
  waiting for transfers between devices  2600 us (80%)
  matrix products  315 us (10%)
  local copies, waits for them, and re-layouts  192 us (6%)
  other arithmetic  95.4 us (3%)
    psum x1, waiting for transfers between devices, local(): lax.psum(totals[1].astype(jnp.bfloat16), ('row', 'col')).astype(jnp.float32)  458 us
    reduce_scatter x2, waiting for transfers between devices, local(): lax.psum_scatter(grads[5].astype(jnp.bfloat16), 'img', scatter_dimension=...  359 us
    reduce_scatter x2, waiting for transfers between devices, local(): lax.psum_scatter(grads[4].astype(jnp.bfloat16), 'img', scatter_dimension=...  247 us
    reduce_scatter x2, waiting for transfers between devices, local(): lax.psum_scatter(grads[3].astype(jnp.bfloat16), 'img', scatter_dimension=...  245 us
    reduce_scatter x2, waiting for transfers between devices, local(): lax.psum_scatter(grads[1].astype(jnp.bfloat16), 'img', scatter_dimension=...  187 us
    all_gather x1, waiting for transfers between devices, local(): wa = lax.all_gather(w_ada, 'img', axis=0, tiled=True)  179 us
    reduce_scatter x2, waiting for transfers between devices, local(): lax.psum_scatter(join_heads(dv_groups).astype(jnp.bfloat16), ('row', 'col...  130 us
    all_gather x1, waiting for transfers between devices, local(): wu = lax.all_gather(w_up, 'img', axis=0, tiled=True)  126 us
  transfers between devices with their start and end apart: 35, of which 29 were waited for; matrix products, arithmetic and copies ran while one was open for 14% of the time, Pallas kernels for 0%

commit v1 on v0

v1 whole, which is shorter than its diff:
```python
import math

import jax
import jax.numpy as jnp
from jax import lax
from jax.experimental import pallas as pl
from jax.experimental.pallas import tpu as pltpu
from jax.sharding import PartitionSpec as P

HEADS = 16
RC = ("row", "col")
BF = jnp.bfloat16
F32 = jnp.float32


def shifted(block, axis, distance):
    size = lax.axis_size(axis)
    return lax.ppermute(block, axis, [((i - distance) % size, i) for i in range(size)])


def layer_norm(value):
    center = value - jnp.mean(value, -1, keepdims=True)
    spread = jnp.mean(center * center, -1, keepdims=True)
    return center * lax.rsqrt(spread + 1e-06)


def modulate(value, shift, scale):
    return layer_norm(value) * (1.0 + scale[:, None, :]) + shift[:, None, :]


def gelu_tanh(value):
    return jax.nn.gelu(value, approximate=True)


def swish(value):
    return value * jax.nn.sigmoid(value)


def sincos(coord, count):
    freqs = 1.0 / 10000.0 ** (jnp.arange(count, dtype=F32) / count)
    angle = coord.astype(F32)[..., None] * freqs
    return jnp.concatenate([jnp.sin(angle), jnp.cos(angle)], axis=-1)


def dotd(left, right, ldim, rdim):
    return lax.dot_general(
        left, right, (((ldim,), (rdim,)), ((), ())), preferred_element_type=F32
    )


def send_down(value, k):
    size = lax.axis_size("img")
    return lax.ppermute(value, "img", [(j, (j - k) % size) for j in range(size)])


def send_up(value, k):
    size = lax.axis_size("img")
    return lax.ppermute(value, "img", [(j, (j + k) % size) for j in range(size)])


def split_own(value, axis):
    size = lax.axis_size("img")
    me = lax.axis_index("img")
    width = value.shape[axis] // size
    blocks = [lax.slice_in_dim(value, i * width, (i + 1) * width, axis=axis) for i in range(size)]
    if size == 2:
        return [
            jnp.where(me == 0, blocks[0], blocks[1]),
            jnp.where(me == 0, blocks[1], blocks[0]),
        ]
    return [
        lax.dynamic_slice_in_dim(value, (me + k) % size * width, width, axis=axis)
        for k in range(size)
    ]


def join_own(items, axis):
    size = lax.axis_size("img")
    me = lax.axis_index("img")
    if size == 2:
        return jnp.concatenate(
            [jnp.where(me == 0, items[0], items[1]), jnp.where(me == 0, items[1], items[0])],
            axis=axis,
        )
    width = items[0].shape[axis]
    twice = jnp.concatenate(list(items) + list(items), axis=axis)
    return lax.dynamic_slice_in_dim(twice, (size - me) % size * width, size * width, axis=axis)


def tied(value, *after):
    return lax.optimization_barrier((value, after))[0]


def swap_parts(parts):
    size = len(parts)
    return [parts[0]] + [send_down(parts[size - k], k) for k in range(1, size)]


def swap_full(value):
    return [value] + [send_down(value, k) for k in range(1, lax.axis_size("img"))]


def other_rows(weight):
    size = lax.axis_size("img")
    tiles = lax.axis_size("row") * lax.axis_size("col")
    at = lax.axis_index("row") * lax.axis_size("col") + lax.axis_index("col")
    rows, width = weight.shape
    each = -(-rows // (tiles * 8)) * 8
    start = jnp.minimum(at * each, rows - each)
    piece = lax.dynamic_slice(weight, (start, 0), (each, width))
    if rows % each:
        lag = jnp.clip(at * each - start, 0, each)
        piece = lax.dynamic_slice(jnp.concatenate([piece, piece], 0), (lag, 0), (each, width))
    pieces = [send_down(piece, k) for k in range(1, size)]
    if size == 2:
        return [lax.all_gather(pieces[0], RC, axis=0, tiled=True)], pieces
    full = lax.all_gather(jnp.stack(pieces), RC, axis=1, tiled=True)
    return [full[k] for k in range(size - 1)], pieces


def widened(part, rows, axis):
    extra = rows - part.shape[axis]
    if extra == 0:
        return part
    pads = [(0, 0), (0, 0)]
    pads[axis] = (0, extra)
    return jnp.pad(part, pads)


def quad_order(rows_n, cols_n):
    def quad(s):
        return s // cols_n * 2 // rows_n * 2 + s % cols_n * 2 // cols_n

    return sorted(range(rows_n * cols_n), key=quad)


def pick_tokens(pieces, par, half):
    lane = lax.broadcasted_iota(jnp.int32, pieces[0].shape, 1)
    tiles = []
    for j in range(0, len(pieces), 2):
        a = pieces[j].astype(F32)
        b = pieces[j + 1].astype(F32)
        if par == 0:
            tile = jnp.where(lane < half, a, pltpu.roll(b, half, 1))
        else:
            tile = jnp.where(lane < half, pltpu.roll(a, half, 1), b)
        tiles.append(tile.astype(BF))
    return jnp.concatenate(tiles, axis=1)


def put_tokens(first, second, spot, half):
    tile = spot // 2
    a = first[:, tile * 2 * half : (tile + 1) * 2 * half]
    b = second[:, tile * 2 * half : (tile + 1) * 2 * half]
    lane = lax.broadcasted_iota(jnp.int32, a.shape, 1)
    if spot % 2 == 0:
        return jnp.where(lane < half, a, pltpu.roll(b, half, 1))
    return jnp.where(lane < half, pltpu.roll(a, half, 1), b)


def attend_kernel(order, half, factor, kind_ref, x_ref, o_ref, lse_ref, qkv_s, o_s):
    step = pl.program_id(1)
    count = len(order) * half
    block = count // 4
    coef = factor * math.log2(math.e)
    for par in range(2):
        for c in range(3):
            qkv_s[c] = pick_tokens([x_ref[s, 0, c] for s in order], par, half)
        single = kind_ref[2 * step + par] == 0
        for b in range(4):
            cols = slice(b * block, (b + 1) * block)

            def work(keys, cols=cols, par=par):
                query = qkv_s[0, :, cols]
                score = dotd(qkv_s[1, :, keys], query, 0, 0)
                top = jnp.max(score, axis=0, keepdims=True)
                expd = jnp.exp2((score - top) * coef)
                total = jnp.sum(expd, axis=0, keepdims=True)
                out = dotd(qkv_s[2, :, keys], expd.astype(BF), 1, 0)
                o_s[par, :, cols] = out * (1.0 / total)
                lse_ref[0, par, :, cols] = top * coef + jnp.log2(total)

            @pl.when(single)
            def _():
                work(slice(0, count))

            @pl.when(jnp.logical_not(single))
            def _():
                work(cols)

    for i, s in enumerate(order):
        o_ref[s, 0] = put_tokens(o_s[0], o_s[1], i, half).astype(BF)


def attend_back_kernel(
    order, half, factor, kind_ref, x_ref, d_ref, lse_ref, g_ref, qkv_s, d_s, g_s
):
    step = pl.program_id(1)
    count = len(order) * half
    block = count // 4
    coef = factor * math.log2(math.e)
    for par in range(2):
        for c in range(3):
            qkv_s[c] = pick_tokens([x_ref[s, 0, c] for s in order], par, half)
        d_s[...] = pick_tokens([d_ref[s, 0] for s in order], par, half)
        single = kind_ref[2 * step + par] == 0
        for b in range(4):
            cols = slice(b * block, (b + 1) * block)

            def work(keys, fresh, cols=cols, par=par):
                query = qkv_s[0, :, cols]
                dout = d_s[:, cols]
                score = dotd(qkv_s[1, :, keys], query, 0, 0)
                prob = jnp.exp2(score * coef - lse_ref[0, par, :, cols])
                dprob = dotd(qkv_s[2, :, keys], dout, 0, 0)
                delta = jnp.sum(prob * dprob, axis=0, keepdims=True)
                dscore = (prob * (dprob - delta)).astype(BF)
                g_s[par, 0, :, cols] = dotd(qkv_s[1, :, keys], dscore, 1, 0) * factor
                dkey = dotd(query, dscore, 1, 1) * factor
                dvalue = dotd(dout, prob.astype(BF), 1, 1)
                if fresh:
                    g_s[par, 1, :, keys] = dkey
                    g_s[par, 2, :, keys] = dvalue
                else:
                    g_s[par, 1, :, keys] += dkey
                    g_s[par, 2, :, keys] += dvalue

            @pl.when(single)
            def _():
                work(slice(0, count), b == 0)

            @pl.when(jnp.logical_not(single))
            def _():
                work(cols, True)

    for c in range(3):
        for i, s in enumerate(order):
            g_ref[s, 0, c] = put_tokens(g_s[0, c], g_s[1, c], i, half).astype(BF)


def attend(kinds, x, order, half, factor):
    tiles, per, _, depth, tokens = x.shape
    count = tiles * half
    pairs = tokens // (2 * half)
    return pl.pallas_call(
        lambda *refs: attend_kernel(order, half, factor, *refs),
        grid_spec=pltpu.PrefetchScalarGridSpec(
            num_scalar_prefetch=1,
            grid=(per, pairs),
            in_specs=[
                pl.BlockSpec((tiles, 1, 3, depth, 2 * half), lambda h, p, kd: (0, h, 0, 0, p))
            ],
            out_specs=[
                pl.BlockSpec((tiles, 1, depth, 2 * half), lambda h, p, kd: (0, h, 0, p)),
                pl.BlockSpec((1, 2, 1, count), lambda h, p, kd: (h, p, 0, 0)),
            ],
            scratch_shapes=[
                pltpu.VMEM((3, depth, count), BF),
                pltpu.VMEM((2, depth, count), F32),
            ],
        ),
        out_shape=[
            jax.ShapeDtypeStruct((tiles, per, depth, tokens), BF),
            jax.ShapeDtypeStruct((per, 2 * pairs, 1, count), F32),
        ],
        name="attend",
        cost_estimate=pl.CostEstimate(
            flops=10**10, bytes_accessed=4 * 10**7, transcendentals=per * tokens * count
        ),
    )(kinds, x)


def attend_back(kinds, x, d, lse, order, half, factor):
    tiles, per, _, depth, tokens = x.shape
    count = tiles * half
    pairs = tokens // (2 * half)
    return pl.pallas_call(
        lambda *refs: attend_back_kernel(order, half, factor, *refs),
        grid_spec=pltpu.PrefetchScalarGridSpec(
            num_scalar_prefetch=1,
            grid=(per, pairs),
            in_specs=[
                pl.BlockSpec((tiles, 1, 3, depth, 2 * half), lambda h, p, kd: (0, h, 0, 0, p)),
                pl.BlockSpec((tiles, 1, depth, 2 * half), lambda h, p, kd: (0, h, 0, p)),
                pl.BlockSpec((1, 2, 1, count), lambda h, p, kd: (h, p, 0, 0)),
            ],
            out_specs=pl.BlockSpec(
                (tiles, 1, 3, depth, 2 * half), lambda h, p, kd: (0, h, 0, 0, p)
            ),
            scratch_shapes=[
                pltpu.VMEM((3, depth, count), BF),
                pltpu.VMEM((depth, count), BF),
                pltpu.VMEM((2, 3, depth, count), F32),
            ],
        ),
        out_shape=jax.ShapeDtypeStruct(x.shape, BF),
        name="attend_back",
        cost_estimate=pl.CostEstimate(
            flops=10**10, bytes_accessed=4 * 10**7, transcendentals=per * tokens * count
        ),
    )(kinds, x, d, lse)


def swapped(value, axis, bit):
    return lax.ppermute(value, axis, [(j, j ^ bit) for j in range(lax.axis_size(axis))])


def added(a, b):
    return (a.astype(F32) + b.astype(F32)).astype(BF)


def halved(value, axis, bit):
    upper = lax.axis_index(axis) // bit % 2
    rows = value.shape[0] // 2
    keep = lax.dynamic_slice_in_dim(value, upper * rows, rows, 0)
    give = lax.dynamic_slice_in_dim(value, (1 - upper) * rows, rows, 0)
    return added(keep, swapped(give, axis, bit))


def doubled(value, axis, bit):
    upper = lax.axis_index(axis) // bit % 2
    got = swapped(value, axis, bit)
    return jnp.where(
        upper == 0, jnp.concatenate([value, got], 0), jnp.concatenate([got, value], 0)
    )


def bits_of(axis):
    return [(axis, 1 << i) for i in range(lax.axis_size(axis).bit_length() - 1)]


def tile_sum(value, cols_first):
    rows, cols = bits_of("row"), bits_of("col")
    if cols_first:
        halves, wholes = rows[:1] + cols[:-1], cols[-1:] + rows[1:]
    else:
        halves, wholes = rows + cols[:-1], cols[-1:]
    for axis, bit in halves:
        value = halved(value, axis, bit)
    for axis, bit in wholes:
        value = added(value, swapped(value, axis, bit))
    for axis, bit in halves[::-1]:
        value = doubled(value, axis, bit)
    return value


def exchange(x):
    return lax.all_to_all(x, RC, split_axis=0, concat_axis=0, tiled=True)


def summed_apart(small, items, finish):
    once = 1 + jnp.minimum(lax.axis_index("row"), 0)
    tiles, each, width = small.shape
    imgs = lax.axis_size("img")

    def body(_, state):
        parts = jnp.sum(exchange(state[0][0]).astype(F32), axis=0).astype(BF)
        parts = jnp.stack(swap_full(parts))
        parts = exchange(jnp.broadcast_to(parts[None], (tiles,) + parts.shape))
        parts = parts.transpose(1, 0, 2, 3)
        done = finish(parts.reshape(imgs, tiles * each, width))
        return parts, done, [tile_sum(value, c % 2 == 1) for c, value in enumerate(state[2])]

    start = jnp.broadcast_to(small[None], (imgs,) + small.shape)
    empty = jax.eval_shape(finish, jax.ShapeDtypeStruct((imgs, tiles * each, width), BF))
    empty = jnp.zeros(empty.shape, empty.dtype)
    small, done, items = lax.fori_loop(0, once, body, (start, empty, items))
    return small.reshape(imgs, tiles * each, width), done, items


def outer_kernel(left_ref, right_ref, out_ref):
    out_ref[...] = dotd(left_ref[...], right_ref[...], 0, 0)


def outer(left, right, block):
    depth, rows = left.shape
    cols = right.shape[1]
    return pl.pallas_call(
        outer_kernel,
        grid=(cols // block,),
        in_specs=[
            pl.BlockSpec((depth, rows), lambda j: (0, 0)),
            pl.BlockSpec((depth, block), lambda j: (0, j)),
        ],
        out_specs=pl.BlockSpec((rows, block), lambda j: (0, j)),
        out_shape=jax.ShapeDtypeStruct((rows, cols), F32),
        name="outer",
    )(left, right)


def local(
    latent,
    cotangent,
    cond,
    canvas_kind,
    w_patch,
    w_qkv,
    w_proj,
    w_up,
    w_down,
    w_ada,
    w_final_ada,
    w_out,
):
    local_n, chans, tile_r, tile_c = latent.shape
    out_ch = cotangent.shape[1]
    slots = cond.shape[1]
    width = cond.shape[2]
    inner = w_up.shape[1]
    imgs = lax.axis_size("img")
    rows_n = lax.axis_size("row")
    cols_n = lax.axis_size("col")
    row_at = lax.axis_index("row")
    col_at = lax.axis_index("col")
    tiles = rows_n * cols_n
    patch_r = tile_r // 2
    patch_c = tile_c // 2
    tile_tok = patch_r * patch_c
    half = patch_r * rows_n // 2
    half_c = patch_c * cols_n // 2
    head_dim = width // HEADS
    per = HEADS // tiles
    factor = head_dim ** (-0.5)
    rows = local_n * tile_tok
    order = quad_order(rows_n, cols_n)

    o_qkv, sent = other_rows(w_qkv)
    w_straight = tied(w_proj, sent)
    o_proj = [send_down(w_straight, k) for k in range(1, imgs)]
    o_up, sent = other_rows(tied(w_up, sent))
    o_down, _ = other_rows(tied(w_down, sent))
    wp = join_own([w_patch] + [send_down(w_patch, k) for k in range(1, imgs)], 0)
    wout = join_own([w_out] + [send_down(w_out, k) for k in range(1, imgs)], 0)

    stacked = jnp.concatenate([latent, cotangent], axis=1)
    upper = shifted(stacked[:, :, -1:, :], "row", 1)
    framed = jnp.concatenate([upper, stacked[:, :, :-1, :]], axis=2)
    beside = shifted(framed[:, :, :, -1:], "col", 1)
    framed = jnp.concatenate([beside, framed[:, :, :, :-1]], axis=3)

    def to_tokens(tile):
        depth = tile.shape[1]
        shaped = tile.reshape(local_n, depth, patch_r, 2, patch_c, 2).transpose(0, 2, 4, 1, 3, 5)
        return shaped.reshape(rows, depth * 4)

    def to_tile(tokens):
        depth = tokens.shape[1] // 4
        shaped = tokens.reshape(local_n, patch_r, patch_c, depth, 2, 2).transpose(0, 3, 1, 4, 2, 5)
        return shaped.reshape(local_n, depth, tile_r, tile_c)

    pieces = to_tokens(framed[:, :chans])
    dout = to_tokens(framed[:, chans:])

    quad = row_at * 2 // rows_n * 2 + col_at * 2 // cols_n
    slot = canvas_kind * quad
    picker = (slot[:, None] == jnp.arange(slots, dtype=jnp.int32)[None, :]).astype(F32)
    silu = swish(cond)
    silu_low = silu.astype(BF)
    chosen = jnp.sum(picker[:, :, None] * silu_low.astype(F32), axis=1).astype(BF)
    packed = jnp.concatenate([chosen, silu_low.reshape(local_n * slots, width)], axis=0)
    packed = swap_parts(split_own(packed, 1))
    silu_all = jnp.concatenate([item[local_n:] for item in packed], axis=0)
    chosen_all = jnp.concatenate([item[:local_n] for item in packed], axis=0)
    part = jnp.concatenate(
        [dotd(chosen_all, w_ada, 1, 0), dotd(chosen_all, w_final_ada, 1, 0)], axis=1
    )
    part = [part[k * local_n : (k + 1) * local_n] for k in range(imgs)]
    mods = part[0]
    for k in range(1, imgs):
        mods = mods + send_up(part[k], k)
    shift1, scale1, gate1, shift2, scale2, gate2, shiftf, scalef = jnp.split(mods, 8, axis=-1)

    prow = row_at * patch_r + jnp.arange(patch_r, dtype=jnp.int32)
    pcol = col_at * patch_c + jnp.arange(patch_c, dtype=jnp.int32)
    lrow = prow[None, :] - canvas_kind[:, None] * (prow[None, :] // half) * half
    lcol = pcol[None, :] - canvas_kind[:, None] * (pcol[None, :] // half_c) * half_c
    table_r = sincos(lrow, width // 4)
    table_c = sincos(lcol, width // 4)
    full = (local_n, patch_r, patch_c, width // 2)
    positions = jnp.concatenate(
        [
            jnp.broadcast_to(table_c[:, None, :, :], full),
            jnp.broadcast_to(table_r[:, :, None, :], full),
        ],
        axis=-1,
    ).reshape(local_n, tile_tok, width)

    def tokens3(value):
        return value.reshape(local_n, tile_tok, -1)

    x0 = tokens3(dotd(pieces, wp, 1, 0)) + positions
    a1 = modulate(x0, shift1, scale1).astype(BF).reshape(rows, width)
    a1_parts = split_own(a1, 1)
    a1_all = jnp.concatenate(swap_parts(a1_parts), 0)

    def product(parts, own, others):
        total = dotd(parts[0], own, 1, 0)
        for part, other in zip(parts[1:], others):
            total = total + dotd(widened(part, other.shape[0], 1), other, 1, 0)
        return total

    def back_product(value, own, others):
        items = [dotd(value, own, 1, 1)]
        for other in others:
            items.append(dotd(value, other, 1, 1)[:, : own.shape[0]])
        return items

    qkv = dotd(w_qkv, a1_parts[0], 0, 1)
    for part, other in zip(a1_parts[1:], o_qkv):
        qkv = qkv + dotd(other, widened(part, other.shape[0], 1), 0, 1)
    qkv = qkv.astype(BF).reshape(3, tiles, per, head_dim, rows).transpose(1, 2, 0, 3, 4)
    qkv = exchange(qkv)
    qkv, o_proj = lax.optimization_barrier((qkv, o_proj))
    att, lse = attend(canvas_kind, qkv, order, tile_tok, factor)
    att = exchange(att).reshape(width, rows)
    att, a1_all = lax.optimization_barrier((att, a1_all))
    att_parts = split_own(att, 0)
    att_all = jnp.concatenate(swap_parts(att_parts), 1)
    proj = dotd(att_parts[0], w_proj, 0, 0)
    for part, other in zip(att_parts[1:], o_proj):
        proj = proj + dotd(widened(part, other.shape[0], 0), other, 0, 0)
    proj = tokens3(proj)
    x1 = x0 + gate1[:, None, :] * proj
    a2 = modulate(x1, shift2, scale2).astype(BF).reshape(rows, width)
    a2_parts = split_own(a2, 1)
    a2_all = jnp.concatenate(swap_parts(a2_parts), 0)
    pre = product(a2_parts, w_up, o_up)
    hid = gelu_tanh(pre).astype(BF)
    hid, att_all, a2_all = lax.optimization_barrier((hid, att_all, a2_all))
    hid_parts = split_own(hid, 1)
    hid_all = jnp.concatenate(swap_parts(hid_parts), 0)
    down = tokens3(product(hid_parts, w_down, o_down))
    x2 = x1 + gate2[:, None, :] * down
    af = modulate(x2, shiftf, scalef).astype(BF).reshape(rows, width)
    outp = dotd(af, wout, 1, 0)

    g_out = dotd(dout, af, 0, 0)
    daf = tokens3(dotd(dout, wout, 1, 1))
    _, pull = jax.vjp(modulate, x2, shiftf, scalef)
    dx2, dshiftf, dscalef = pull(daf)
    dgate2 = jnp.sum(dx2 * down, axis=1)
    ddown = (gate2[:, None, :] * dx2).astype(BF).reshape(rows, width)
    ddown_all = jnp.concatenate(swap_full(ddown), 0)
    dhid = join_own(back_product(ddown, w_down, o_down), 1)
    _, pull = jax.vjp(gelu_tanh, pre)
    dpre = pull(dhid)[0].astype(BF)
    dpre, hid_all = lax.optimization_barrier((dpre, hid_all))
    dpre_all = jnp.concatenate(swap_full(dpre), 0)
    da2 = tokens3(join_own(back_product(dpre, w_up, o_up), 1))
    da2, ddown_all = lax.optimization_barrier((da2, ddown_all))
    g_down = dotd(hid_all, ddown_all, 0, 0).astype(BF)
    da2, g_down = lax.optimization_barrier((da2, g_down))
    g_down = lax.psum_scatter(g_down, RC, scatter_dimension=0, tiled=True)
    _, pull = jax.vjp(modulate, x1, shift2, scale2)
    dx1_norm, dshift2, dscale2 = pull(da2)
    dx1 = dx2 + dx1_norm
    dgate1 = jnp.sum(dx1 * proj, axis=1)
    dproj = (gate1[:, None, :] * dx1).astype(BF).reshape(rows, width)
    datt = [dotd(w_proj, dproj, 1, 1)]
    for other in o_proj:
        datt.append(dotd(other, dproj, 1, 1)[: w_proj.shape[0]])
    datt = join_own(datt, 0).astype(BF)
    datt = exchange(datt.reshape(tiles, per, head_dim, rows))
    dproj_all = jnp.concatenate(swap_full(dproj), 0)
    dqkv = attend_back(canvas_kind, qkv, datt, lse, order, tile_tok, factor)
    dqkv, dpre_all = lax.optimization_barrier((dqkv, dpre_all))
    dqkv = exchange(dqkv)
    g_up = dotd(a2_all, dpre_all, 0, 0).astype(BF)
    dqkv, g_up, g_down, dproj_all = lax.optimization_barrier((dqkv, g_up, g_down, dproj_all))
    g_down = lax.all_gather(g_down, RC, axis=0, tiled=True)
    dqkv = dqkv.transpose(2, 0, 1, 3, 4).reshape(3 * width, rows)
    dqkv_all = jnp.concatenate(swap_full(dqkv), 1)
    dqkv_all, g_up, g_down = lax.optimization_barrier((dqkv_all, g_up, g_down))
    g_up = lax.psum(g_up, RC)
    da1 = [dotd(dqkv, w_qkv, 0, 1)]
    for other in o_qkv:
        da1.append(dotd(dqkv, other, 0, 1)[:, : w_qkv.shape[0]])
    da1 = tokens3(join_own(da1, 1))
    g_proj = dotd(att_all, dproj_all, 1, 0).astype(BF)
    g_att = [
        dotd(a1_all, dqkv_all[c * width : (c + 1) * width], 0, 1).astype(BF) for c in range(3)
    ]
    _, pull = jax.vjp(modulate, x0, shift1, scale1)
    dx0_norm, dshift1, dscale1 = pull(da1)
    dtok = (dx1 + dx0_norm).astype(BF).reshape(rows, width)
    g_patch = dotd(pieces, dtok, 0, 0)
    dpatch = dotd(dtok, wp, 1, 1)

    dmods = jnp.concatenate(
        [dshift1, dscale1, dgate1, dshift2, dscale2, dgate2, dshiftf, dscalef], axis=-1
    )
    dmods = (picker[:, :, None] * dmods[:, None, :]).reshape(local_n * slots * 8, width)
    small = jnp.concatenate([g_patch, g_out, dmods], axis=0)
    n_patch = g_patch.shape[0]
    n_out = g_out.shape[0]
    count = small.shape[0]
    each = -(-count // tiles)
    small = jnp.pad(small, ((0, each * tiles - count), (0, 0))).astype(BF)
    step = local_n * slots

    def split_small(value):
        return value[:, n_patch + n_out : count].reshape(imgs * step, 8 * width)

    def back_cond(value):
        dmods = split_small(value)
        dsilu = dotd(dmods[:, : 6 * width], w_ada, 1, 1)
        dsilu = dsilu + dotd(dmods[:, 6 * width :], w_final_ada, 1, 1)
        dsilu = [dsilu[k * step : (k + 1) * step] for k in range(imgs)]
        dsilu = [dsilu[0]] + [send_up(dsilu[imgs - k], imgs - k) for k in range(1, imgs)]
        return join_own(dsilu, 1)

    small, dsilu, g_att = summed_apart(
        small.reshape(tiles, each, width), g_att + [g_proj], back_cond
    )
    g_qkv = jnp.concatenate(g_att[:3], axis=1)
    g_proj = g_att[3]
    sums = jnp.sum(small[:, : n_patch + n_out].astype(F32), axis=0)
    g_patch = split_own(sums[:n_patch], 0)[0]
    g_out = split_own(sums[n_patch:], 1)[0].T
    dmods = split_small(small)
    g_ada = outer(silu_all, dmods[:, : 6 * width], width)
    g_fada = outer(silu_all, dmods[:, 6 * width :], width)
    dsilu = dsilu.reshape(local_n, slots, width)
    _, pull = jax.vjp(swish, cond)
    cond_grad = pull(dsilu)[0]

    joined = jnp.concatenate([to_tile(outp), to_tile(dpatch)], axis=1)
    right_rim = shifted(joined[:, :, :, :1], "col", -1)
    joined = jnp.concatenate([joined[:, :, :, 1:], right_rim], axis=3)
    lower_rim = shifted(joined[:, :, :1, :], "row", -1)
    joined = jnp.concatenate([joined[:, :, 1:, :], lower_rim], axis=2)
    return (
        joined[:, :out_ch],
        joined[:, out_ch:],
        cond_grad,
        g_patch,
        g_qkv.astype(F32),
        g_proj.astype(F32),
        g_up.astype(F32),
        g_down.astype(F32),
        g_ada,
        g_fada,
        g_out,
    )


def solution(mesh):
    rows = P("img", None)
    tile = P("img", None, "row", "col")
    whole = P("img", None, None)
    return jax.shard_map(
        local,
        mesh=mesh,
        in_specs=(tile, tile, whole, P("img")) + (rows,) * 8,
        out_specs=(tile, tile, whole) + (rows,) * 8,
        check_vma=False,
    )
```

time: 3250 us -> 720 us (0.22)
  waiting for transfers between devices: 2600 us -> 285 us
  matrix products: 315 us -> 107 us
  local copies, waits for them, and re-layouts: 192 us -> 60.7 us
  starting transfers between devices: 9.47 us -> 76.5 us
  Pallas kernels: 0 us -> 39.6 us
    reduce_scatter x16 -> x1, waiting for transfers between devices: 1360 us -> 0.01 us  [local(): g_down = lax.psum_scatter(g_down, RC, scatter_dimension=0, tiled=True)]
    all_gather x10 -> x4, waiting for transfers between devices: 701 us -> 8.21 us  [the longest x3 7.39 us: other_rows(): return ([lax.all_gather(pieces[0], RC, axis=0, tiled=True)], pieces)]
    psum x2 -> x1, waiting for transfers between devices: 530 us -> 0.01 us  [local(): g_up = lax.psum(g_up, RC)]
    dot_general x105 -> x32, matrix products: 315 us -> 107 us  [dotd(): lax.dot_general(left, right, (((ldim,), (rdim,)), ((), ())), preferred_el...]
    ppermute x4 -> x48, waiting for transfers between devices: 3.45 us -> 205 us  [the longest x26 98.4 us: swapped(): lax.ppermute(value, axis, [(j, j ^ bit) for j in range(lax.axis_size(axis...]
    all_to_all x0 -> x5, waiting for transfers between devices: none -> 72 us  [exchange(): return lax.all_to_all(x, RC, split_axis=0, concat_axis=0, tiled=True)]
    while x102 -> x26, local copies, waits for them, and re-layouts: 51.6 us -> 0.07 us
    ppermute x4 -> x48, starting transfers between devices: 6.41 us -> 56.3 us  [the longest x16 25.9 us: send_down(): lax.ppermute(value, 'img', [(j, (j - k) % size) for j in range(size)])]
  transfers between devices with their start and end apart: 35 -> 59, of which waited for: 29 -> 29; matrix products, arithmetic and copies ran while one was open for 14% -> 34% of each run, Pallas kernels for 0% -> 6%
where the time goes in v1:
time: 720 us; the launch traced here: 709 us
  waiting for transfers between devices  285 us (40%)
  matrix products  107 us (15%)
  other arithmetic  103 us (14%)
  starting transfers between devices  76.5 us (11%)
  local copies, waits for them, and re-layouts  60.7 us (8%)
  Pallas kernels  39.6 us (6%)
  blocking collectives  21.6 us (3%)
  between operations  15.7 us (2%)
    dot_general x32, matrix products, dotd(): lax.dot_general(left, right, (((ldim,), (rdim,)), ((), ())), preferred_el...  107 us
    ppermute x26, waiting for transfers between devices, swapped(): lax.ppermute(value, axis, [(j, j ^ bit) for j in range(lax.axis_size(axis...  98.4 us
    ppermute x16, waiting for transfers between devices, send_down(): lax.ppermute(value, 'img', [(j, (j - k) % size) for j in range(size)])  93.1 us
    all_to_all x5, waiting for transfers between devices, exchange(): return lax.all_to_all(x, RC, split_axis=0, concat_axis=0, tiled=True)  72 us
    ppermute x16, starting transfers between devices, send_down(): lax.ppermute(value, 'img', [(j, (j - k) % size) for j in range(size)])  25.9 us
    ppermute x26, starting transfers between devices, swapped(): lax.ppermute(value, axis, [(j, j ^ bit) for j in range(lax.axis_size(axis...  24.3 us
    all_to_all x1, blocking collectives, exchange(): return lax.all_to_all(x, RC, split_axis=0, concat_axis=0, tiled=True)  21.6 us
    all_to_all x5, starting transfers between devices, exchange(): return lax.all_to_all(x, RC, split_axis=0, concat_axis=0, tiled=True)  19.1 us
  transfers between devices with their start and end apart: 59, of which 29 were waited for; matrix products, arithmetic and copies ran while one was open for 34% of the time, Pallas kernels for 6%

profile of v1, /device:TPU:0, one launch (start us, length us, event | category | flops | bytes accessed | tf_op | source)
XLA Modules:
  0.0 709.2 jit_solution(7818234393991171124)
XLA Ops:
  11.6 6.6 collective-permute-done.33
  22.2 8.0 %collective-permute-done.36 = bf16[40,4608]{1,0:T(8,128)(2,1)S(1)} collective-permute-done((bf16[40,4608]{1,0:T(8,128)(2,1)S(1)}, bf16[40,4608]{1,0:T(8,128)(2,1)S(1)}, u32[]{:S(2)}, u32[]{:S(2)}) %collective-permute-start.36) | collective-permute-done | bytes 368672 | tf_op jit(solution)/shard_map/ppermute | solution.py:53
  36.7 5.2 collective-permute-done.29
  45.7 4.9 fusion.42
  52.2 4.4 collective-permute-done.32
  59.1 5.6 convolution_bitcast_fusion
  64.7 7.4 %all-gather.5.cloned.1.call-done = bf16[640,3456]{1,0:T(8,128)(2,1)} async-done(((bf16[40,3456]{1,0:T(8,128)(2,1)}), bf16[640,3456]{1,0:T(8,128)(2,1)}) %all-gather.5.cloned.1.call-update) | async-done | bytes 4423696 | tf_op jit(solution)/shard_map/all_gather | solution.py:116
  72.1 5.1 fusion.5
  88.8 8.7 %collective-permute-done.39 = bf16[144,1152]{1,0:T(8,128)(2,1)} collective-permute-done((bf16[144,1152]{1,0:T(8,128)(2,1)S(1)}, bf16[144,1152]{1,0:T(8,128)(2,1)}, u32[]{:S(2)}, u32[]{:S(2)}) %collective-permute-start.39) | collective-permute-done | bytes 331808 | tf_op jit(solution)/shard_map/ppermute | solution.py:53
  99.0 29.4 %collective-permute-done.34 = bf16[576,1152]{1,0:T(8,128)(2,1)} collective-permute-done((bf16[576,1152]{1,0:T(8,128)(2,1)}, bf16[576,1152]{1,0:T(8,128)(2,1)}, u32[]{:S(2)}, u32[]{:S(2)}) %collective-permute-start.34) | collective-permute-done | bytes 1327136 | tf_op jit(solution)/shard_map/ppermute | solution.py:53
  128.4 30.8 %all-to-all-done.2.refs_1_ = bf16[16,1,3,72,256]{4,3,2,1,0:T(8,128)(2,1)S(1)} async-done(((bf16[16,1,3,72,256]{4,3,2,1,0:T(8,128)(2,1)}), bf16[16,1,3,72,256]{4,3,2,1,0:T(8,128)(2,1)S(1)}, u32[]{:S(2)}, u32[]{:S(2)}) %all-to-all-start.2) | async-done | bytes 1769504 | tf_op jit(solution)/shard_map/all_to_all | solution.py:348
  160.4 12.0 %attend.1 = (bf16[16,1,72,256]{3,2,1,0:T(8,128)(2,1)}, f32[1,4,1,1024]{3,2,1,0:T(1,128)}) custom-call(s32[4]{0:T(128)} %refs_0_.3, bf16[16,1,3,72,256]{4,3,2,1,0:T(8,128)(2,1)} %copy-done.30), custom_call_target="tpu_custom_call" | custom-call | flops 10000000000 | bytes 40000000 | tf_op jit(solution)/shard_map/attend/pallas_call | solution.py:245
  172.4 3.7 all-to-all-start.3
  180.9 7.1 collective-permute-done.40
  189.5 8.7 %all-to-all-done.3 = bf16[16,1,72,256]{3,2,1,0:T(8,128)(2,1)S(1)} async-done(((bf16[16,1,72,256]{3,2,1,0:T(8,128)(2,1)}), bf16[16,1,72,256]{3,2,1,0:T(8,128)(2,1)S(1)}, u32[]{:S(2)}, u32[]{:S(2)}) %all-to-all-start.3) | async-done | bytes 589856 | tf_op jit(solution)/shard_map/all_to_all | solution.py:348
  211.6 6.9 fusion.60
  218.5 9.7 %multiply_convert_fusion = (bf16[256,4608]{1,0:T(8,128)(2,1)S(1)}, f32[256,4608]{1,0:T(8,128)}) fusion(f32[256,4608]{1,0:T(8,128)} %fusion.60, bf16[640,4608]{1,0:T(8,128)(2,1)} %all-gather.7.cloned.1.call-done, bf16[256,576]{0,1:T(8,128)(2,1)S(1)} %get-tuple-element.335), kind=kOutput, calls=%fused_computation.64 | convolution fusion | flops 1521745920 | bytes 17989632 | tf_op jit(solution)/shard_map/dot_general | solution.py:46
  233.6 5.2 fusion.61
  238.9 4.9 convolution_add_fusion.5
  248.4 4.4 fusion.62
  255.2 4.2 fusion.12
  259.4 11.6 %collective-permute-done.42 = bf16[256,1152]{1,0:T(8,128)(2,1)S(1)} collective-permute-done((bf16[256,1152]{1,0:T(8,128)(2,1)S(1)}, bf16[256,1152]{1,0:T(8,128)(2,1)S(1)}, u32[]{:S(2)}, u32[]{:S(2)}) %collective-permute-start.42) | collective-permute-done | bytes 589856 | tf_op jit(solution)/shard_map/ppermute | solution.py:53
  285.8 7.6 %convolution_convert_fusion = bf16[2304,1152]{1,0:T(8,128)(2,1)} fusion(bf16[512,2304]{1,0:T(8,128)(2,1)} %pad_maximum_fusion.5, bf16[512,1152]{1,0:T(8,128)(2,1)} %pad_maximum_fusion.7), kind=kOutput, calls=%fused_computation.45 | convolution fusion | flops 2720563200 | bytes 8847360 | tf_op jit(solution)/shard_map/dot_general | solution.py:46
  305.3 21.6 %all_to_all.40.refs_2_ = bf16[16,1,72,256]{3,2,1,0:T(8,128)(2,1)} all-to-all(bf16[16,1,72,256]{3,2,1,0:T(8,128)(2,1)S(1)} %bitcast.200), channel_id=1, replica_groups=mesh['img'=2,'row'=4,'col'=4] {'row','col'}, dimensions={0} | all-to-all | bytes 1179648 | tf_op jit(solution)/shard_map/all_to_all | solution.py:348
  326.9 15.7 %attend_back.1 = bf16[16,1,3,72,256]{4,3,2,1,0:T(8,128)(2,1)} custom-call(s32[4]{0:T(128)} %refs_0_.3, bf16[16,1,3,72,256]{4,3,2,1,0:T(8,128)(2,1)} %copy-done.30, bf16[16,1,72,256]{3,2,1,0:T(8,128)(2,1)} %all_to_all.40.refs_2_, f32[1,4,1,1024]{3,2,1,0:T(1,128)} %get-tuple-element.228.refs_3_), custom_call_target="tpu_custom_call" | custom-call | flops 10000000000 | bytes 40000000 | tf_op jit(solution)/shard_map/attend_back/pallas_call | solution.py:277
  342.6 4.9 pad_maximum_fusion.3
  347.5 3.8 all-to-all-start.5
  359.3 9.3 %collective-permute-done.44 = bf16[256,1152]{1,0:T(8,128)(2,1)} collective-permute-done((bf16[256,1152]{1,0:T(8,128)(2,1)}, bf16[256,1152]{1,0:T(8,128)(2,1)}, u32[]{:S(2)}, u32[]{:S(2)}) %collective-permute-start.44) | collective-permute-done | bytes 589856 | tf_op jit(solution)/shard_map/ppermute | solution.py:53
  371.0 7.0 convolution_convert_fusion.1
  378.0 26.2 %all-to-all-done.5 = bf16[16,1,3,72,256]{4,3,2,1,0:T(8,128)(2,1)S(1)} async-done(((bf16[16,1,3,72,256]{4,3,2,1,0:T(8,128)(2,1)}), bf16[16,1,3,72,256]{4,3,2,1,0:T(8,128)(2,1)S(1)}, u32[]{:S(2)}, u32[]{:S(2)}) %all-to-all-start.5) | async-done | bytes 1769504 | tf_op jit(solution)/shard_map/all_to_all | solution.py:348
  445.4 12.5 %collective-permute-done.47 = bf16[3456,256]{1,0:T(8,128)(2,1)} collective-permute-done((bf16[3456,256]{1,0:T(8,128)(2,1)}, bf16[3456,256]{1,0:T(8,128)(2,1)}, u32[]{:S(2)}, u32[]{:S(2)}) %collective-permute-start.47) | collective-permute-done | bytes 1769504 | tf_op jit(solution)/shard_map/ppermute | solution.py:53
  470.7 191.1 %while.23 = (s32[]{:T(128)}, bf16[2,16,11,1152]{3,0,2,1:T(2,128)(2,1)S(1)}, f32[16,1152]{1,0:T(8,128)}, bf16[576,1152]{1,0:T(8,128)(2,1)}, bf16[576,1152]{1,0:T(...) while((s32[]{:T(128)}, ...), condition=%wide.region_24.25_spmd, body=%wide.region_22.24_spmd.sunk | while | flops 390771072 | bytes 159709072 | solution.py:367
  472.0 4.3 all-to-all-start
  493.1 6.2 all-to-all-done
  518.5 7.9 %collective-permute-done.23 = bf16[144,1152]{1,0:T(8,128)(2,1)} collective-permute-done((bf16[144,1152]{1,0:T(8,128)(2,1)}, bf16[144,1152]{1,0:T(8,128)(2,1)}, u32[]{:S(2)}, u32[]{:S(2)}) %collective-permute-start.23) | collective-permute-done | bytes 331808 | tf_op jit(solution)/shard_map/while/body/ppermute | solution.py:305
  528.1 27.2 %collective-permute-done.4 = bf16[72,1152]{1,0:T(8,128)(2,1)S(1)} collective-permute-done((bf16[72,1152]{1,0:T(8,128)(2,1)S(1)}, bf16[72,1152]{1,0:T(8,128)(2,1)S(1)}, u32[]{:S(2)}, u32[]{:S(2)}) %collective-permute-start.4) | collective-permute-done | bytes 165920 | tf_op jit(solution)/shard_map/while/body/ppermute | solution.py:305
  555.4 8.4 %collective-permute-done.17 = bf16[72,1152]{1,0:T(8,128)(2,1)S(1)} collective-permute-done((bf16[72,1152]{1,0:T(8,128)(2,1)S(1)}, bf16[72,1152]{1,0:T(8,128)(2,1)S(1)}, u32[]{:S(2)}, u32[]{:S(2)}) %collective-permute-start.17) | collective-permute-done | bytes 165920 | tf_op jit(solution)/shard_map/while/body/ppermute | solution.py:305
  563.9 24.6 %collective-permute-done.5 = bf16[72,1152]{1,0:T(8,128)(2,1)S(1)} collective-permute-done((bf16[72,1152]{1,0:T(8,128)(2,1)S(1)}, bf16[72,1152]{1,0:T(8,128)(2,1)S(1)}, u32[]{:S(2)}, u32[]{:S(2)}) %collective-permute-start.5) | collective-permute-done | bytes 165920 | tf_op jit(solution)/shard_map/while/body/ppermute | solution.py:305
  601.2 4.5 collective-permute-done.12
  608.2 6.3 collective-permute-done.25
  617.3 4.3 collective-permute-done.7
  622.6 9.5 %collective-permute-done.20 = bf16[144,1152]{1,0:T(8,128)(2,1)S(1)} collective-permute-done((bf16[144,1152]{1,0:T(8,128)(2,1)S(1)}, bf16[144,1152]{1,0:T(8,128)(2,1)S(1)}, u32[]{:S(2)}, u32[]{:S(2)}) %collective-permute-start.20) | collective-permute-done | bytes 331808 | tf_op jit(solution)/shard_map/while/body/ppermute | solution.py:305
  638.0 5.9 fusion.120
  666.5 7.3 %convert_element_type.477 = f32[2304,1152]{1,0:T(8,128)} convert(bf16[2304,1152]{1,0:T(8,128)(2,1)} %all-gather.11.cloned.1.call-done) | non-fusion elementwise | flops 2654208 | bytes 15925248 | tf_op jit(solution)/shard_map/convert_element_type | solution.py:640
  673.8 8.0 %outer.2 = f32[576,6912]{1,0:T(8,128)} custom-call(bf16[32,576]{1,0:T(8,128)(2,1)} %pad_maximum_fusion.23.left_ref, bf16[32,6912]{1,0:T(8,128)(2,1)} %slice.246.right_ref), custom_call_target="tpu_custom_call" | custom-call | tf_op jit(solution)/shard_map/outer/pallas_call | solution.py:378
  681.7 4.0 outer.3
  689.2 4.6 maximum_convert_fusion
  693.8 8.1 %convert_element_type.476 = f32[576,4608]{1,0:T(8,128)} convert(bf16[576,4608]{1,0:T(8,128)(2,1)} %all-reduce.4.cloned.1.call-done) | non-fusion elementwise | flops 2654208 | bytes 15925248 | tf_op jit(solution)/shard_map/convert_element_type | solution.py:639
  (490 shorter events, 248.6 us)
Async XLA Ops:
  7.2 64.9 %all-gather.5.cloned.1.call-start = ((), (), s32[]{:S(2)}) async-start(), calls=%async_computation.7 | async-start | bytes 4700160 | tf_op jit(solution)/shard_map/all_gather | solution.py:116
  8.5 9.6 %collective-permute-start.33 = (bf16[40,3456]{1,0:T(8,128)(2,1)S(1)}, bf16[40,3456]{1,0:T(8,128)(2,1)S(1)}, u32[]{:S(2)}, u32[]{:S(2)}) collective-permute-start(bf16[40,3456]{1,0:T(8,128)(2,1)S(1)} %fusion.25), channel_id=1, source_target_pairs={{0,16},{16,0},{1,17},{17,1},{2,18},{18,2},{3,19},{19,3},{4,20},{20... | collective-permute-start | bytes 829448 | tf_op jit(solution)/shard_map/ppermute | solution.py:53
  18.9 199.6 %all-gather.7.cloned.1.call-start = ((), (), s32[]{:S(2)}) async-start(), calls=%async_computation.8 | async-start | bytes 6266880 | tf_op jit(solution)/shard_map/all_gather | solution.py:116
  20.4 9.8 %collective-permute-start.36 = (bf16[40,4608]{1,0:T(8,128)(2,1)S(1)}, bf16[40,4608]{1,0:T(8,128)(2,1)S(1)}, u32[]{:S(2)}, u32[]{:S(2)}) collective-permute-start(bf16[40,4608]{1,0:T(8,128)(2,1)S(1)} %fusion.22), channel_id=1, source_target_pairs={{0,16},{16,0},{1,17},{17,1},{2,18},{18,2},{3,19},{19,3},{4,20},{20... | collective-permute-start | bytes 1105928 | tf_op jit(solution)/shard_map/ppermute | solution.py:53
  31.8 11.6 %collective-permute-start.30 = (bf16[8,1152]{1,0:T(8,128)(2,1)S(1)}, bf16[8,1152]{1,0:T(8,128)(2,1)S(1)}, u32[]{:S(2)}, u32[]{:S(2)}) collective-permute-start(bf16[8,1152]{1,0:T(8,128)(2,1)S(1)} %copy-done.78), channel_id=1, source_target_pairs={{0,16},{16,0},{1,17},{17,1},{2,18},{18,2},{3,19},{19,3},{4,20},{20... | collective-permute-start | bytes 55304 | tf_op jit(solution)/shard_map/ppermute | solution.py:53
  33.6 10.6 %collective-permute-start.31 = (bf16[20,576]{1,0:T(8,128)(2,1)S(1)}, bf16[20,576]{1,0:T(8,128)(2,1)S(1)}, u32[]{:S(2)}, u32[]{:S(2)}) collective-permute-start(bf16[20,576]{1,0:T(8,128)(2,1)S(1)} %get-tuple-element.356), channel_id=1, source_target_pairs={{0,16},{16,0},{1,17},{17,1},{2,18},{18,2},{3,19},{19,3},{4,20},{20... | collective-permute-start | bytes 69128 | tf_op jit(solution)/shard_map/ppermute | solution.py:53
  82.3 76.9 %all-to-all-start.2 = ((bf16[16,1,3,72,256]{4,3,2,1,0:T(8,128)(2,1)}), bf16[16,1,3,72,256]{4,3,2,1,0:T(8,128)(2,1)S(1)}, u32[]{:S(2)}, u32[]{:S(2)}) async-start(bf16[16,1,3,72,256]{4,3,2,1,0:T(8,128)(2,1)} %bitcast.145), calls=%async_computation.2 | async-start | bytes 3538944 | tf_op jit(solution)/shard_map/all_to_all | solution.py:348
  86.0 152.9 %all-gather.9.cloned.1.call-start = ((), (), s32[]{:S(2)}) async-start(), calls=%async_computation.9 | async-start | bytes 5640192 | tf_op jit(solution)/shard_map/all_gather | solution.py:116
  87.3 10.2 %collective-permute-start.39 = (bf16[144,1152]{1,0:T(8,128)(2,1)S(1)}, bf16[144,1152]{1,0:T(8,128)(2,1)}, u32[]{:S(2)}, u32[]{:S(2)}) collective-permute-start(bf16[144,1152]{1,0:T(8,128)(2,1)S(1)} %constant_dynamic-slice_fusion.10), channel_id=1, source_target_pairs={{0,16},{16,0},{1,17},{17,1},{2,18},{18,2},{3,19},{19,3},{4,20},{20... | collective-permute-start | bytes 995336 | tf_op jit(solution)/shard_map/ppermute | solution.py:53
  97.5 30.9 %collective-permute-start.34 = (bf16[576,1152]{1,0:T(8,128)(2,1)}, bf16[576,1152]{1,0:T(8,128)(2,1)}, u32[]{:S(2)}, u32[]{:S(2)}) collective-permute-start(bf16[576,1152]{1,0:T(8,128)(2,1)} %param.20), channel_id=1, source_target_pairs={{0,16},{16,0},{1,17},{17,1},{2,18},{18,2},{3,19},{19,3},{4,20},{20... | collective-permute-start | bytes 3981320 | tf_op jit(solution)/shard_map/ppermute | solution.py:53
  172.4 25.9 %all-to-all-start.3 = ((bf16[16,1,72,256]{3,2,1,0:T(8,128)(2,1)}), bf16[16,1,72,256]{3,2,1,0:T(8,128)(2,1)S(1)}, u32[]{:S(2)}, u32[]{:S(2)}) async-start(bf16[16,1,72,256]{3,2,1,0:T(8,128)(2,1)} %get-tuple-element.217), calls=%async_computation.3 | async-start | bytes 1179648 | tf_op jit(solution)/shard_map/all_to_all | solution.py:348
  176.1 228.1 %reduce-scatter.2.cloned.1.call-start = ((), (), s32[]{:S(2)}) async-start(), calls=%async_computation.10 | async-start | bytes 5640192 | tf_op jit(solution)/shard_map/reduce_scatter | solution.py:553
  176.6 12.1 %collective-permute-start.35 = (bf16[256,576]{0,1:T(8,128)(2,1)}, bf16[256,576]{0,1:T(8,128)(2,1)S(1)}, u32[]{:S(2)}, u32[]{:S(2)}) collective-permute-start(bf16[256,576]{0,1:T(8,128)(2,1)} %get-tuple-element.341), channel_id=1, source_target_pairs={{0,16},{16,0},{1,17},{17,1},{2,18},{18,2},{3,19},{19,3},{4,20},{20... | collective-permute-start | bytes 884744 | tf_op jit(solution)/shard_map/ppermute | solution.py:53
  179.4 8.6 %collective-permute-start.40 = (bf16[576,32]{0,1:T(8,128)(2,1)}, bf16[576,32]{0,1:T(8,128)(2,1)S(1)}, u32[]{:S(2)}, u32[]{:S(2)}) collective-permute-start(bf16[576,32]{0,1:T(8,128)(2,1)} %param.25), channel_id=1, source_target_pairs={{0,16},{16,0},{1,17},{17,1},{2,18},{18,2},{3,19},{19,3},{4,20},{20... | collective-permute-start | bytes 110600 | tf_op jit(solution)/shard_map/ppermute | solution.py:53
  199.0 29.2 %collective-permute-start.37 = (bf16[576,256]{1,0:T(8,128)(2,1)}, bf16[576,256]{1,0:T(8,128)(2,1)}, u32[]{:S(2)}, u32[]{:S(2)}) collective-permute-start(bf16[576,256]{1,0:T(8,128)(2,1)} %get-tuple-element.339), channel_id=1, source_target_pairs={{0,16},{16,0},{1,17},{17,1},{2,18},{18,2},{3,19},{19,3},{4,20},{20... | collective-permute-start | bytes 884744 | tf_op jit(solution)/shard_map/ppermute | solution.py:53
  211.1 19.0 %collective-permute-start.38 = (bf16[256,576]{0,1:T(8,128)(2,1)S(1)}, bf16[256,576]{0,1:T(8,128)(2,1)S(1)}, u32[]{:S(2)}, u32[]{:S(2)}) collective-permute-start(bf16[256,576]{0,1:T(8,128)(2,1)S(1)} %get-tuple-element.335), channel_id=1, source_target_pairs={{0,16},{16,0},{1,17},{17,1},{2,18},{18,2},{3,19},{19,3},{4,20},{20... | collective-permute-start | bytes 884744 | tf_op jit(solution)/shard_map/ppermute | solution.py:53
  232.1 40.0 %collective-permute-start.41 = (bf16[256,2304]{1,0:T(8,128)(2,1)}, bf16[256,2304]{1,0:T(8,128)(2,1)}, u32[]{:S(2)}, u32[]{:S(2)}) collective-permute-start(bf16[256,2304]{1,0:T(8,128)(2,1)} %get-tuple-element.324), channel_id=1, source_target_pairs={{0,16},{16,0},{1,17},{17,1},{2,18},{18,2},{3,19},{19,3},{4,20},{20... | collective-permute-start | bytes 3538952 | tf_op jit(solution)/shard_map/ppermute | solution.py:53
  252.9 18.1 %collective-permute-start.42 = (bf16[256,1152]{1,0:T(8,128)(2,1)S(1)}, bf16[256,1152]{1,0:T(8,128)(2,1)S(1)}, u32[]{:S(2)}, u32[]{:S(2)}) collective-permute-start(bf16[256,1152]{1,0:T(8,128)(2,1)S(1)} %bitcast.182), channel_id=1, source_target_pairs={{0,16},{16,0},{1,17},{17,1},{2,18},{18,2},{3,19},{19,3},{4,20},{20... | collective-permute-start | bytes 1769480 | tf_op jit(solution)/shard_map/ppermute | solution.py:53
  275.0 67.6 %collective-permute-start.43 = (bf16[256,4608]{1,0:T(8,128)(2,1)}, bf16[256,4608]{1,0:T(8,128)(2,1)}, u32[]{:S(2)}, u32[]{:S(2)}) collective-permute-start(bf16[256,4608]{1,0:T(8,128)(2,1)} %fusion.12), channel_id=1, source_target_pairs={{0,16},{16,0},{1,17},{17,1},{2,18},{18,2},{3,19},{19,3},{4,20},{20... | collective-permute-start | bytes 7077896 | tf_op jit(solution)/shard_map/ppermute | solution.py:53
  347.5 56.7 %all-to-all-start.5 = ((bf16[16,1,3,72,256]{4,3,2,1,0:T(8,128)(2,1)}), bf16[16,1,3,72,256]{4,3,2,1,0:T(8,128)(2,1)S(1)}, u32[]{:S(2)}, u32[]{:S(2)}) async-start(bf16[16,1,3,72,256]{4,3,2,1,0:T(8,128)(2,1)} %attend_back.1), calls=%async_computation.5 | async-start | bytes 3538944 | tf_op jit(solution)/shard_map/all_to_all | solution.py:348
  351.3 109.8 %all-gather.11.cloned.1.call-start = ((), (), s32[]{:S(2)}) async-start(), calls=%async_computation.11 | async-start | bytes 5640192 | tf_op jit(solution)/shard_map/all_gather | solution.py:570
  351.5 17.1 %collective-permute-start.44 = (bf16[256,1152]{1,0:T(8,128)(2,1)}, bf16[256,1152]{1,0:T(8,128)(2,1)}, u32[]{:S(2)}, u32[]{:S(2)}) collective-permute-start(bf16[256,1152]{1,0:T(8,128)(2,1)} %bitcast.205), channel_id=1, source_target_pairs={{0,16},{16,0},{1,17},{17,1},{2,18},{18,2},{3,19},{19,3},{4,20},{20... | collective-permute-start | bytes 1769480 | tf_op jit(solution)/shard_map/ppermute | solution.py:53
  404.2 289.6 %all-reduce.4.cloned.1.call-start = ((), (), s32[]{:S(2)}) async-start(), calls=%async_computation.12 | async-start | bytes 10616832 | tf_op jit(solution)/shard_map/psum | solution.py:574
  416.2 41.7 %collective-permute-start.47 = (bf16[3456,256]{1,0:T(8,128)(2,1)}, bf16[3456,256]{1,0:T(8,128)(2,1)}, u32[]{:S(2)}, u32[]{:S(2)}) collective-permute-start(bf16[3456,256]{1,0:T(8,128)(2,1)} %bitcast.33), channel_id=1, source_target_pairs={{0,16},{16,0},{1,17},{17,1},{2,18},{18,2},{3,19},{19,3},{4,20},{20... | collective-permute-start | bytes 5308424 | tf_op jit(solution)/shard_map/ppermute | solution.py:53
  472.0 27.3 %all-to-all-start = ((bf16[16,11,1152]{2,1,0:T(8,128)(2,1)}), bf16[16,11,1152]{2,1,0:T(8,128)(2,1)}, u32[]{:S(2)}, u32[]{:S(2)}) async-start(bf16[16,11,1152]{2,1,0:T(8,128)(2,1)} %copy.134), calls=%async_computation | async-start | bytes 1179648 | tf_op jit(solution)/shard_map/while/body/all_to_all | solution.py:348
  480.7 8.5 %collective-permute-start.15 = (bf16[288,1152]{1,0:T(8,128)(2,1)}, bf16[288,1152]{1,0:T(8,128)(2,1)}, u32[]{:S(2)}, u32[]{:S(2)}) collective-permute-start(bf16[288,1152]{1,0:T(8,128)(2,1)} %constant_dynamic-slice_fusion.28), channel_id=1, source_target_pairs={{0,4},{4,0},{8,12},{12,8},{1,5},{5,1},{9,13},{13,9},{2,6},{6,2},{1... | collective-permute-start | bytes 1990664 | tf_op jit(solution)/shard_map/while/body/ppermute | solution.py:305
  481.0 10.8 %collective-permute-start.22 = (bf16[288,1152]{1,0:T(8,128)(2,1)S(1)}, bf16[288,1152]{1,0:T(8,128)(2,1)}, u32[]{:S(2)}, u32[]{:S(2)}) collective-permute-start(bf16[288,1152]{1,0:T(8,128)(2,1)S(1)} %constant_dynamic-slice_fusion.31), channel_id=1, source_target_pairs={{0,4},{4,0},{8,12},{12,8},{1,5},{5,1},{9,13},{13,9},{2,6},{6,2},{1... | collective-permute-start | bytes 1990664 | tf_op jit(solution)/shard_map/while/body/ppermute | solution.py:305
  483.8 26.3 %collective-permute-start.3 = (bf16[144,1152]{1,0:T(8,128)(2,1)}, bf16[144,1152]{1,0:T(8,128)(2,1)}, u32[]{:S(2)}, u32[]{:S(2)}) collective-permute-start(bf16[144,1152]{1,0:T(8,128)(2,1)} %constant_dynamic-slice_fusion.24), channel_id=1, source_target_pairs={{0,8},{4,12},{8,0},{12,4},{1,9},{5,13},{9,1},{13,5},{2,10},{6,14},... | collective-permute-start | bytes 995336 | tf_op jit(solution)/shard_map/while/body/ppermute | solution.py:305
  487.7 25.6 %collective-permute-start.10 = (bf16[144,1152]{1,0:T(8,128)(2,1)}, bf16[144,1152]{1,0:T(8,128)(2,1)}, u32[]{:S(2)}, u32[]{:S(2)}) collective-permute-start(bf16[144,1152]{1,0:T(8,128)(2,1)} %constant_dynamic-slice_fusion.27), channel_id=1, source_target_pairs={{0,1},{1,0},{2,3},{3,2},{4,5},{5,4},{6,7},{7,6},{8,9},{9,8},{10,11... | collective-permute-start | bytes 995336 | tf_op jit(solution)/shard_map/while/body/ppermute | solution.py:305
  491.3 25.5 %collective-permute-start.16 = (bf16[144,1152]{1,0:T(8,128)(2,1)}, bf16[144,1152]{1,0:T(8,128)(2,1)}, u32[]{:S(2)}, u32[]{:S(2)}) collective-permute-start(bf16[144,1152]{1,0:T(8,128)(2,1)} %constant_dynamic-slice_fusion.29), channel_id=1, source_target_pairs={{0,8},{4,12},{8,0},{12,4},{1,9},{5,13},{9,1},{13,5},{2,10},{6,14},... | collective-permute-start | bytes 995336 | tf_op jit(solution)/shard_map/while/body/ppermute | solution.py:305
  502.8 23.6 %collective-permute-start.23 = (bf16[144,1152]{1,0:T(8,128)(2,1)}, bf16[144,1152]{1,0:T(8,128)(2,1)}, u32[]{:S(2)}, u32[]{:S(2)}) collective-permute-start(bf16[144,1152]{1,0:T(8,128)(2,1)} %constant_dynamic-slice_fusion.32), channel_id=1, source_target_pairs={{0,1},{1,0},{2,3},{3,2},{4,5},{5,4},{6,7},{7,6},{8,9},{9,8},{10,11... | collective-permute-start | bytes 995336 | tf_op jit(solution)/shard_map/while/body/ppermute | solution.py:305
  506.4 128.2 %all-to-all-start.1 = ((bf16[16,2,11,1152]{3,1,2,0:T(2,128)(2,1)}), bf16[16,2,11,1152]{3,1,2,0:T(2,128)(2,1)S(1)}, u32[]{:S(2)}, u32[]{:S(2)}) async-start(bf16[16,2,11,1152]{3,1,2,0:T(2,128)(2,1)} %broadcast_in_dim.57), calls=%async_computation.1 | async-start | bytes 1622016 | tf_op jit(solution)/shard_map/while/body/all_to_all | solution.py:348
  511.4 43.9 %collective-permute-start.4 = (bf16[72,1152]{1,0:T(8,128)(2,1)S(1)}, bf16[72,1152]{1,0:T(8,128)(2,1)S(1)}, u32[]{:S(2)}, u32[]{:S(2)}) collective-permute-start(bf16[72,1152]{1,0:T(8,128)(2,1)S(1)} %constant_dynamic-slice_fusion.25), channel_id=1, source_target_pairs={{0,1},{1,0},{2,3},{3,2},{4,5},{5,4},{6,7},{7,6},{8,9},{9,8},{10,11... | collective-permute-start | bytes 497672 | tf_op jit(solution)/shard_map/while/body/ppermute | solution.py:305
  514.3 77.3 %collective-permute-start.11 = (bf16[144,1152]{1,0:T(8,128)(2,1)S(1)}, bf16[144,1152]{1,0:T(8,128)(2,1)S(1)}, u32[]{:S(2)}, u32[]{:S(2)}) collective-permute-start(bf16[144,1152]{1,0:T(8,128)(2,1)S(1)} %add_convert_fusion.41), channel_id=1, source_target_pairs={{0,2},{1,3},{2,0},{3,1},{4,6},{5,7},{6,4},{7,5},{8,10},{9,11},{10,... | collective-permute-start | bytes 995336 | tf_op jit(solution)/shard_map/while/body/ppermute | solution.py:305
  517.9 45.9 %collective-permute-start.17 = (bf16[72,1152]{1,0:T(8,128)(2,1)S(1)}, bf16[72,1152]{1,0:T(8,128)(2,1)S(1)}, u32[]{:S(2)}, u32[]{:S(2)}) collective-permute-start(bf16[72,1152]{1,0:T(8,128)(2,1)S(1)} %constant_dynamic-slice_fusion.30), channel_id=1, source_target_pairs={{0,1},{1,0},{2,3},{3,2},{4,5},{5,4},{6,7},{7,6},{8,9},{9,8},{10,11... | collective-permute-start | bytes 497672 | tf_op jit(solution)/shard_map/while/body/ppermute | solution.py:305
  527.5 66.5 %collective-permute-start.24 = (bf16[144,1152]{1,0:T(8,128)(2,1)S(1)}, bf16[144,1152]{1,0:T(8,128)(2,1)S(1)}, u32[]{:S(2)}, u32[]{:S(2)}) collective-permute-start(bf16[144,1152]{1,0:T(8,128)(2,1)S(1)} %add_convert_fusion.49), channel_id=1, source_target_pairs={{0,2},{1,3},{2,0},{3,1},{4,6},{5,7},{6,4},{7,5},{8,10},{9,11},{10,... | collective-permute-start | bytes 995336 | tf_op jit(solution)/shard_map/while/body/ppermute | solution.py:305
  555.3 33.2 %collective-permute-start.5 = (bf16[72,1152]{1,0:T(8,128)(2,1)S(1)}, bf16[72,1152]{1,0:T(8,128)(2,1)S(1)}, u32[]{:S(2)}, u32[]{:S(2)}) collective-permute-start(bf16[72,1152]{1,0:T(8,128)(2,1)S(1)} %add_convert_fusion.38), channel_id=1, source_target_pairs={{0,2},{1,3},{2,0},{3,1},{4,6},{5,7},{6,4},{7,5},{8,10},{9,11},{10,... | collective-permute-start | bytes 497672 | tf_op jit(solution)/shard_map/while/body/ppermute | solution.py:305
  563.8 27.7 %collective-permute-start.18 = (bf16[72,1152]{1,0:T(8,128)(2,1)S(1)}, bf16[72,1152]{1,0:T(8,128)(2,1)S(1)}, u32[]{:S(2)}, u32[]{:S(2)}) collective-permute-start(bf16[72,1152]{1,0:T(8,128)(2,1)S(1)} %add_convert_fusion.46), channel_id=1, source_target_pairs={{0,2},{1,3},{2,0},{3,1},{4,6},{5,7},{6,4},{7,5},{8,10},{9,11},{10,... | collective-permute-start | bytes 497672 | tf_op jit(solution)/shard_map/while/body/ppermute | solution.py:305
  591.8 14.0 %collective-permute-start.12 = (bf16[144,1152]{1,0:T(8,128)(2,1)S(1)}, bf16[144,1152]{1,0:T(8,128)(2,1)S(1)}, u32[]{:S(2)}, u32[]{:S(2)}) collective-permute-start(bf16[144,1152]{1,0:T(8,128)(2,1)S(1)} %add_convert_fusion.42), channel_id=1, source_target_pairs={{0,8},{4,12},{8,0},{12,4},{1,9},{5,13},{9,1},{13,5},{2,10},{6,14},... | collective-permute-start | bytes 995336 | tf_op jit(solution)/shard_map/while/body/ppermute | solution.py:305
  594.1 20.4 %collective-permute-start.25 = (bf16[144,1152]{1,0:T(8,128)(2,1)S(1)}, bf16[144,1152]{1,0:T(8,128)(2,1)S(1)}, u32[]{:S(2)}, u32[]{:S(2)}) collective-permute-start(bf16[144,1152]{1,0:T(8,128)(2,1)S(1)} %add_convert_fusion.50), channel_id=1, source_target_pairs={{0,8},{4,12},{8,0},{12,4},{1,9},{5,13},{9,1},{13,5},{2,10},{6,14},... | collective-permute-start | bytes 995336 | tf_op jit(solution)/shard_map/while/body/ppermute | solution.py:305
  595.8 25.8 %collective-permute-start.7 = (bf16[144,1152]{1,0:T(8,128)(2,1)S(1)}, bf16[144,1152]{1,0:T(8,128)(2,1)S(1)}, u32[]{:S(2)}, u32[]{:S(2)}) collective-permute-start(bf16[144,1152]{1,0:T(8,128)(2,1)S(1)} %maximum_select_fusion.20), channel_id=1, source_target_pairs={{0,8},{4,12},{8,0},{12,4},{1,9},{5,13},{9,1},{13,5},{2,10},{6,14},... | collective-permute-start | bytes 995336 | tf_op jit(solution)/shard_map/while/body/ppermute | solution.py:305
  599.0 33.1 %collective-permute-start.20 = (bf16[144,1152]{1,0:T(8,128)(2,1)S(1)}, bf16[144,1152]{1,0:T(8,128)(2,1)S(1)}, u32[]{:S(2)}, u32[]{:S(2)}) collective-permute-start(bf16[144,1152]{1,0:T(8,128)(2,1)S(1)} %maximum_select_fusion.25), channel_id=1, source_target_pairs={{0,8},{4,12},{8,0},{12,4},{1,9},{5,13},{9,1},{13,5},{2,10},{6,14},... | collective-permute-start | bytes 995336 | tf_op jit(solution)/shard_map/while/body/ppermute | solution.py:305
  605.8 27.3 %collective-permute-start.13 = (bf16[144,1152]{1,0:T(8,128)(2,1)S(1)}, bf16[144,1152]{1,0:T(8,128)(2,1)S(1)}, u32[]{:S(2)}, u32[]{:S(2)}) collective-permute-start(bf16[144,1152]{1,0:T(8,128)(2,1)S(1)} %add_convert_fusion.43), channel_id=1, source_target_pairs={{0,1},{1,0},{2,3},{3,2},{4,5},{5,4},{6,7},{7,6},{8,9},{9,8},{10,11... | collective-permute-start | bytes 995336 | tf_op jit(solution)/shard_map/while/body/ppermute | solution.py:305
  615.3 31.7 %collective-permute-start.26 = (bf16[144,1152]{1,0:T(8,128)(2,1)}, bf16[144,1152]{1,0:T(8,128)(2,1)}, u32[]{:S(2)}, u32[]{:S(2)}) collective-permute-start(bf16[144,1152]{1,0:T(8,128)(2,1)} %add_convert_fusion.51), channel_id=1, source_target_pairs={{0,1},{1,0},{2,3},{3,2},{4,5},{5,4},{6,7},{7,6},{8,9},{9,8},{10,11... | collective-permute-start | bytes 995336 | tf_op jit(solution)/shard_map/while/body/ppermute | solution.py:305
  622.6 28.0 %collective-permute-start.8 = (bf16[288,1152]{1,0:T(8,128)(2,1)}, bf16[288,1152]{1,0:T(8,128)(2,1)}, u32[]{:S(2)}, u32[]{:S(2)}) collective-permute-start(bf16[288,1152]{1,0:T(8,128)(2,1)} %maximum_select_fusion.21), channel_id=1, source_target_pairs={{0,4},{4,0},{8,12},{12,8},{1,5},{5,1},{9,13},{13,9},{2,6},{6,2},{1... | collective-permute-start | bytes 1990664 | tf_op jit(solution)/shard_map/while/body/ppermute | solution.py:305
  633.1 20.6 %collective-permute-start.21 = (bf16[288,1152]{1,0:T(8,128)(2,1)}, bf16[288,1152]{1,0:T(8,128)(2,1)}, u32[]{:S(2)}, u32[]{:S(2)}) collective-permute-start(bf16[288,1152]{1,0:T(8,128)(2,1)} %maximum_select_fusion.26), channel_id=1, source_target_pairs={{0,4},{4,0},{8,12},{12,8},{1,5},{5,1},{9,13},{13,9},{2,6},{6,2},{1... | collective-permute-start | bytes 1990664 | tf_op jit(solution)/shard_map/while/body/ppermute | solution.py:305
  634.1 22.8 %collective-permute-start.14 = (bf16[288,1152]{1,0:T(8,128)(2,1)}, bf16[288,1152]{1,0:T(8,128)(2,1)}, u32[]{:S(2)}, u32[]{:S(2)}) collective-permute-start(bf16[288,1152]{1,0:T(8,128)(2,1)} %maximum_select_fusion.23), channel_id=1, source_target_pairs={{0,4},{4,0},{8,12},{12,8},{1,5},{5,1},{9,13},{13,9},{2,6},{6,2},{1... | collective-permute-start | bytes 1990664 | tf_op jit(solution)/shard_map/while/body/ppermute | solution.py:305
  648.4 11.6 %collective-permute-start.27 = (bf16[288,1152]{1,0:T(8,128)(2,1)S(1)}, bf16[288,1152]{1,0:T(8,128)(2,1)S(1)}, u32[]{:S(2)}, u32[]{:S(2)}) collective-permute-start(bf16[288,1152]{1,0:T(8,128)(2,1)S(1)} %maximum_select_fusion.28), channel_id=1, source_target_pairs={{0,4},{4,0},{8,12},{12,8},{1,5},{5,1},{9,13},{13,9},{2,6},{6,2},{1... | collective-permute-start | bytes 1990664 | tf_op jit(solution)/shard_map/while/body/ppermute | solution.py:305
  (102 other events, 974.5 us)
Sparse Core Ops, SparseCore 0:
  19.0 53.0 all-gather.4
  75.0 85.9 all-gather.6
  163.2 60.7 all-gather.8
  297.2 94.9 reduce-scatter.1
  404.4 56.7 all-gather.10
  468.6 192.8 all-reduce.3

commit v2 on v1

--- a/solution.py
+++ b/solution.py
@@ -329,23 +329,32 @@
     return [(axis, 1 << i) for i in range(lax.axis_size(axis).bit_length() - 1)]
 
 
-def tile_sum(value, cols_first):
-    rows, cols = bits_of("row"), bits_of("col")
-    if cols_first:
-        halves, wholes = rows[:1] + cols[:-1], cols[-1:] + rows[1:]
-    else:
-        halves, wholes = rows + cols[:-1], cols[-1:]
-    for axis, bit in halves:
+def tile_halved(value):
+    bits = bits_of("row") + bits_of("col")
+    for axis, bit in bits[:-1]:
         value = halved(value, axis, bit)
-    for axis, bit in wholes:
-        value = added(value, swapped(value, axis, bit))
-    for axis, bit in halves[::-1]:
+    axis, bit = bits[-1]
+    return added(value, swapped(value, axis, bit))
+
+
+def tile_doubled(value):
+    bits = bits_of("row") + bits_of("col")
+    for axis, bit in bits[-2::-1]:
         value = doubled(value, axis, bit)
     return value
 
 
 def exchange(x):
     return lax.all_to_all(x, RC, split_axis=0, concat_axis=0, tiled=True)
+
+
+def blank(shape, dtype):
+    return pl.pallas_call(
+        lambda ref: None,
+        out_specs=pl.BlockSpec(memory_space=pl.ANY),
+        out_shape=jax.ShapeDtypeStruct(shape, dtype),
+        name="blank",
+    )()
 
 
 def summed_apart(small, items, finish):
@@ -354,18 +363,19 @@
     imgs = lax.axis_size("img")
 
     def body(_, state):
-        parts = jnp.sum(exchange(state[0][0]).astype(F32), axis=0).astype(BF)
+        parts = jnp.sum(exchange(state[0]).astype(F32), axis=0).astype(BF)
         parts = jnp.stack(swap_full(parts))
         parts = exchange(jnp.broadcast_to(parts[None], (tiles,) + parts.shape))
         parts = parts.transpose(1, 0, 2, 3)
         done = finish(parts.reshape(imgs, tiles * each, width))
-        return parts, done, [tile_sum(value, c % 2 == 1) for c, value in enumerate(state[2])]
-
-    start = jnp.broadcast_to(small[None], (imgs,) + small.shape)
+        sums = [tile_halved(value) for value in state[1]]
+        late = len(sums) // 2
+        sums[late:], done = lax.optimization_barrier((sums[late:], done))
+        return parts[0], [tile_doubled(value) for value in sums], done
+
     empty = jax.eval_shape(finish, jax.ShapeDtypeStruct((imgs, tiles * each, width), BF))
-    empty = jnp.zeros(empty.shape, empty.dtype)
-    small, done, items = lax.fori_loop(0, once, body, (start, empty, items))
-    return small.reshape(imgs, tiles * each, width), done, items
+    empty = jax.tree.map(lambda item: blank(item.shape, item.dtype), empty)
+    return lax.fori_loop(0, once, body, (small, items, empty))[1:]
 
 
 def outer_kernel(left_ref, right_ref, out_ref):
@@ -425,10 +435,12 @@
     order = quad_order(rows_n, cols_n)
 
     o_qkv, sent = other_rows(w_qkv)
-    w_straight = tied(w_proj, sent)
-    o_proj = [send_down(w_straight, k) for k in range(1, imgs)]
     o_up, sent = other_rows(tied(w_up, sent))
-    o_down, _ = other_rows(tied(w_down, sent))
+    lower = w_down.shape[0] // 3
+    w_straight = tied(w_down[:lower], sent)
+    o_low = [send_down(w_straight, k) for k in range(1, imgs)]
+    w_straight = tied(w_down[lower : 2 * lower], o_low)
+    o_mid = [send_down(w_straight, k) for k in range(1, imgs)]
     wp = join_own([w_patch] + [send_down(w_patch, k) for k in range(1, imgs)], 0)
     wout = join_own([w_out] + [send_down(w_out, k) for k in range(1, imgs)], 0)
 
@@ -490,6 +502,8 @@
 
     x0 = tokens3(dotd(pieces, wp, 1, 0)) + positions
     a1 = modulate(x0, shift1, scale1).astype(BF).reshape(rows, width)
+    o_proj, _ = other_rows(tied(w_proj, a1))
+    o_high, _ = other_rows(tied(w_down[2 * lower :], a1))
     a1_parts = split_own(a1, 1)
     a1_all = jnp.concatenate(swap_parts(a1_parts), 0)
 
@@ -510,10 +524,10 @@
         qkv = qkv + dotd(other, widened(part, other.shape[0], 1), 0, 1)
     qkv = qkv.astype(BF).reshape(3, tiles, per, head_dim, rows).transpose(1, 2, 0, 3, 4)
     qkv = exchange(qkv)
-    qkv, o_proj = lax.optimization_barrier((qkv, o_proj))
+    qkv, o_low = lax.optimization_barrier((qkv, o_low))
     att, lse = attend(canvas_kind, qkv, order, tile_tok, factor)
     att = exchange(att).reshape(width, rows)
-    att, a1_all = lax.optimization_barrier((att, a1_all))
+    att, a1_all, o_mid = lax.optimization_barrier((att, a1_all, o_mid))
     att_parts = split_own(att, 0)
     att_all = jnp.concatenate(swap_parts(att_parts), 1)
     proj = dotd(att_parts[0], w_proj, 0, 0)
@@ -528,8 +542,13 @@
     hid = gelu_tanh(pre).astype(BF)
     hid, att_all, a2_all = lax.optimization_barrier((hid, att_all, a2_all))
     hid_parts = split_own(hid, 1)
-    hid_all = jnp.concatenate(swap_parts(hid_parts), 0)
-    down = tokens3(product(hid_parts, w_down, o_down))
+    hid_all = swap_parts(hid_parts)
+    down = dotd(hid_parts[0], w_down, 1, 0)
+    for part, low, mid, high in zip(hid_parts[1:], o_low, o_mid, o_high):
+        straight = jnp.concatenate([low, mid], axis=0)
+        down = down + dotd(part[:, : 2 * lower], straight, 1, 0)
+        down = down + dotd(widened(part[:, 2 * lower :], high.shape[0], 1), high, 1, 0)
+    down = tokens3(down)
     x2 = x1 + gate2[:, None, :] * down
     af = modulate(x2, shiftf, scalef).astype(BF).reshape(rows, width)
     outp = dotd(af, wout, 1, 0)
@@ -540,15 +559,20 @@
     dx2, dshiftf, dscalef = pull(daf)
     dgate2 = jnp.sum(dx2 * down, axis=1)
     ddown = (gate2[:, None, :] * dx2).astype(BF).reshape(rows, width)
-    ddown_all = jnp.concatenate(swap_full(ddown), 0)
-    dhid = join_own(back_product(ddown, w_down, o_down), 1)
+    ddown_all = swap_full(ddown)
+    dhid = [dotd(ddown, w_down, 1, 1)]
+    for low, mid, high in zip(o_low, o_mid, o_high):
+        straight = jnp.concatenate([low, mid], axis=0)
+        last = w_down.shape[0] - 2 * lower
+        items = [dotd(ddown, straight, 1, 1), dotd(ddown, high, 1, 1)[:, :last]]
+        dhid.append(jnp.concatenate(items, axis=1))
+    dhid = join_own(dhid, 1)
     _, pull = jax.vjp(gelu_tanh, pre)
     dpre = pull(dhid)[0].astype(BF)
-    dpre, hid_all = lax.optimization_barrier((dpre, hid_all))
-    dpre_all = jnp.concatenate(swap_full(dpre), 0)
+    dpre_all = swap_full(dpre)
     da2 = tokens3(join_own(back_product(dpre, w_up, o_up), 1))
-    da2, ddown_all = lax.optimization_barrier((da2, ddown_all))
-    g_down = dotd(hid_all, ddown_all, 0, 0).astype(BF)
+    da2, hid_all, ddown_all = lax.optimization_barrier((da2, hid_all, ddown_all))
+    g_down = dotd(jnp.concatenate(hid_all, 0), jnp.concatenate(ddown_all, 0), 0, 0).astype(BF)
     da2, g_down = lax.optimization_barrier((da2, g_down))
     g_down = lax.psum_scatter(g_down, RC, scatter_dimension=0, tiled=True)
     _, pull = jax.vjp(modulate, x1, shift2, scale2)
@@ -565,8 +589,11 @@
     dqkv = attend_back(canvas_kind, qkv, datt, lse, order, tile_tok, factor)
     dqkv, dpre_all = lax.optimization_barrier((dqkv, dpre_all))
     dqkv = exchange(dqkv)
-    g_up = dotd(a2_all, dpre_all, 0, 0).astype(BF)
-    dqkv, g_up, g_down, dproj_all = lax.optimization_barrier((dqkv, g_up, g_down, dproj_all))
+    g_up = dotd(a2_all, jnp.concatenate(dpre_all, 0), 0, 0).astype(BF)
+    g_proj = dotd(att_all, dproj_all, 1, 0).astype(BF)
+    dqkv, g_up, g_down, g_proj, outp, g_out = lax.optimization_barrier(
+        (dqkv, g_up, g_down, g_proj, outp, g_out)
+    )
     g_down = lax.all_gather(g_down, RC, axis=0, tiled=True)
     dqkv = dqkv.transpose(2, 0, 1, 3, 4).reshape(3 * width, rows)
     dqkv_all = jnp.concatenate(swap_full(dqkv), 1)
@@ -576,7 +603,6 @@
     for other in o_qkv:
         da1.append(dotd(dqkv, other, 0, 1)[:, : w_qkv.shape[0]])
     da1 = tokens3(join_own(da1, 1))
-    g_proj = dotd(att_all, dproj_all, 1, 0).astype(BF)
     g_att = [
         dotd(a1_all, dqkv_all[c * width : (c + 1) * width], 0, 1).astype(BF) for c in range(3)
     ]
@@ -601,25 +627,27 @@
     def split_small(value):
         return value[:, n_patch + n_out : count].reshape(imgs * step, 8 * width)
 
-    def back_cond(value):
+    def finish(value):
+        sums = jnp.sum(value[:, : n_patch + n_out].astype(F32), axis=0)
         dmods = split_small(value)
         dsilu = dotd(dmods[:, : 6 * width], w_ada, 1, 1)
         dsilu = dsilu + dotd(dmods[:, 6 * width :], w_final_ada, 1, 1)
         dsilu = [dsilu[k * step : (k + 1) * step] for k in range(imgs)]
         dsilu = [dsilu[0]] + [send_up(dsilu[imgs - k], imgs - k) for k in range(1, imgs)]
-        return join_own(dsilu, 1)
-
-    small, dsilu, g_att = summed_apart(
-        small.reshape(tiles, each, width), g_att + [g_proj], back_cond
-    )
+        return (
+            sums,
+            join_own(dsilu, 1),
+            outer(silu_all, dmods[:, : 6 * width], width),
+            outer(silu_all, dmods[:, 6 * width :], width),
+            g_down.astype(F32),
+        )
+
+    g_att, done = summed_apart(small.reshape(tiles, each, width), g_att + [g_proj], finish)
+    sums, dsilu, g_ada, g_fada, g_down = done
     g_qkv = jnp.concatenate(g_att[:3], axis=1)
     g_proj = g_att[3]
-    sums = jnp.sum(small[:, : n_patch + n_out].astype(F32), axis=0)
     g_patch = split_own(sums[:n_patch], 0)[0]
     g_out = split_own(sums[n_patch:], 1)[0].T
-    dmods = split_small(small)
-    g_ada = outer(silu_all, dmods[:, : 6 * width], width)
-    g_fada = outer(silu_all, dmods[:, 6 * width :], width)
     dsilu = dsilu.reshape(local_n, slots, width)
     _, pull = jax.vjp(swish, cond)
     cond_grad = pull(dsilu)[0]
@@ -637,7 +665,7 @@
         g_qkv.astype(F32),
         g_proj.astype(F32),
         g_up.astype(F32),
-        g_down.astype(F32),
+        g_down,
         g_ada,
         g_fada,
         g_out,

time: 720 us -> 671 us (0.932)
  waiting for transfers between devices: 285 us -> 244 us
  other arithmetic: 103 us -> 84 us
  local copies, waits for them, and re-layouts: 60.7 us -> 73.1 us
    all_to_all x5, waiting for transfers between devices: 72 us -> 27.1 us  [exchange(): return lax.all_to_all(x, RC, split_axis=0, concat_axis=0, tiled=True)]
    ppermute x16 -> x18, waiting for transfers between devices: 93.1 us -> 111 us  [send_down(): lax.ppermute(value, 'img', [(j, (j - k) % size) for j in range(size)])]
    ppermute x26 -> x28, waiting for transfers between devices: 98.4 us -> 82.2 us  [swapped(): lax.ppermute(value, axis, [(j, j ^ bit) for j in range(lax.axis_size(axis...]
    concatenate x4 -> x0, other arithmetic: 11.3 us -> none  [the longest x1 4.87 us: local(): dpre_all = jnp.concatenate(swap_full(dpre), 0)]
    unnamed x171 -> x162, local copies, waits for them, and re-layouts: 15.1 us -> 22.6 us
    ppermute x16 -> x18, starting transfers between devices: 25.9 us -> 19.1 us  [send_down(): lax.ppermute(value, 'img', [(j, (j - k) % size) for j in range(size)])]
    select_n x10 -> x12, other arithmetic: 15.5 us -> 9.54 us  [doubled(): jnp.where(upper == 0, jnp.concatenate([value, got], 0), jnp.concatenate([...]
    dot_general x32 -> x34, matrix products: 107 us -> 102 us  [dotd(): lax.dot_general(left, right, (((ldim,), (rdim,)), ((), ())), preferred_el...]
  transfers between devices with their start and end apart: 59 -> 64, of which waited for: 29 -> 34; matrix products, arithmetic and copies ran while one was open for 34% -> 35% of each run, Pallas kernels for 6% -> 7%
where the time goes in v2:
time: 671 us; the launch traced here: 661 us
  waiting for transfers between devices  244 us (36%)
  matrix products  102 us (15%)
  other arithmetic  84 us (13%)
  local copies, waits for them, and re-layouts  73.1 us (11%)
  starting transfers between devices  72 us (11%)
  Pallas kernels  46.7 us (7%)
  blocking collectives  23.3 us (3%)
  between operations  15.9 us (2%)
    ppermute x18, waiting for transfers between devices, send_down(): lax.ppermute(value, 'img', [(j, (j - k) % size) for j in range(size)])  111 us
    dot_general x34, matrix products, dotd(): lax.dot_general(left, right, (((ldim,), (rdim,)), ((), ())), preferred_el...  102 us
    ppermute x28, waiting for transfers between devices, swapped(): lax.ppermute(value, axis, [(j, j ^ bit) for j in range(lax.axis_size(axis...  82.2 us
    all_to_all x5, waiting for transfers between devices, exchange(): return lax.all_to_all(x, RC, split_axis=0, concat_axis=0, tiled=True)  27.1 us
    ppermute x28, starting transfers between devices, swapped(): lax.ppermute(value, axis, [(j, j ^ bit) for j in range(lax.axis_size(axis...  25.3 us
    all_to_all x1, blocking collectives, exchange(): return lax.all_to_all(x, RC, split_axis=0, concat_axis=0, tiled=True)  23.3 us
    unnamed x162, local copies, waits for them, and re-layouts  22.6 us
    all_to_all x5, starting transfers between devices, exchange(): return lax.all_to_all(x, RC, split_axis=0, concat_axis=0, tiled=True)  22.4 us
  transfers between devices with their start and end apart: 64, of which 34 were waited for; matrix products, arithmetic and copies ran while one was open for 35% of the time, Pallas kernels for 7%

profile of v2, /device:TPU:0, one launch (start us, length us, event | category | flops | bytes accessed | tf_op | source)
XLA Modules:
  0.0 661.3 jit_solution(16043976873250238868)
XLA Ops:
  13.5 5.0 collective-permute-done.35
  23.9 4.0 collective-permute-done.31
  35.2 4.6 collective-permute-done.34
  41.5 4.2 collective-permute-done.41
  47.9 7.0 %collective-permute-done.36 = bf16[40,4608]{1,0:T(8,128)(2,1)} collective-permute-done((bf16[40,4608]{1,0:T(8,128)(2,1)S(1)}, bf16[40,4608]{1,0:T(8,128)(2,1)}, u32[]{:S(2)}, u32[]{:S(2)}) %collective-permute-start.36) | collective-permute-done | bytes 368672 | tf_op jit(solution)/shard_map/ppermute | solution.py:53
  60.7 5.6 convolution_bitcast_fusion
  66.3 6.1 all-gather.6.cloned.1.call-done
  72.4 6.2 fusion.5
  85.3 4.6 all-to-all-start.2
  89.9 4.7 fusion.77
  96.1 39.6 %collective-permute-done.37 = bf16[768,1152]{1,0:T(8,128)(2,1)} collective-permute-done((bf16[768,1152]{1,0:T(8,128)(2,1)S(1)}, bf16[768,1152]{1,0:T(8,128)(2,1)}, u32[]{:S(2)}, u32[]{:S(2)}) %collective-permute-start.37) | collective-permute-done | bytes 1769504 | tf_op jit(solution)/shard_map/ppermute | solution.py:53
  138.1 14.6 %attend.1 = (bf16[16,1,72,256]{3,2,1,0:T(8,128)(2,1)}, f32[1,4,1,1024]{3,2,1,0:T(1,128)}) custom-call(s32[4]{0:T(128)} %refs_0_.3, bf16[16,1,3,72,256]{4,3,2,1,0:T(8,128)(2,1)} %all-to-all-done.2.refs_1_), custom_call_target="tpu_custom_call" | custom-call | flops 10000000000 | bytes 40000000 | tf_op jit(solution)/shard_map/attend/pallas_call | solution.py:245
  152.7 4.9 all-to-all-start.3
  163.8 14.5 %collective-permute-done.38 = bf16[576,32]{0,1:T(8,128)(2,1)} collective-permute-done((bf16[576,32]{0,1:T(8,128)(2,1)S(1)}, bf16[576,32]{0,1:T(8,128)(2,1)}, u32[]{:S(2)}, u32[]{:S(2)}) %collective-permute-start.38) | collective-permute-done | bytes 36896 | tf_op jit(solution)/shard_map/ppermute | solution.py:53
  179.2 6.5 collective-permute-done.44
  207.0 6.7 %fusion.83 = f32[256,4608]{1,0:T(8,128)} fusion(bf16[256,576]{0,1:T(8,128)(2,1)S(1)} %get-tuple-element.499, bf16[576,4608]{1,0:T(8,128)(2,1)} %param.21), kind=kOutput, calls=%fused_computation.291 | convolution fusion | flops 1358954496 | bytes 10321920 | tf_op jit(solution)/shard_map/dot_general | solution.py:46
  214.1 9.7 %multiply_convert_fusion = (bf16[256,4608]{1,0:T(8,128)(2,1)S(1)}, f32[256,4608]{1,0:T(8,128)}) fusion(f32[256,4608]{1,0:T(8,128)} %fusion.83, bf16[640,4608]{1,0:T(8,128)(2,1)} %all-gather.10.cloned.1.call-done, bf16[256,576]{0,1:T(8,128)(2,1)} %get-tuple-element.498), kind=kOutput, calls=%fused_computation.72 | convolution fusion | flops 1521745920 | bytes 17989632 | tf_op jit(solution)/shard_map/dot_general | solution.py:46
  232.3 4.3 fusion.84
  253.4 4.2 fusion.12
  272.5 7.4 %convolution_convert_fusion = bf16[2304,1152]{1,0:T(8,128)(2,1)} fusion(bf16[256,2304]{1,0:T(8,128)(2,1)} %collective-permute-done.45, bf16[256,2304]{1,0:T(8,128)(2,1)} %copy-done.22, bf16[256,1152]{1,0:T(8,128)(2,1)} %collective-permute-done.46, bf16[256,1152]{1,0:T(8,128)(2,1)S(1)} %bitcast.177), kind=kOutput, calls=%fused_computation.51 | convolution fusion | flops 2727641088 | bytes 8847360 | tf_op jit(solution)/shard_map/dot_general | solution.py:46
  287.7 23.3 %all_to_all.40.refs_2_ = bf16[16,1,72,256]{3,2,1,0:T(8,128)(2,1)} all-to-all(bf16[16,1,72,256]{3,2,1,0:T(8,128)(2,1)S(1)} %bitcast.190), channel_id=1, replica_groups=mesh['img'=2,'row'=4,'col'=4] {'row','col'}, dimensions={0} | all-to-all | bytes 1179648 | tf_op jit(solution)/shard_map/all_to_all | solution.py:348
  311.0 20.3 %attend_back.1 = bf16[16,1,3,72,256]{4,3,2,1,0:T(8,128)(2,1)} custom-call(s32[4]{0:T(128)} %refs_0_.3, bf16[16,1,3,72,256]{4,3,2,1,0:T(8,128)(2,1)} %all-to-all-done.2.refs_1_, bf16[16,1,72,256]{3,2,1,0:T(8,128)(2,1)} %all_to_all.40.refs_2_, f32[1,4,1,1024]{3,2,1,0:T(1,128)} %get-tuple-element.327.refs_3_), custom_call_target="tpu_custom_call" | custom-call | flops 10000000000 | bytes 40000000 | tf_op jit(solution)/shard_map/attend_back/pallas_call | solution.py:277
  331.3 4.6 all-to-all-start.5
  337.6 14.4 %collective-permute-done.48 = bf16[256,1152]{1,0:T(8,128)(2,1)} collective-permute-done((bf16[256,1152]{1,0:T(8,128)(2,1)}, bf16[256,1152]{1,0:T(8,128)(2,1)}, u32[]{:S(2)}, u32[]{:S(2)}) %collective-permute-start.48) | collective-permute-done | bytes 589856 | tf_op jit(solution)/shard_map/ppermute | solution.py:53
  355.1 7.7 %convolution_convert_fusion.1 = bf16[576,4608]{1,0:T(8,128)(2,1)} fusion(bf16[512,576]{0,1:T(8,128)(2,1)S(1)} %copy-done.30, bf16[256,4608]{1,0:T(8,128)(2,1)} %collective-permute-done.47, bf16[256,4608]{1,0:T(8,128)(2,1)} %fusion.12), kind=kOutput, calls=%fused_computation.52 | convolution fusion | flops 2730000384 | bytes 10616832 | tf_op jit(solution)/shard_map/dot_general | solution.py:46
  362.8 26.1 %all-to-all-done.5 = bf16[16,1,3,72,256]{4,3,2,1,0:T(8,128)(2,1)} async-done(((bf16[16,1,3,72,256]{4,3,2,1,0:T(8,128)(2,1)}), bf16[16,1,3,72,256]{4,3,2,1,0:T(8,128)(2,1)}, u32[]{:S(2)}, u32[]{:S(2)}) %all-to-all-start.5) | async-done | bytes 1769504 | tf_op jit(solution)/shard_map/all_to_all | solution.py:348
  393.9 4.2 fusion.89
  418.6 15.8 %collective-permute-done.51 = bf16[3456,256]{1,0:T(8,128)(2,1)} collective-permute-done((bf16[3456,256]{1,0:T(8,128)(2,1)}, bf16[3456,256]{1,0:T(8,128)(2,1)}, u32[]{:S(2)}, u32[]{:S(2)}) %collective-permute-start.51) | collective-permute-done | bytes 1769504 | tf_op jit(solution)/shard_map/ppermute | solution.py:53
  434.4 4.1 pad_maximum_fusion.3
  438.5 4.7 all-gather.14.cloned.1.call-done
  449.8 185.3 %while.31 = (s32[]{:T(128)}, bf16[16,11,1152]{2,0,1:T(8,128)(2,1)S(1)}, bf16[576,1152]{1,0:T(8,128)(2,1)S(1)}, bf16[576,1152]{1,0:T(8,128)(2,1)}, bf16[576,1152]...) while((s32[]{:T(128)}, ...), condition=%wide.region_25.26_spmd, body=%wide.region_22.25_spmd.sunk | while | flops 395250112 | bytes 143718128 | solution.py:378
  460.9 7.3 %convert_element_type.653 = f32[2304,1152]{1,0:T(8,128)} convert(bf16[2304,1152]{1,0:T(8,128)(2,1)} %get-tuple-element.718) | non-fusion elementwise | flops 2654208 | bytes 15925248 | tf_op jit(solution)/shard_map/while/body/convert_element_type | solution.py:642
  485.5 4.7 all-to-all-start.1
  496.4 8.5 %collective-permute-done.16 = bf16[144,1152]{1,0:T(8,128)(2,1)} collective-permute-done((bf16[144,1152]{1,0:T(8,128)(2,1)}, bf16[144,1152]{1,0:T(8,128)(2,1)}, u32[]{:S(2)}, u32[]{:S(2)}) %collective-permute-start.16) | collective-permute-done | bytes 331808 | tf_op jit(solution)/shard_map/while/body/ppermute | solution.py:305
  506.1 7.6 %collective-permute-done.20 = bf16[144,1152]{1,0:T(8,128)(2,1)} collective-permute-done((bf16[144,1152]{1,0:T(8,128)(2,1)}, bf16[144,1152]{1,0:T(8,128)(2,1)}, u32[]{:S(2)}, u32[]{:S(2)}) %collective-permute-start.20) | collective-permute-done | bytes 331808 | tf_op jit(solution)/shard_map/while/body/ppermute | solution.py:305
  519.5 6.3 collective-permute-done.10
  525.9 5.9 collective-permute-done.17
  532.4 5.9 collective-permute-done.21
  541.7 11.3 %collective-permute-done.11 = bf16[72,1152]{1,0:T(8,128)(2,1)S(1)} collective-permute-done((bf16[72,1152]{1,0:T(8,128)(2,1)S(1)}, bf16[72,1152]{1,0:T(8,128)(2,1)S(1)}, u32[]{:S(2)}, u32[]{:S(2)}) %collective-permute-start.11) | collective-permute-done | bytes 165920 | tf_op jit(solution)/shard_map/while/body/ppermute | solution.py:305
  561.3 4.6 collective-permute-done.12
  567.5 5.1 collective-permute-done.6
  576.3 5.8 fusion.143
  587.7 8.0 %outer.10 = f32[576,6912]{1,0:T(8,128)} custom-call(bf16[32,576]{1,0:T(8,128)(2,1)S(1)} %get-tuple-element.717.left_ref, bf16[32,6912]{1,0:T(8,128)(2,1)} %slice.353.right_ref), custom_call_target="tpu_custom_call" | custom-call | tf_op jit(solution)/shard_map/while/body/outer/pallas_call | solution.py:388
  603.7 7.2 %collective-permute-done.24 = bf16[72,1152]{1,0:T(8,128)(2,1)S(1)} collective-permute-done((bf16[72,1152]{1,0:T(8,128)(2,1)S(1)}, bf16[72,1152]{1,0:T(8,128)(2,1)S(1)}, u32[]{:S(2)}, u32[]{:S(2)}) %collective-permute-start.24) | collective-permute-done | bytes 165920 | tf_op jit(solution)/shard_map/while/body/ppermute | solution.py:305
  612.6 5.2 collective-permute-done.27
  620.4 6.9 %collective-permute-done.28 = bf16[144,1152]{1,0:T(8,128)(2,1)S(1)} collective-permute-done((bf16[144,1152]{1,0:T(8,128)(2,1)S(1)}, bf16[144,1152]{1,0:T(8,128)(2,1)S(1)}, u32[]{:S(2)}, u32[]{:S(2)}) %collective-permute-start.28) | collective-permute-done | bytes 331808 | tf_op jit(solution)/shard_map/while/body/ppermute | solution.py:305
  641.1 4.8 maximum_convert_fusion
  645.9 8.2 %convert_element_type.482 = f32[576,4608]{1,0:T(8,128)} convert(bf16[576,4608]{1,0:T(8,128)(2,1)} %all-reduce.5.cloned.1.call-done) | non-fusion elementwise | flops 2654208 | bytes 15925248 | tf_op jit(solution)/shard_map/convert_element_type | solution.py:667
  (479 shorter events, 241.8 us)
Async XLA Ops:
  7.2 65.2 %all-gather.6.cloned.1.call-start = ((), (), s32[]{:S(2)}) async-start(), calls=%async_computation.7 | async-start | bytes 4700160 | tf_op jit(solution)/shard_map/all_gather | solution.py:116
  13.4 15.9 %collective-permute-start.32 = (bf16[8,1152]{1,0:T(8,128)(2,1)S(1)}, bf16[8,1152]{1,0:T(8,128)(2,1)S(1)}, u32[]{:S(2)}, u32[]{:S(2)}) collective-permute-start(bf16[8,1152]{1,0:T(8,128)(2,1)S(1)} %copy-done.64), channel_id=1, source_target_pairs={{0,16},{16,0},{1,17},{17,1},{2,18},{18,2},{3,19},{19,3},{4,20},{20... | collective-permute-start | bytes 55304 | tf_op jit(solution)/shard_map/ppermute | solution.py:53
  19.2 176.6 %all-gather.8.cloned.1.call-start = ((), (), s32[]{:S(2)}) async-start(), calls=%async_computation.8 | async-start | bytes 1566720 | tf_op jit(solution)/shard_map/all_gather | solution.py:116
  45.8 168.3 %all-gather.10.cloned.1.call-start = ((), (), s32[]{:S(2)}) async-start(), calls=%async_computation.9 | async-start | bytes 6266880 | tf_op jit(solution)/shard_map/all_gather | solution.py:116
  85.3 52.8 %all-to-all-start.2 = ((bf16[16,1,3,72,256]{4,3,2,1,0:T(8,128)(2,1)}), bf16[16,1,3,72,256]{4,3,2,1,0:T(8,128)(2,1)}, u32[]{:S(2)}, u32[]{:S(2)}) async-start(bf16[16,1,3,72,256]{4,3,2,1,0:T(8,128)(2,1)} %bitcast.171), calls=%async_computation.2 | async-start | bytes 3538944 | tf_op jit(solution)/shard_map/all_to_all | solution.py:348
  94.6 41.0 %collective-permute-start.37 = (bf16[768,1152]{1,0:T(8,128)(2,1)S(1)}, bf16[768,1152]{1,0:T(8,128)(2,1)}, u32[]{:S(2)}, u32[]{:S(2)}) collective-permute-start(bf16[768,1152]{1,0:T(8,128)(2,1)S(1)} %get-tuple-element.311), channel_id=1, source_target_pairs={{0,16},{16,0},{1,17},{17,1},{2,18},{18,2},{3,19},{19,3},{4,20},{20... | collective-permute-start | bytes 5308424 | tf_op jit(solution)/shard_map/ppermute | solution.py:53
  135.7 55.1 %collective-permute-start.40 = (bf16[768,1152]{1,0:T(8,128)(2,1)}, bf16[768,1152]{1,0:T(8,128)(2,1)}, u32[]{:S(2)}, u32[]{:S(2)}) collective-permute-start(bf16[768,1152]{1,0:T(8,128)(2,1)} %get-tuple-element.314), channel_id=1, source_target_pairs={{0,16},{16,0},{1,17},{17,1},{2,18},{18,2},{3,19},{19,3},{4,20},{20... | collective-permute-start | bytes 5308424 | tf_op jit(solution)/shard_map/ppermute | solution.py:53
  152.7 38.0 %all-to-all-start.3 = ((bf16[16,1,72,256]{3,2,1,0:T(8,128)(2,1)}), bf16[16,1,72,256]{3,2,1,0:T(8,128)(2,1)}, u32[]{:S(2)}, u32[]{:S(2)}) async-start(bf16[16,1,72,256]{3,2,1,0:T(8,128)(2,1)} %get-tuple-element.313), calls=%async_computation.3 | async-start | bytes 1179648 | tf_op jit(solution)/shard_map/all_to_all | solution.py:348
  157.6 82.4 %all-gather.12.cloned.1.call-start = ((), (), s32[]{:S(2)}) async-start(), calls=%async_computation.10 | async-start | bytes 1880064 | tf_op jit(solution)/shard_map/all_gather | solution.py:116
  157.6 20.7 %collective-permute-start.38 = (bf16[576,32]{0,1:T(8,128)(2,1)S(1)}, bf16[576,32]{0,1:T(8,128)(2,1)}, u32[]{:S(2)}, u32[]{:S(2)}) collective-permute-start(bf16[576,32]{0,1:T(8,128)(2,1)S(1)} %copy-done.51), channel_id=1, source_target_pairs={{0,16},{16,0},{1,17},{17,1},{2,18},{18,2},{3,19},{19,3},{4,20},{20... | collective-permute-start | bytes 110600 | tf_op jit(solution)/shard_map/ppermute | solution.py:53
  160.8 25.3 %collective-permute-start.39 = (bf16[256,576]{0,1:T(8,128)(2,1)}, bf16[256,576]{0,1:T(8,128)(2,1)}, u32[]{:S(2)}, u32[]{:S(2)}) collective-permute-start(bf16[256,576]{0,1:T(8,128)(2,1)} %copy-done.23), channel_id=1, source_target_pairs={{0,16},{16,0},{1,17},{17,1},{2,18},{18,2},{3,19},{19,3},{4,20},{20... | collective-permute-start | bytes 884744 | tf_op jit(solution)/shard_map/ppermute | solution.py:53
  163.7 21.9 %collective-permute-start.44 = (bf16[48,1152]{1,0:T(8,128)(2,1)S(1)}, bf16[48,1152]{1,0:T(8,128)(2,1)}, u32[]{:S(2)}, u32[]{:S(2)}) collective-permute-start(bf16[48,1152]{1,0:T(8,128)(2,1)S(1)} %constant_dynamic-slice_fusion.12), channel_id=1, source_target_pairs={{0,16},{16,0},{1,17},{17,1},{2,18},{18,2},{3,19},{19,3},{4,20},{20... | collective-permute-start | bytes 331784 | tf_op jit(solution)/shard_map/ppermute | solution.py:53
  185.6 203.3 %reduce-scatter.2.cloned.1.call-start = ((), (), s32[]{:S(2)}) async-start(), calls=%async_computation.11 | async-start | bytes 5640192 | tf_op jit(solution)/shard_map/reduce_scatter | solution.py:577
  194.3 31.3 %collective-permute-start.42 = (bf16[576,256]{1,0:T(8,128)(2,1)}, bf16[576,256]{1,0:T(8,128)(2,1)}, u32[]{:S(2)}, u32[]{:S(2)}) collective-permute-start(bf16[576,256]{1,0:T(8,128)(2,1)} %get-tuple-element.502), channel_id=1, source_target_pairs={{0,16},{16,0},{1,17},{17,1},{2,18},{18,2},{3,19},{19,3},{4,20},{20... | collective-permute-start | bytes 884744 | tf_op jit(solution)/shard_map/ppermute | solution.py:53
  213.7 14.0 %collective-permute-start.43 = (bf16[256,576]{0,1:T(8,128)(2,1)}, bf16[256,576]{0,1:T(8,128)(2,1)}, u32[]{:S(2)}, u32[]{:S(2)}) collective-permute-start(bf16[256,576]{0,1:T(8,128)(2,1)} %get-tuple-element.498), channel_id=1, source_target_pairs={{0,16},{16,0},{1,17},{17,1},{2,18},{18,2},{3,19},{19,3},{4,20},{20... | collective-permute-start | bytes 884744 | tf_op jit(solution)/shard_map/ppermute | solution.py:53
  230.7 41.8 %collective-permute-start.45 = (bf16[256,2304]{1,0:T(8,128)(2,1)}, bf16[256,2304]{1,0:T(8,128)(2,1)}, u32[]{:S(2)}, u32[]{:S(2)}) collective-permute-start(bf16[256,2304]{1,0:T(8,128)(2,1)} %get-tuple-element.487), channel_id=1, source_target_pairs={{0,16},{16,0},{1,17},{17,1},{2,18},{18,2},{3,19},{19,3},{4,20},{20... | collective-permute-start | bytes 3538952 | tf_op jit(solution)/shard_map/ppermute | solution.py:53
  249.3 23.2 %collective-permute-start.46 = (bf16[256,1152]{1,0:T(8,128)(2,1)S(1)}, bf16[256,1152]{1,0:T(8,128)(2,1)}, u32[]{:S(2)}, u32[]{:S(2)}) collective-permute-start(bf16[256,1152]{1,0:T(8,128)(2,1)S(1)} %bitcast.174), channel_id=1, source_target_pairs={{0,16},{16,0},{1,17},{17,1},{2,18},{18,2},{3,19},{19,3},{4,20},{20... | collective-permute-start | bytes 1769480 | tf_op jit(solution)/shard_map/ppermute | solution.py:53
  260.9 70.4 %collective-permute-start.47 = (bf16[256,4608]{1,0:T(8,128)(2,1)}, bf16[256,4608]{1,0:T(8,128)(2,1)}, u32[]{:S(2)}, u32[]{:S(2)}) collective-permute-start(bf16[256,4608]{1,0:T(8,128)(2,1)} %fusion.12), channel_id=1, source_target_pairs={{0,16},{16,0},{1,17},{17,1},{2,18},{18,2},{3,19},{19,3},{4,20},{20... | collective-permute-start | bytes 7077896 | tf_op jit(solution)/shard_map/ppermute | solution.py:53
  331.3 57.6 %all-to-all-start.5 = ((bf16[16,1,3,72,256]{4,3,2,1,0:T(8,128)(2,1)}), bf16[16,1,3,72,256]{4,3,2,1,0:T(8,128)(2,1)}, u32[]{:S(2)}, u32[]{:S(2)}) async-start(bf16[16,1,3,72,256]{4,3,2,1,0:T(8,128)(2,1)} %attend_back.1), calls=%async_computation.5 | async-start | bytes 3538944 | tf_op jit(solution)/shard_map/all_to_all | solution.py:348
  335.9 107.2 %all-gather.14.cloned.1.call-start = ((), (), s32[]{:S(2)}) async-start(), calls=%async_computation.12 | async-start | bytes 5640192 | tf_op jit(solution)/shard_map/all_gather | solution.py:597
  336.2 15.9 %collective-permute-start.48 = (bf16[256,1152]{1,0:T(8,128)(2,1)}, bf16[256,1152]{1,0:T(8,128)(2,1)}, u32[]{:S(2)}, u32[]{:S(2)}) collective-permute-start(bf16[256,1152]{1,0:T(8,128)(2,1)} %bitcast.196), channel_id=1, source_target_pairs={{0,16},{16,0},{1,17},{17,1},{2,18},{18,2},{3,19},{19,3},{4,20},{20... | collective-permute-start | bytes 1769480 | tf_op jit(solution)/shard_map/ppermute | solution.py:53
  388.9 256.9 %all-reduce.5.cloned.1.call-start = ((), (), s32[]{:S(2)}) async-start(), calls=%async_computation.13 | async-start | bytes 10616832 | tf_op jit(solution)/shard_map/psum | solution.py:601
  393.9 40.5 %collective-permute-start.51 = (bf16[3456,256]{1,0:T(8,128)(2,1)}, bf16[3456,256]{1,0:T(8,128)(2,1)}, u32[]{:S(2)}, u32[]{:S(2)}) collective-permute-start(bf16[3456,256]{1,0:T(8,128)(2,1)} %bitcast.30), channel_id=1, source_target_pairs={{0,16},{16,0},{1,17},{17,1},{2,18},{18,2},{3,19},{19,3},{4,20},{20... | collective-permute-start | bytes 5308424 | tf_op jit(solution)/shard_map/ppermute | solution.py:53
  450.9 29.1 %all-to-all-start = ((bf16[16,11,1152]{2,1,0:T(8,128)(2,1)}), bf16[16,11,1152]{2,1,0:T(8,128)(2,1)S(1)}, u32[]{:S(2)}, u32[]{:S(2)}) async-start(bf16[16,11,1152]{2,1,0:T(8,128)(2,1)} %copy.153), calls=%async_computation | async-start | bytes 1179648 | tf_op jit(solution)/shard_map/while/body/all_to_all | solution.py:348
  454.6 13.6 %collective-permute-start.1 = (bf16[288,1152]{1,0:T(8,128)(2,1)S(1)}, bf16[288,1152]{1,0:T(8,128)(2,1)}, u32[]{:S(2)}, u32[]{:S(2)}) collective-permute-start(bf16[288,1152]{1,0:T(8,128)(2,1)S(1)} %constant_dynamic-slice_fusion.28), channel_id=1, source_target_pairs={{0,4},{4,0},{8,12},{12,8},{1,5},{5,1},{9,13},{13,9},{2,6},{6,2},{1... | collective-permute-start | bytes 1990664 | tf_op jit(solution)/shard_map/while/body/ppermute | solution.py:305
  456.9 15.1 %collective-permute-start.8 = (bf16[288,1152]{1,0:T(8,128)(2,1)}, bf16[288,1152]{1,0:T(8,128)(2,1)}, u32[]{:S(2)}, u32[]{:S(2)}) collective-permute-start(bf16[288,1152]{1,0:T(8,128)(2,1)} %constant_dynamic-slice_fusion.31), channel_id=1, source_target_pairs={{0,4},{4,0},{8,12},{12,8},{1,5},{5,1},{9,13},{13,9},{2,6},{6,2},{1... | collective-permute-start | bytes 1990664 | tf_op jit(solution)/shard_map/while/body/ppermute | solution.py:305
  459.1 15.3 %collective-permute-start.15 = (bf16[288,1152]{1,0:T(8,128)(2,1)}, bf16[288,1152]{1,0:T(8,128)(2,1)}, u32[]{:S(2)}, u32[]{:S(2)}) collective-permute-start(bf16[288,1152]{1,0:T(8,128)(2,1)} %constant_dynamic-slice_fusion.34), channel_id=1, source_target_pairs={{0,4},{4,0},{8,12},{12,8},{1,5},{5,1},{9,13},{13,9},{2,6},{6,2},{1... | collective-permute-start | bytes 1990664 | tf_op jit(solution)/shard_map/while/body/ppermute | solution.py:305
  460.6 18.0 %collective-permute-start.19 = (bf16[288,1152]{1,0:T(8,128)(2,1)S(1)}, bf16[288,1152]{1,0:T(8,128)(2,1)}, u32[]{:S(2)}, u32[]{:S(2)}) collective-permute-start(bf16[288,1152]{1,0:T(8,128)(2,1)S(1)} %constant_dynamic-slice_fusion.37), channel_id=1, source_target_pairs={{0,4},{4,0},{8,12},{12,8},{1,5},{5,1},{9,13},{13,9},{2,6},{6,2},{1... | collective-permute-start | bytes 1990664 | tf_op jit(solution)/shard_map/while/body/ppermute | solution.py:305
  470.2 20.1 %collective-permute-start.2 = (bf16[144,1152]{1,0:T(8,128)(2,1)}, bf16[144,1152]{1,0:T(8,128)(2,1)}, u32[]{:S(2)}, u32[]{:S(2)}) collective-permute-start(bf16[144,1152]{1,0:T(8,128)(2,1)} %constant_dynamic-slice_fusion.29), channel_id=1, source_target_pairs={{0,8},{4,12},{8,0},{12,4},{1,9},{5,13},{9,1},{13,5},{2,10},{6,14},... | collective-permute-start | bytes 995336 | tf_op jit(solution)/shard_map/while/body/ppermute | solution.py:305
  474.3 19.1 %collective-permute-start.9 = (bf16[144,1152]{1,0:T(8,128)(2,1)}, bf16[144,1152]{1,0:T(8,128)(2,1)}, u32[]{:S(2)}, u32[]{:S(2)}) collective-permute-start(bf16[144,1152]{1,0:T(8,128)(2,1)} %constant_dynamic-slice_fusion.32), channel_id=1, source_target_pairs={{0,8},{4,12},{8,0},{12,4},{1,9},{5,13},{9,1},{13,5},{2,10},{6,14},... | collective-permute-start | bytes 995336 | tf_op jit(solution)/shard_map/while/body/ppermute | solution.py:305
  476.7 28.2 %collective-permute-start.16 = (bf16[144,1152]{1,0:T(8,128)(2,1)}, bf16[144,1152]{1,0:T(8,128)(2,1)}, u32[]{:S(2)}, u32[]{:S(2)}) collective-permute-start(bf16[144,1152]{1,0:T(8,128)(2,1)} %constant_dynamic-slice_fusion.35), channel_id=1, source_target_pairs={{0,8},{4,12},{8,0},{12,4},{1,9},{5,13},{9,1},{13,5},{2,10},{6,14},... | collective-permute-start | bytes 995336 | tf_op jit(solution)/shard_map/while/body/ppermute | solution.py:305
  482.8 30.8 %collective-permute-start.20 = (bf16[144,1152]{1,0:T(8,128)(2,1)}, bf16[144,1152]{1,0:T(8,128)(2,1)}, u32[]{:S(2)}, u32[]{:S(2)}) collective-permute-start(bf16[144,1152]{1,0:T(8,128)(2,1)} %constant_dynamic-slice_fusion.38), channel_id=1, source_target_pairs={{0,8},{4,12},{8,0},{12,4},{1,9},{5,13},{9,1},{13,5},{2,10},{6,14},... | collective-permute-start | bytes 995336 | tf_op jit(solution)/shard_map/while/body/ppermute | solution.py:305
  485.5 87.4 %all-to-all-start.1 = ((bf16[16,2,11,1152]{3,1,2,0:T(2,128)(2,1)}), bf16[16,2,11,1152]{3,1,2,0:T(2,128)(2,1)S(1)}, u32[]{:S(2)}, u32[]{:S(2)}) async-start(bf16[16,2,11,1152]{3,1,2,0:T(2,128)(2,1)} %broadcast_in_dim.51), calls=%async_computation.1 | async-start | bytes 1622016 | tf_op jit(solution)/shard_map/while/body/all_to_all | solution.py:348
  491.4 25.8 %collective-permute-start.3 = (bf16[72,1152]{1,0:T(8,128)(2,1)S(1)}, bf16[72,1152]{1,0:T(8,128)(2,1)S(1)}, u32[]{:S(2)}, u32[]{:S(2)}) collective-permute-start(bf16[72,1152]{1,0:T(8,128)(2,1)S(1)} %constant_dynamic-slice_fusion.30), channel_id=1, source_target_pairs={{0,1},{1,0},{2,3},{3,2},{4,5},{5,4},{6,7},{7,6},{8,9},{9,8},{10,11... | collective-permute-start | bytes 497672 | tf_op jit(solution)/shard_map/while/body/ppermute | solution.py:305
  494.5 31.3 %collective-permute-start.10 = (bf16[72,1152]{1,0:T(8,128)(2,1)S(1)}, bf16[72,1152]{1,0:T(8,128)(2,1)S(1)}, u32[]{:S(2)}, u32[]{:S(2)}) collective-permute-start(bf16[72,1152]{1,0:T(8,128)(2,1)S(1)} %constant_dynamic-slice_fusion.33), channel_id=1, source_target_pairs={{0,1},{1,0},{2,3},{3,2},{4,5},{5,4},{6,7},{7,6},{8,9},{9,8},{10,11... | collective-permute-start | bytes 497672 | tf_op jit(solution)/shard_map/while/body/ppermute | solution.py:305
  506.0 25.9 %collective-permute-start.17 = (bf16[72,1152]{1,0:T(8,128)(2,1)S(1)}, bf16[72,1152]{1,0:T(8,128)(2,1)S(1)}, u32[]{:S(2)}, u32[]{:S(2)}) collective-permute-start(bf16[72,1152]{1,0:T(8,128)(2,1)S(1)} %constant_dynamic-slice_fusion.36), channel_id=1, source_target_pairs={{0,1},{1,0},{2,3},{3,2},{4,5},{5,4},{6,7},{7,6},{8,9},{9,8},{10,11... | collective-permute-start | bytes 497672 | tf_op jit(solution)/shard_map/while/body/ppermute | solution.py:305
  514.7 23.6 %collective-permute-start.21 = (bf16[72,1152]{1,0:T(8,128)(2,1)S(1)}, bf16[72,1152]{1,0:T(8,128)(2,1)S(1)}, u32[]{:S(2)}, u32[]{:S(2)}) collective-permute-start(bf16[72,1152]{1,0:T(8,128)(2,1)S(1)} %constant_dynamic-slice_fusion.39), channel_id=1, source_target_pairs={{0,1},{1,0},{2,3},{3,2},{4,5},{5,4},{6,7},{7,6},{8,9},{9,8},{10,11... | collective-permute-start | bytes 497672 | tf_op jit(solution)/shard_map/while/body/ppermute | solution.py:305
  517.2 21.8 %collective-permute-start.4 = (bf16[72,1152]{1,0:T(8,128)(2,1)S(1)}, bf16[72,1152]{1,0:T(8,128)(2,1)S(1)}, u32[]{:S(2)}, u32[]{:S(2)}) collective-permute-start(bf16[72,1152]{1,0:T(8,128)(2,1)S(1)} %add_convert_fusion.38), channel_id=1, source_target_pairs={{0,2},{1,3},{2,0},{3,1},{4,6},{5,7},{6,4},{7,5},{8,10},{9,11},{10,... | collective-permute-start | bytes 497672 | tf_op jit(solution)/shard_map/while/body/ppermute | solution.py:305
  525.9 27.1 %collective-permute-start.11 = (bf16[72,1152]{1,0:T(8,128)(2,1)S(1)}, bf16[72,1152]{1,0:T(8,128)(2,1)S(1)}, u32[]{:S(2)}, u32[]{:S(2)}) collective-permute-start(bf16[72,1152]{1,0:T(8,128)(2,1)S(1)} %add_convert_fusion.42), channel_id=1, source_target_pairs={{0,2},{1,3},{2,0},{3,1},{4,6},{5,7},{6,4},{7,5},{8,10},{9,11},{10,... | collective-permute-start | bytes 497672 | tf_op jit(solution)/shard_map/while/body/ppermute | solution.py:305
  531.9 25.2 %collective-permute-start.18 = (bf16[72,1152]{1,0:T(8,128)(2,1)S(1)}, bf16[72,1152]{1,0:T(8,128)(2,1)S(1)}, u32[]{:S(2)}, u32[]{:S(2)}) collective-permute-start(bf16[72,1152]{1,0:T(8,128)(2,1)S(1)} %add_convert_fusion.46), channel_id=1, source_target_pairs={{0,2},{1,3},{2,0},{3,1},{4,6},{5,7},{6,4},{7,5},{8,10},{9,11},{10,... | collective-permute-start | bytes 497672 | tf_op jit(solution)/shard_map/while/body/ppermute | solution.py:305
  538.4 22.2 %collective-permute-start.22 = (bf16[72,1152]{1,0:T(8,128)(2,1)S(1)}, bf16[72,1152]{1,0:T(8,128)(2,1)S(1)}, u32[]{:S(2)}, u32[]{:S(2)}) collective-permute-start(bf16[72,1152]{1,0:T(8,128)(2,1)S(1)} %add_convert_fusion.50), channel_id=1, source_target_pairs={{0,2},{1,3},{2,0},{3,1},{4,6},{5,7},{6,4},{7,5},{8,10},{9,11},{10,... | collective-permute-start | bytes 497672 | tf_op jit(solution)/shard_map/while/body/ppermute | solution.py:305
  539.1 18.1 %collective-permute-start.5 = (bf16[72,1152]{1,0:T(8,128)(2,1)S(1)}, bf16[72,1152]{1,0:T(8,128)(2,1)S(1)}, u32[]{:S(2)}, u32[]{:S(2)}) collective-permute-start(bf16[72,1152]{1,0:T(8,128)(2,1)S(1)} %add_convert_fusion.39), channel_id=1, source_target_pairs={{0,1},{1,0},{2,3},{3,2},{4,5},{5,4},{6,7},{7,6},{8,9},{9,8},{10,11... | collective-permute-start | bytes 497672 | tf_op jit(solution)/shard_map/while/body/ppermute | solution.py:305
  557.2 15.4 %collective-permute-start.6 = (bf16[144,1152]{1,0:T(8,128)(2,1)S(1)}, bf16[144,1152]{1,0:T(8,128)(2,1)S(1)}, u32[]{:S(2)}, u32[]{:S(2)}) collective-permute-start(bf16[144,1152]{1,0:T(8,128)(2,1)S(1)} %maximum_select_fusion.24), channel_id=1, source_target_pairs={{0,8},{4,12},{8,0},{12,4},{1,9},{5,13},{9,1},{13,5},{2,10},{6,14},... | collective-permute-start | bytes 995336 | tf_op jit(solution)/shard_map/while/body/ppermute | solution.py:305
  566.0 34.3 %collective-permute-start.13 = (bf16[144,1152]{1,0:T(8,128)(2,1)S(1)}, bf16[144,1152]{1,0:T(8,128)(2,1)}, u32[]{:S(2)}, u32[]{:S(2)}) collective-permute-start(bf16[144,1152]{1,0:T(8,128)(2,1)S(1)} %maximum_select_fusion.27), channel_id=1, source_target_pairs={{0,8},{4,12},{8,0},{12,4},{1,9},{5,13},{9,1},{13,5},{2,10},{6,14},... | collective-permute-start | bytes 995336 | tf_op jit(solution)/shard_map/while/body/ppermute | solution.py:305
  572.8 54.6 %collective-permute-start.7 = (bf16[288,1152]{1,0:T(8,128)(2,1)S(1)}, bf16[288,1152]{1,0:T(8,128)(2,1)}, u32[]{:S(2)}, u32[]{:S(2)}) collective-permute-start(bf16[288,1152]{1,0:T(8,128)(2,1)S(1)} %maximum_select_fusion.25), channel_id=1, source_target_pairs={{0,4},{4,0},{8,12},{12,8},{1,5},{5,1},{9,13},{13,9},{2,6},{6,2},{1... | collective-permute-start | bytes 1990664 | tf_op jit(solution)/shard_map/while/body/ppermute | solution.py:305
  583.6 15.9 %collective-permute-start.23 = (f32[16,576]{1,0:T(8,128)}, f32[16,576]{1,0:T(8,128)S(1)}, u32[]{:S(2)}, u32[]{:S(2)}) collective-permute-start(f32[16,576]{1,0:T(8,128)} %slice.352), channel_id=1, source_target_pairs={{0,16},{16,0},{1,17},{17,1},{2,18},{18,2},{3,19},{19,3},{4,20},{20... | collective-permute-start | bytes 110600 | tf_op jit(solution)/shard_map/while/body/ppermute | solution.py:58
  601.6 28.7 %collective-permute-start.14 = (bf16[288,1152]{1,0:T(8,128)(2,1)S(1)}, bf16[288,1152]{1,0:T(8,128)(2,1)S(1)}, u32[]{:S(2)}, u32[]{:S(2)}) collective-permute-start(bf16[288,1152]{1,0:T(8,128)(2,1)S(1)} %maximum_select_fusion.28), channel_id=1, source_target_pairs={{0,4},{4,0},{8,12},{12,8},{1,5},{5,1},{9,13},{13,9},{2,6},{6,2},{1... | collective-permute-start | bytes 1990664 | tf_op jit(solution)/shard_map/while/body/ppermute | solution.py:305
  601.8 16.0 %collective-permute-start.27 = (bf16[72,1152]{1,0:T(8,128)(2,1)S(1)}, bf16[72,1152]{1,0:T(8,128)(2,1)S(1)}, u32[]{:S(2)}, u32[]{:S(2)}) collective-permute-start(bf16[72,1152]{1,0:T(8,128)(2,1)S(1)} %copy-done.9), channel_id=1, source_target_pairs={{0,1},{1,0},{2,3},{3,2},{4,5},{5,4},{6,7},{7,6},{8,9},{9,8},{10,11... | collective-permute-start | bytes 497672 | tf_op jit(solution)/shard_map/while/body/ppermute | solution.py:305
  (92 other events, 527.2 us)
Sparse Core Ops, SparseCore 0:
  19.3 53.0 all-gather.5
  74.6 51.6 all-gather.7
  128.6 69.1 all-gather.9
  199.9 38.3 all-gather.11
  280.1 100.9 reduce-scatter.1
  389.1 54.0 all-gather.13
  449.9 177.1 all-reduce.4

commit v3 on v2

--- a/solution.py
+++ b/solution.py
@@ -193,7 +193,7 @@
 
 
 def attend_back_kernel(
-    order, half, factor, kind_ref, x_ref, d_ref, lse_ref, g_ref, qkv_s, d_s, g_s
+    order, half, factor, kind_ref, x_ref, d_ref, o_ref, lse_ref, g_ref, qkv_s, d_s, e_s, g_s
 ):
     step = pl.program_id(1)
     count = len(order) * half
@@ -202,7 +202,10 @@
     for par in range(2):
         for c in range(3):
             qkv_s[c] = pick_tokens([x_ref[s, 0, c] for s in order], par, half)
-        d_s[...] = pick_tokens([d_ref[s, 0] for s in order], par, half)
+        dout_all = pick_tokens([d_ref[s, 0] for s in order], par, half)
+        out_all = pick_tokens([o_ref[s, 0] for s in order], par, half)
+        d_s[...] = dout_all
+        e_s[...] = jnp.sum(dout_all.astype(F32) * out_all.astype(F32), axis=0, keepdims=True)
         single = kind_ref[2 * step + par] == 0
         for b in range(4):
             cols = slice(b * block, (b + 1) * block)
@@ -213,8 +216,7 @@
                 score = dotd(qkv_s[1, :, keys], query, 0, 0)
                 prob = jnp.exp2(score * coef - lse_ref[0, par, :, cols])
                 dprob = dotd(qkv_s[2, :, keys], dout, 0, 0)
-                delta = jnp.sum(prob * dprob, axis=0, keepdims=True)
-                dscore = (prob * (dprob - delta)).astype(BF)
+                dscore = (prob * (dprob - e_s[:, cols])).astype(BF)
                 g_s[par, 0, :, cols] = dotd(qkv_s[1, :, keys], dscore, 1, 0) * factor
                 dkey = dotd(query, dscore, 1, 1) * factor
                 dvalue = dotd(dout, prob.astype(BF), 1, 1)
@@ -270,7 +272,7 @@
     )(kinds, x)
 
 
-def attend_back(kinds, x, d, lse, order, half, factor):
+def attend_back(kinds, x, d, o, lse, order, half, factor):
     tiles, per, _, depth, tokens = x.shape
     count = tiles * half
     pairs = tokens // (2 * half)
@@ -282,6 +284,7 @@
             in_specs=[
                 pl.BlockSpec((tiles, 1, 3, depth, 2 * half), lambda h, p, kd: (0, h, 0, 0, p)),
                 pl.BlockSpec((tiles, 1, depth, 2 * half), lambda h, p, kd: (0, h, 0, p)),
+                pl.BlockSpec((tiles, 1, depth, 2 * half), lambda h, p, kd: (0, h, 0, p)),
                 pl.BlockSpec((1, 2, 1, count), lambda h, p, kd: (h, p, 0, 0)),
             ],
             out_specs=pl.BlockSpec(
@@ -290,6 +293,7 @@
             scratch_shapes=[
                 pltpu.VMEM((3, depth, count), BF),
                 pltpu.VMEM((depth, count), BF),
+                pltpu.VMEM((1, count), F32),
                 pltpu.VMEM((2, 3, depth, count), F32),
             ],
         ),
@@ -298,7 +302,7 @@
         cost_estimate=pl.CostEstimate(
             flops=10**10, bytes_accessed=4 * 10**7, transcendentals=per * tokens * count
         ),
-    )(kinds, x, d, lse)
+    )(kinds, x, d, o, lse)
 
 
 def swapped(value, axis, bit):
@@ -526,6 +530,7 @@
     qkv = exchange(qkv)
     qkv, o_low = lax.optimization_barrier((qkv, o_low))
     att, lse = attend(canvas_kind, qkv, order, tile_tok, factor)
+    att_head = att
     att = exchange(att).reshape(width, rows)
     att, a1_all, o_mid = lax.optimization_barrier((att, a1_all, o_mid))
     att_parts = split_own(att, 0)
@@ -586,7 +591,7 @@
     datt = join_own(datt, 0).astype(BF)
     datt = exchange(datt.reshape(tiles, per, head_dim, rows))
     dproj_all = jnp.concatenate(swap_full(dproj), 0)
-    dqkv = attend_back(canvas_kind, qkv, datt, lse, order, tile_tok, factor)
+    dqkv = attend_back(canvas_kind, qkv, datt, att_head, lse, order, tile_tok, factor)
     dqkv, dpre_all = lax.optimization_barrier((dqkv, dpre_all))
     dqkv = exchange(dqkv)
     g_up = dotd(a2_all, jnp.concatenate(dpre_all, 0), 0, 0).astype(BF)

time: 671 us -> 669 us (level)
  starting transfers between devices: 72 us -> 82.8 us
  Pallas kernels: 46.7 us -> 38.1 us
    ppermute x18, starting transfers between devices: 19.1 us -> 27.3 us  [send_down(): lax.ppermute(value, 'img', [(j, (j - k) % size) for j in range(size)])]
  transfers between devices with their start and end apart: 64 -> 64, of which waited for: 34 -> 34; matrix products, arithmetic and copies ran while one was open for 35% -> 36% of each run, Pallas kernels for 7% -> 6%
where the time goes in v3:
time: 669 us; the launch traced here: 659 us
  waiting for transfers between devices  240 us (36%)
  matrix products  102 us (15%)
  other arithmetic  84.1 us (13%)
  starting transfers between devices  82.8 us (12%)
  local copies, waits for them, and re-layouts  73.1 us (11%)
  Pallas kernels  38.1 us (6%)
  blocking collectives  23.2 us (3%)
  between operations  15.6 us (2%)
    ppermute x18, waiting for transfers between devices, send_down(): lax.ppermute(value, 'img', [(j, (j - k) % size) for j in range(size)])  108 us
    dot_general x34, matrix products, dotd(): lax.dot_general(left, right, (((ldim,), (rdim,)), ((), ())), preferred_el...  102 us
    ppermute x28, waiting for transfers between devices, swapped(): lax.ppermute(value, axis, [(j, j ^ bit) for j in range(lax.axis_size(axis...  81 us
    all_to_all x5, waiting for transfers between devices, exchange(): return lax.all_to_all(x, RC, split_axis=0, concat_axis=0, tiled=True)  28.1 us
    ppermute x18, starting transfers between devices, send_down(): lax.ppermute(value, 'img', [(j, (j - k) % size) for j in range(size)])  27.3 us
    ppermute x28, starting transfers between devices, swapped(): lax.ppermute(value, axis, [(j, j ^ bit) for j in range(lax.axis_size(axis...  25.9 us
    all_to_all x1, blocking collectives, exchange(): return lax.all_to_all(x, RC, split_axis=0, concat_axis=0, tiled=True)  23.2 us
    all_to_all x5, starting transfers between devices, exchange(): return lax.all_to_all(x, RC, split_axis=0, concat_axis=0, tiled=True)  23 us
  transfers between devices with their start and end apart: 64, of which 34 were waited for; matrix products, arithmetic and copies ran while one was open for 36% of the time, Pallas kernels for 6%

profile of v3, /device:TPU:0, one launch (start us, length us, event | category | flops | bytes accessed | tf_op | source)
XLA Modules:
  0.0 658.7 jit_solution(17671109277135793991)
XLA Ops:
  13.5 5.0 collective-permute-done.35
  35.2 4.6 collective-permute-done.34
  41.5 4.2 collective-permute-done.41
  47.9 7.0 %collective-permute-done.36 = bf16[40,4608]{1,0:T(8,128)(2,1)} collective-permute-done((bf16[40,4608]{1,0:T(8,128)(2,1)S(1)}, bf16[40,4608]{1,0:T(8,128)(2,1)}, u32[]{:S(2)}, u32[]{:S(2)}) %collective-permute-start.36) | collective-permute-done | bytes 368672 | tf_op jit(solution)/shard_map/ppermute | solution.py:53
  60.7 5.6 convolution_bitcast_fusion
  66.3 6.1 all-gather.6.cloned.1.call-done
  72.4 6.2 fusion.5
  85.3 4.6 all-to-all-start.2
  89.9 4.7 fusion.77
  96.1 39.6 %collective-permute-done.37 = bf16[768,1152]{1,0:T(8,128)(2,1)} collective-permute-done((bf16[768,1152]{1,0:T(8,128)(2,1)S(1)}, bf16[768,1152]{1,0:T(8,128)(2,1)}, u32[]{:S(2)}, u32[]{:S(2)}) %collective-permute-start.37) | collective-permute-done | bytes 1769504 | tf_op jit(solution)/shard_map/ppermute | solution.py:53
  138.1 12.0 %attend.1 = (bf16[16,1,72,256]{3,2,1,0:T(8,128)(2,1)}, f32[1,4,1,1024]{3,2,1,0:T(1,128)}) custom-call(s32[4]{0:T(128)} %refs_0_.3, bf16[16,1,3,72,256]{4,3,2,1,0:T(8,128)(2,1)} %all-to-all-done.2.refs_1_), custom_call_target="tpu_custom_call" | custom-call | flops 10000000000 | bytes 40000000 | tf_op jit(solution)/shard_map/attend/pallas_call | solution.py:247
  150.1 4.9 all-to-all-start.3
  164.7 13.6 %collective-permute-done.38 = bf16[576,32]{0,1:T(8,128)(2,1)} collective-permute-done((bf16[576,32]{0,1:T(8,128)(2,1)S(1)}, bf16[576,32]{0,1:T(8,128)(2,1)}, u32[]{:S(2)}, u32[]{:S(2)}) %collective-permute-start.38) | collective-permute-done | bytes 36896 | tf_op jit(solution)/shard_map/ppermute | solution.py:53
  179.2 6.5 collective-permute-done.44
  206.8 6.8 %fusion.83 = f32[256,4608]{1,0:T(8,128)} fusion(bf16[256,576]{0,1:T(8,128)(2,1)S(1)} %get-tuple-element.499, bf16[576,4608]{1,0:T(8,128)(2,1)} %param.21), kind=kOutput, calls=%fused_computation.291 | convolution fusion | flops 1358954496 | bytes 10321920 | tf_op jit(solution)/shard_map/dot_general | solution.py:46
  214.1 9.7 %multiply_convert_fusion = (bf16[256,4608]{1,0:T(8,128)(2,1)S(1)}, f32[256,4608]{1,0:T(8,128)}) fusion(f32[256,4608]{1,0:T(8,128)} %fusion.83, bf16[640,4608]{1,0:T(8,128)(2,1)} %all-gather.10.cloned.1.call-done, bf16[256,576]{0,1:T(8,128)(2,1)} %get-tuple-element.498), kind=kOutput, calls=%fused_computation.72 | convolution fusion | flops 1521745920 | bytes 17989632 | tf_op jit(solution)/shard_map/dot_general | solution.py:46
  232.1 4.3 fusion.84
  253.8 4.2 fusion.12
  272.4 7.4 %convolution_convert_fusion = bf16[2304,1152]{1,0:T(8,128)(2,1)} fusion(bf16[256,2304]{1,0:T(8,128)(2,1)} %collective-permute-done.45, bf16[256,2304]{1,0:T(8,128)(2,1)} %copy-done.22, bf16[256,1152]{1,0:T(8,128)(2,1)} %collective-permute-done.46, bf16[256,1152]{1,0:T(8,128)(2,1)S(1)} %bitcast.177), kind=kOutput, calls=%fused_computation.51 | convolution fusion | flops 2727641088 | bytes 8847360 | tf_op jit(solution)/shard_map/dot_general | solution.py:46
  287.6 23.2 %all_to_all.40.refs_2_ = bf16[16,1,72,256]{3,2,1,0:T(8,128)(2,1)} all-to-all(bf16[16,1,72,256]{3,2,1,0:T(8,128)(2,1)S(1)} %bitcast.190), channel_id=1, replica_groups=mesh['img'=2,'row'=4,'col'=4] {'row','col'}, dimensions={0} | all-to-all | bytes 1179648 | tf_op jit(solution)/shard_map/all_to_all | solution.py:352
  310.8 14.3 %attend_back.1 = bf16[16,1,3,72,256]{4,3,2,1,0:T(8,128)(2,1)} custom-call(s32[4]{0:T(128)} %refs_0_.3, bf16[16,1,3,72,256]{4,3,2,1,0:T(8,128)(2,1)} %all-to-all-done.2.refs_1_, bf16[16,1,72,256]{3,2,1,0:T(8,128)(2,1)} %all_to_all.40.refs_2_, bf16[16,1,72,256]{3,2,1,0:T(8,128)(2,1)} %get-tuple-element.313.refs_3_, f32[1,4,1,1024]{3,2,1,0:T(1,128)} %get-tuple-element.327.refs_4_), custom_call_target="tpu_custom_call" | custom-call | flops 10000000000 | bytes 40000000 | tf_op jit(solution)/shard_map/attend_back/pallas_call | solution.py:279
  325.1 4.6 all-to-all-start.5
  330.2 4.3 collective-permute-start.48
  335.8 12.7 %collective-permute-done.48 = bf16[256,1152]{1,0:T(8,128)(2,1)} collective-permute-done((bf16[256,1152]{1,0:T(8,128)(2,1)}, bf16[256,1152]{1,0:T(8,128)(2,1)}, u32[]{:S(2)}, u32[]{:S(2)}) %collective-permute-start.48) | collective-permute-done | bytes 589856 | tf_op jit(solution)/shard_map/ppermute | solution.py:53
  351.6 7.7 %convolution_convert_fusion.1 = bf16[576,4608]{1,0:T(8,128)(2,1)} fusion(bf16[512,576]{0,1:T(8,128)(2,1)S(1)} %copy-done.30, bf16[256,4608]{1,0:T(8,128)(2,1)} %collective-permute-done.47, bf16[256,4608]{1,0:T(8,128)(2,1)} %fusion.12), kind=kOutput, calls=%fused_computation.52 | convolution fusion | flops 2730000384 | bytes 10616832 | tf_op jit(solution)/shard_map/dot_general | solution.py:46
  359.3 27.1 %all-to-all-done.5 = bf16[16,1,3,72,256]{4,3,2,1,0:T(8,128)(2,1)} async-done(((bf16[16,1,3,72,256]{4,3,2,1,0:T(8,128)(2,1)}), bf16[16,1,3,72,256]{4,3,2,1,0:T(8,128)(2,1)}, u32[]{:S(2)}, u32[]{:S(2)}) %all-to-all-start.5) | async-done | bytes 1769504 | tf_op jit(solution)/shard_map/all_to_all | solution.py:352
  392.6 4.2 fusion.89
  417.5 14.8 %collective-permute-done.51 = bf16[3456,256]{1,0:T(8,128)(2,1)} collective-permute-done((bf16[3456,256]{1,0:T(8,128)(2,1)}, bf16[3456,256]{1,0:T(8,128)(2,1)}, u32[]{:S(2)}, u32[]{:S(2)}) %collective-permute-start.51) | collective-permute-done | bytes 1769504 | tf_op jit(solution)/shard_map/ppermute | solution.py:53
  436.3 4.3 all-gather.14.cloned.1.call-done
  447.3 185.4 %while.31 = (s32[]{:T(128)}, bf16[16,11,1152]{2,0,1:T(8,128)(2,1)S(1)}, bf16[576,1152]{1,0:T(8,128)(2,1)S(1)}, bf16[576,1152]{1,0:T(8,128)(2,1)}, bf16[576,1152]...) while((s32[]{:T(128)}, ...), condition=%wide.region_25.26_spmd, body=%wide.region_22.25_spmd.sunk | while | flops 395250112 | bytes 143718128 | solution.py:382
  448.3 4.3 all-to-all-start
  459.0 7.4 %convert_element_type.653 = f32[2304,1152]{1,0:T(8,128)} convert(bf16[2304,1152]{1,0:T(8,128)(2,1)} %get-tuple-element.718) | non-fusion elementwise | flops 2654208 | bytes 15925248 | tf_op jit(solution)/shard_map/while/body/convert_element_type | solution.py:647
  483.7 4.7 all-to-all-start.1
  494.7 8.4 %collective-permute-done.16 = bf16[144,1152]{1,0:T(8,128)(2,1)} collective-permute-done((bf16[144,1152]{1,0:T(8,128)(2,1)}, bf16[144,1152]{1,0:T(8,128)(2,1)}, u32[]{:S(2)}, u32[]{:S(2)}) %collective-permute-start.16) | collective-permute-done | bytes 331808 | tf_op jit(solution)/shard_map/while/body/ppermute | solution.py:309
  504.3 7.6 %collective-permute-done.20 = bf16[144,1152]{1,0:T(8,128)(2,1)} collective-permute-done((bf16[144,1152]{1,0:T(8,128)(2,1)}, bf16[144,1152]{1,0:T(8,128)(2,1)}, u32[]{:S(2)}, u32[]{:S(2)}) %collective-permute-start.20) | collective-permute-done | bytes 331808 | tf_op jit(solution)/shard_map/while/body/ppermute | solution.py:309
  517.8 5.8 collective-permute-done.10
  523.6 5.8 collective-permute-done.17
  529.8 6.1 collective-permute-done.21
  539.0 12.1 %collective-permute-done.11 = bf16[72,1152]{1,0:T(8,128)(2,1)S(1)} collective-permute-done((bf16[72,1152]{1,0:T(8,128)(2,1)S(1)}, bf16[72,1152]{1,0:T(8,128)(2,1)S(1)}, u32[]{:S(2)}, u32[]{:S(2)}) %collective-permute-start.11) | collective-permute-done | bytes 165920 | tf_op jit(solution)/shard_map/while/body/ppermute | solution.py:309
  558.9 4.7 collective-permute-done.12
  565.4 4.9 collective-permute-done.6
  573.9 5.8 fusion.143
  585.4 8.0 %outer.10 = f32[576,6912]{1,0:T(8,128)} custom-call(bf16[32,576]{1,0:T(8,128)(2,1)S(1)} %get-tuple-element.717.left_ref, bf16[32,6912]{1,0:T(8,128)(2,1)} %slice.353.right_ref), custom_call_target="tpu_custom_call" | custom-call | tf_op jit(solution)/shard_map/while/body/outer/pallas_call | solution.py:392
  601.3 7.2 %collective-permute-done.24 = bf16[72,1152]{1,0:T(8,128)(2,1)S(1)} collective-permute-done((bf16[72,1152]{1,0:T(8,128)(2,1)S(1)}, bf16[72,1152]{1,0:T(8,128)(2,1)S(1)}, u32[]{:S(2)}, u32[]{:S(2)}) %collective-permute-start.24) | collective-permute-done | bytes 165920 | tf_op jit(solution)/shard_map/while/body/ppermute | solution.py:309
  610.3 5.2 collective-permute-done.27
  618.0 6.9 %collective-permute-done.28 = bf16[144,1152]{1,0:T(8,128)(2,1)S(1)} collective-permute-done((bf16[144,1152]{1,0:T(8,128)(2,1)S(1)}, bf16[144,1152]{1,0:T(8,128)(2,1)S(1)}, u32[]{:S(2)}, u32[]{:S(2)}) %collective-permute-start.28) | collective-permute-done | bytes 331808 | tf_op jit(solution)/shard_map/while/body/ppermute | solution.py:309
  638.7 4.8 maximum_convert_fusion
  643.5 8.2 %convert_element_type.482 = f32[576,4608]{1,0:T(8,128)} convert(bf16[576,4608]{1,0:T(8,128)(2,1)} %all-reduce.5.cloned.1.call-done) | non-fusion elementwise | flops 2654208 | bytes 15925248 | tf_op jit(solution)/shard_map/convert_element_type | solution.py:672
  (479 shorter events, 250.7 us)
Async XLA Ops:
  7.2 65.2 %all-gather.6.cloned.1.call-start = ((), (), s32[]{:S(2)}) async-start(), calls=%async_computation.7 | async-start | bytes 4700160 | tf_op jit(solution)/shard_map/all_gather | solution.py:116
  13.4 15.9 %collective-permute-start.32 = (bf16[8,1152]{1,0:T(8,128)(2,1)S(1)}, bf16[8,1152]{1,0:T(8,128)(2,1)S(1)}, u32[]{:S(2)}, u32[]{:S(2)}) collective-permute-start(bf16[8,1152]{1,0:T(8,128)(2,1)S(1)} %copy-done.64), channel_id=1, source_target_pairs={{0,16},{16,0},{1,17},{17,1},{2,18},{18,2},{3,19},{19,3},{4,20},{20... | collective-permute-start | bytes 55304 | tf_op jit(solution)/shard_map/ppermute | solution.py:53
  19.2 176.5 %all-gather.8.cloned.1.call-start = ((), (), s32[]{:S(2)}) async-start(), calls=%async_computation.8 | async-start | bytes 1566720 | tf_op jit(solution)/shard_map/all_gather | solution.py:116
  45.8 168.3 %all-gather.10.cloned.1.call-start = ((), (), s32[]{:S(2)}) async-start(), calls=%async_computation.9 | async-start | bytes 6266880 | tf_op jit(solution)/shard_map/all_gather | solution.py:116
  85.3 52.8 %all-to-all-start.2 = ((bf16[16,1,3,72,256]{4,3,2,1,0:T(8,128)(2,1)}), bf16[16,1,3,72,256]{4,3,2,1,0:T(8,128)(2,1)}, u32[]{:S(2)}, u32[]{:S(2)}) async-start(bf16[16,1,3,72,256]{4,3,2,1,0:T(8,128)(2,1)} %bitcast.171), calls=%async_computation.2 | async-start | bytes 3538944 | tf_op jit(solution)/shard_map/all_to_all | solution.py:352
  94.6 41.0 %collective-permute-start.37 = (bf16[768,1152]{1,0:T(8,128)(2,1)S(1)}, bf16[768,1152]{1,0:T(8,128)(2,1)}, u32[]{:S(2)}, u32[]{:S(2)}) collective-permute-start(bf16[768,1152]{1,0:T(8,128)(2,1)S(1)} %get-tuple-element.311), channel_id=1, source_target_pairs={{0,16},{16,0},{1,17},{17,1},{2,18},{18,2},{3,19},{19,3},{4,20},{20... | collective-permute-start | bytes 5308424 | tf_op jit(solution)/shard_map/ppermute | solution.py:53
  135.7 55.1 %collective-permute-start.40 = (bf16[768,1152]{1,0:T(8,128)(2,1)}, bf16[768,1152]{1,0:T(8,128)(2,1)}, u32[]{:S(2)}, u32[]{:S(2)}) collective-permute-start(bf16[768,1152]{1,0:T(8,128)(2,1)} %get-tuple-element.314), channel_id=1, source_target_pairs={{0,16},{16,0},{1,17},{17,1},{2,18},{18,2},{3,19},{19,3},{4,20},{20... | collective-permute-start | bytes 5308424 | tf_op jit(solution)/shard_map/ppermute | solution.py:53
  150.1 40.6 %all-to-all-start.3 = ((bf16[16,1,72,256]{3,2,1,0:T(8,128)(2,1)}), bf16[16,1,72,256]{3,2,1,0:T(8,128)(2,1)}, u32[]{:S(2)}, u32[]{:S(2)}) async-start(bf16[16,1,72,256]{3,2,1,0:T(8,128)(2,1)} %get-tuple-element.313.refs_3_), calls=%async_computation.3 | async-start | bytes 1179648 | tf_op jit(solution)/shard_map/all_to_all | solution.py:352
  155.0 84.8 %all-gather.12.cloned.1.call-start = ((), (), s32[]{:S(2)}) async-start(), calls=%async_computation.10 | async-start | bytes 1880064 | tf_op jit(solution)/shard_map/all_gather | solution.py:116
  155.1 23.3 %collective-permute-start.38 = (bf16[576,32]{0,1:T(8,128)(2,1)S(1)}, bf16[576,32]{0,1:T(8,128)(2,1)}, u32[]{:S(2)}, u32[]{:S(2)}) collective-permute-start(bf16[576,32]{0,1:T(8,128)(2,1)S(1)} %copy-done.51), channel_id=1, source_target_pairs={{0,16},{16,0},{1,17},{17,1},{2,18},{18,2},{3,19},{19,3},{4,20},{20... | collective-permute-start | bytes 110600 | tf_op jit(solution)/shard_map/ppermute | solution.py:53
  161.7 24.4 %collective-permute-start.39 = (bf16[256,576]{0,1:T(8,128)(2,1)}, bf16[256,576]{0,1:T(8,128)(2,1)}, u32[]{:S(2)}, u32[]{:S(2)}) collective-permute-start(bf16[256,576]{0,1:T(8,128)(2,1)} %copy-done.23), channel_id=1, source_target_pairs={{0,16},{16,0},{1,17},{17,1},{2,18},{18,2},{3,19},{19,3},{4,20},{20... | collective-permute-start | bytes 884744 | tf_op jit(solution)/shard_map/ppermute | solution.py:53
  162.6 23.0 %collective-permute-start.44 = (bf16[48,1152]{1,0:T(8,128)(2,1)S(1)}, bf16[48,1152]{1,0:T(8,128)(2,1)}, u32[]{:S(2)}, u32[]{:S(2)}) collective-permute-start(bf16[48,1152]{1,0:T(8,128)(2,1)S(1)} %constant_dynamic-slice_fusion.12), channel_id=1, source_target_pairs={{0,16},{16,0},{1,17},{17,1},{2,18},{18,2},{3,19},{19,3},{4,20},{20... | collective-permute-start | bytes 331784 | tf_op jit(solution)/shard_map/ppermute | solution.py:53
  185.6 200.7 %reduce-scatter.2.cloned.1.call-start = ((), (), s32[]{:S(2)}) async-start(), calls=%async_computation.11 | async-start | bytes 5640192 | tf_op jit(solution)/shard_map/reduce_scatter | solution.py:582
  194.3 31.3 %collective-permute-start.42 = (bf16[576,256]{1,0:T(8,128)(2,1)}, bf16[576,256]{1,0:T(8,128)(2,1)}, u32[]{:S(2)}, u32[]{:S(2)}) collective-permute-start(bf16[576,256]{1,0:T(8,128)(2,1)} %get-tuple-element.502), channel_id=1, source_target_pairs={{0,16},{16,0},{1,17},{17,1},{2,18},{18,2},{3,19},{19,3},{4,20},{20... | collective-permute-start | bytes 884744 | tf_op jit(solution)/shard_map/ppermute | solution.py:53
  213.5 14.1 %collective-permute-start.43 = (bf16[256,576]{0,1:T(8,128)(2,1)}, bf16[256,576]{0,1:T(8,128)(2,1)}, u32[]{:S(2)}, u32[]{:S(2)}) collective-permute-start(bf16[256,576]{0,1:T(8,128)(2,1)} %get-tuple-element.498), channel_id=1, source_target_pairs={{0,16},{16,0},{1,17},{17,1},{2,18},{18,2},{3,19},{19,3},{4,20},{20... | collective-permute-start | bytes 884744 | tf_op jit(solution)/shard_map/ppermute | solution.py:53
  230.6 41.8 %collective-permute-start.45 = (bf16[256,2304]{1,0:T(8,128)(2,1)}, bf16[256,2304]{1,0:T(8,128)(2,1)}, u32[]{:S(2)}, u32[]{:S(2)}) collective-permute-start(bf16[256,2304]{1,0:T(8,128)(2,1)} %get-tuple-element.487), channel_id=1, source_target_pairs={{0,16},{16,0},{1,17},{17,1},{2,18},{18,2},{3,19},{19,3},{4,20},{20... | collective-permute-start | bytes 3538952 | tf_op jit(solution)/shard_map/ppermute | solution.py:53
  249.1 23.3 %collective-permute-start.46 = (bf16[256,1152]{1,0:T(8,128)(2,1)S(1)}, bf16[256,1152]{1,0:T(8,128)(2,1)}, u32[]{:S(2)}, u32[]{:S(2)}) collective-permute-start(bf16[256,1152]{1,0:T(8,128)(2,1)S(1)} %bitcast.174), channel_id=1, source_target_pairs={{0,16},{16,0},{1,17},{17,1},{2,18},{18,2},{3,19},{19,3},{4,20},{20... | collective-permute-start | bytes 1769480 | tf_op jit(solution)/shard_map/ppermute | solution.py:53
  261.4 63.7 %collective-permute-start.47 = (bf16[256,4608]{1,0:T(8,128)(2,1)}, bf16[256,4608]{1,0:T(8,128)(2,1)}, u32[]{:S(2)}, u32[]{:S(2)}) collective-permute-start(bf16[256,4608]{1,0:T(8,128)(2,1)} %fusion.12), channel_id=1, source_target_pairs={{0,16},{16,0},{1,17},{17,1},{2,18},{18,2},{3,19},{19,3},{4,20},{20... | collective-permute-start | bytes 7077896 | tf_op jit(solution)/shard_map/ppermute | solution.py:53
  325.1 61.3 %all-to-all-start.5 = ((bf16[16,1,3,72,256]{4,3,2,1,0:T(8,128)(2,1)}), bf16[16,1,3,72,256]{4,3,2,1,0:T(8,128)(2,1)}, u32[]{:S(2)}, u32[]{:S(2)}) async-start(bf16[16,1,3,72,256]{4,3,2,1,0:T(8,128)(2,1)} %attend_back.1), calls=%async_computation.5 | async-start | bytes 3538944 | tf_op jit(solution)/shard_map/all_to_all | solution.py:352
  329.7 111.0 %all-gather.14.cloned.1.call-start = ((), (), s32[]{:S(2)}) async-start(), calls=%async_computation.12 | async-start | bytes 5640192 | tf_op jit(solution)/shard_map/all_gather | solution.py:602
  330.2 18.3 %collective-permute-start.48 = (bf16[256,1152]{1,0:T(8,128)(2,1)}, bf16[256,1152]{1,0:T(8,128)(2,1)}, u32[]{:S(2)}, u32[]{:S(2)}) collective-permute-start(bf16[256,1152]{1,0:T(8,128)(2,1)} %bitcast.196), channel_id=1, source_target_pairs={{0,16},{16,0},{1,17},{17,1},{2,18},{18,2},{3,19},{19,3},{4,20},{20... | collective-permute-start | bytes 1769480 | tf_op jit(solution)/shard_map/ppermute | solution.py:53
  386.4 257.1 %all-reduce.5.cloned.1.call-start = ((), (), s32[]{:S(2)}) async-start(), calls=%async_computation.13 | async-start | bytes 10616832 | tf_op jit(solution)/shard_map/psum | solution.py:606
  391.3 40.9 %collective-permute-start.51 = (bf16[3456,256]{1,0:T(8,128)(2,1)}, bf16[3456,256]{1,0:T(8,128)(2,1)}, u32[]{:S(2)}, u32[]{:S(2)}) collective-permute-start(bf16[3456,256]{1,0:T(8,128)(2,1)} %bitcast.30), channel_id=1, source_target_pairs={{0,16},{16,0},{1,17},{17,1},{2,18},{18,2},{3,19},{19,3},{4,20},{20... | collective-permute-start | bytes 5308424 | tf_op jit(solution)/shard_map/ppermute | solution.py:53
  448.3 29.9 %all-to-all-start = ((bf16[16,11,1152]{2,1,0:T(8,128)(2,1)}), bf16[16,11,1152]{2,1,0:T(8,128)(2,1)S(1)}, u32[]{:S(2)}, u32[]{:S(2)}) async-start(bf16[16,11,1152]{2,1,0:T(8,128)(2,1)} %copy.153), calls=%async_computation | async-start | bytes 1179648 | tf_op jit(solution)/shard_map/while/body/all_to_all | solution.py:352
  452.7 13.7 %collective-permute-start.1 = (bf16[288,1152]{1,0:T(8,128)(2,1)S(1)}, bf16[288,1152]{1,0:T(8,128)(2,1)}, u32[]{:S(2)}, u32[]{:S(2)}) collective-permute-start(bf16[288,1152]{1,0:T(8,128)(2,1)S(1)} %constant_dynamic-slice_fusion.28), channel_id=1, source_target_pairs={{0,4},{4,0},{8,12},{12,8},{1,5},{5,1},{9,13},{13,9},{2,6},{6,2},{1... | collective-permute-start | bytes 1990664 | tf_op jit(solution)/shard_map/while/body/ppermute | solution.py:309
  455.1 15.1 %collective-permute-start.8 = (bf16[288,1152]{1,0:T(8,128)(2,1)}, bf16[288,1152]{1,0:T(8,128)(2,1)}, u32[]{:S(2)}, u32[]{:S(2)}) collective-permute-start(bf16[288,1152]{1,0:T(8,128)(2,1)} %constant_dynamic-slice_fusion.31), channel_id=1, source_target_pairs={{0,4},{4,0},{8,12},{12,8},{1,5},{5,1},{9,13},{13,9},{2,6},{6,2},{1... | collective-permute-start | bytes 1990664 | tf_op jit(solution)/shard_map/while/body/ppermute | solution.py:309
  457.3 15.4 %collective-permute-start.15 = (bf16[288,1152]{1,0:T(8,128)(2,1)}, bf16[288,1152]{1,0:T(8,128)(2,1)}, u32[]{:S(2)}, u32[]{:S(2)}) collective-permute-start(bf16[288,1152]{1,0:T(8,128)(2,1)} %constant_dynamic-slice_fusion.34), channel_id=1, source_target_pairs={{0,4},{4,0},{8,12},{12,8},{1,5},{5,1},{9,13},{13,9},{2,6},{6,2},{1... | collective-permute-start | bytes 1990664 | tf_op jit(solution)/shard_map/while/body/ppermute | solution.py:309
  458.8 18.0 %collective-permute-start.19 = (bf16[288,1152]{1,0:T(8,128)(2,1)S(1)}, bf16[288,1152]{1,0:T(8,128)(2,1)}, u32[]{:S(2)}, u32[]{:S(2)}) collective-permute-start(bf16[288,1152]{1,0:T(8,128)(2,1)S(1)} %constant_dynamic-slice_fusion.37), channel_id=1, source_target_pairs={{0,4},{4,0},{8,12},{12,8},{1,5},{5,1},{9,13},{13,9},{2,6},{6,2},{1... | collective-permute-start | bytes 1990664 | tf_op jit(solution)/shard_map/while/body/ppermute | solution.py:309
  468.4 20.0 %collective-permute-start.2 = (bf16[144,1152]{1,0:T(8,128)(2,1)}, bf16[144,1152]{1,0:T(8,128)(2,1)}, u32[]{:S(2)}, u32[]{:S(2)}) collective-permute-start(bf16[144,1152]{1,0:T(8,128)(2,1)} %constant_dynamic-slice_fusion.29), channel_id=1, source_target_pairs={{0,8},{4,12},{8,0},{12,4},{1,9},{5,13},{9,1},{13,5},{2,10},{6,14},... | collective-permute-start | bytes 995336 | tf_op jit(solution)/shard_map/while/body/ppermute | solution.py:309
  472.5 19.2 %collective-permute-start.9 = (bf16[144,1152]{1,0:T(8,128)(2,1)}, bf16[144,1152]{1,0:T(8,128)(2,1)}, u32[]{:S(2)}, u32[]{:S(2)}) collective-permute-start(bf16[144,1152]{1,0:T(8,128)(2,1)} %constant_dynamic-slice_fusion.32), channel_id=1, source_target_pairs={{0,8},{4,12},{8,0},{12,4},{1,9},{5,13},{9,1},{13,5},{2,10},{6,14},... | collective-permute-start | bytes 995336 | tf_op jit(solution)/shard_map/while/body/ppermute | solution.py:309
  474.9 28.2 %collective-permute-start.16 = (bf16[144,1152]{1,0:T(8,128)(2,1)}, bf16[144,1152]{1,0:T(8,128)(2,1)}, u32[]{:S(2)}, u32[]{:S(2)}) collective-permute-start(bf16[144,1152]{1,0:T(8,128)(2,1)} %constant_dynamic-slice_fusion.35), channel_id=1, source_target_pairs={{0,8},{4,12},{8,0},{12,4},{1,9},{5,13},{9,1},{13,5},{2,10},{6,14},... | collective-permute-start | bytes 995336 | tf_op jit(solution)/shard_map/while/body/ppermute | solution.py:309
  480.5 31.4 %collective-permute-start.20 = (bf16[144,1152]{1,0:T(8,128)(2,1)}, bf16[144,1152]{1,0:T(8,128)(2,1)}, u32[]{:S(2)}, u32[]{:S(2)}) collective-permute-start(bf16[144,1152]{1,0:T(8,128)(2,1)} %constant_dynamic-slice_fusion.38), channel_id=1, source_target_pairs={{0,8},{4,12},{8,0},{12,4},{1,9},{5,13},{9,1},{13,5},{2,10},{6,14},... | collective-permute-start | bytes 995336 | tf_op jit(solution)/shard_map/while/body/ppermute | solution.py:309
  483.7 86.8 %all-to-all-start.1 = ((bf16[16,2,11,1152]{3,1,2,0:T(2,128)(2,1)}), bf16[16,2,11,1152]{3,1,2,0:T(2,128)(2,1)S(1)}, u32[]{:S(2)}, u32[]{:S(2)}) async-start(bf16[16,2,11,1152]{3,1,2,0:T(2,128)(2,1)} %broadcast_in_dim.51), calls=%async_computation.1 | async-start | bytes 1622016 | tf_op jit(solution)/shard_map/while/body/all_to_all | solution.py:352
  489.5 25.6 %collective-permute-start.3 = (bf16[72,1152]{1,0:T(8,128)(2,1)S(1)}, bf16[72,1152]{1,0:T(8,128)(2,1)S(1)}, u32[]{:S(2)}, u32[]{:S(2)}) collective-permute-start(bf16[72,1152]{1,0:T(8,128)(2,1)S(1)} %constant_dynamic-slice_fusion.30), channel_id=1, source_target_pairs={{0,1},{1,0},{2,3},{3,2},{4,5},{5,4},{6,7},{7,6},{8,9},{9,8},{10,11... | collective-permute-start | bytes 497672 | tf_op jit(solution)/shard_map/while/body/ppermute | solution.py:309
  492.8 30.8 %collective-permute-start.10 = (bf16[72,1152]{1,0:T(8,128)(2,1)S(1)}, bf16[72,1152]{1,0:T(8,128)(2,1)S(1)}, u32[]{:S(2)}, u32[]{:S(2)}) collective-permute-start(bf16[72,1152]{1,0:T(8,128)(2,1)S(1)} %constant_dynamic-slice_fusion.33), channel_id=1, source_target_pairs={{0,1},{1,0},{2,3},{3,2},{4,5},{5,4},{6,7},{7,6},{8,9},{9,8},{10,11... | collective-permute-start | bytes 497672 | tf_op jit(solution)/shard_map/while/body/ppermute | solution.py:309
  504.2 25.3 %collective-permute-start.17 = (bf16[72,1152]{1,0:T(8,128)(2,1)S(1)}, bf16[72,1152]{1,0:T(8,128)(2,1)S(1)}, u32[]{:S(2)}, u32[]{:S(2)}) collective-permute-start(bf16[72,1152]{1,0:T(8,128)(2,1)S(1)} %constant_dynamic-slice_fusion.36), channel_id=1, source_target_pairs={{0,1},{1,0},{2,3},{3,2},{4,5},{5,4},{6,7},{7,6},{8,9},{9,8},{10,11... | collective-permute-start | bytes 497672 | tf_op jit(solution)/shard_map/while/body/ppermute | solution.py:309
  512.9 22.9 %collective-permute-start.21 = (bf16[72,1152]{1,0:T(8,128)(2,1)S(1)}, bf16[72,1152]{1,0:T(8,128)(2,1)S(1)}, u32[]{:S(2)}, u32[]{:S(2)}) collective-permute-start(bf16[72,1152]{1,0:T(8,128)(2,1)S(1)} %constant_dynamic-slice_fusion.39), channel_id=1, source_target_pairs={{0,1},{1,0},{2,3},{3,2},{4,5},{5,4},{6,7},{7,6},{8,9},{9,8},{10,11... | collective-permute-start | bytes 497672 | tf_op jit(solution)/shard_map/while/body/ppermute | solution.py:309
  515.2 21.2 %collective-permute-start.4 = (bf16[72,1152]{1,0:T(8,128)(2,1)S(1)}, bf16[72,1152]{1,0:T(8,128)(2,1)S(1)}, u32[]{:S(2)}, u32[]{:S(2)}) collective-permute-start(bf16[72,1152]{1,0:T(8,128)(2,1)S(1)} %add_convert_fusion.38), channel_id=1, source_target_pairs={{0,2},{1,3},{2,0},{3,1},{4,6},{5,7},{6,4},{7,5},{8,10},{9,11},{10,... | collective-permute-start | bytes 497672 | tf_op jit(solution)/shard_map/while/body/ppermute | solution.py:309
  523.6 27.5 %collective-permute-start.11 = (bf16[72,1152]{1,0:T(8,128)(2,1)S(1)}, bf16[72,1152]{1,0:T(8,128)(2,1)S(1)}, u32[]{:S(2)}, u32[]{:S(2)}) collective-permute-start(bf16[72,1152]{1,0:T(8,128)(2,1)S(1)} %add_convert_fusion.42), channel_id=1, source_target_pairs={{0,2},{1,3},{2,0},{3,1},{4,6},{5,7},{6,4},{7,5},{8,10},{9,11},{10,... | collective-permute-start | bytes 497672 | tf_op jit(solution)/shard_map/while/body/ppermute | solution.py:309
  529.5 25.3 %collective-permute-start.18 = (bf16[72,1152]{1,0:T(8,128)(2,1)S(1)}, bf16[72,1152]{1,0:T(8,128)(2,1)S(1)}, u32[]{:S(2)}, u32[]{:S(2)}) collective-permute-start(bf16[72,1152]{1,0:T(8,128)(2,1)S(1)} %add_convert_fusion.46), channel_id=1, source_target_pairs={{0,2},{1,3},{2,0},{3,1},{4,6},{5,7},{6,4},{7,5},{8,10},{9,11},{10,... | collective-permute-start | bytes 497672 | tf_op jit(solution)/shard_map/while/body/ppermute | solution.py:309
  535.9 22.3 %collective-permute-start.22 = (bf16[72,1152]{1,0:T(8,128)(2,1)S(1)}, bf16[72,1152]{1,0:T(8,128)(2,1)S(1)}, u32[]{:S(2)}, u32[]{:S(2)}) collective-permute-start(bf16[72,1152]{1,0:T(8,128)(2,1)S(1)} %add_convert_fusion.50), channel_id=1, source_target_pairs={{0,2},{1,3},{2,0},{3,1},{4,6},{5,7},{6,4},{7,5},{8,10},{9,11},{10,... | collective-permute-start | bytes 497672 | tf_op jit(solution)/shard_map/while/body/ppermute | solution.py:309
  536.4 18.4 %collective-permute-start.5 = (bf16[72,1152]{1,0:T(8,128)(2,1)S(1)}, bf16[72,1152]{1,0:T(8,128)(2,1)S(1)}, u32[]{:S(2)}, u32[]{:S(2)}) collective-permute-start(bf16[72,1152]{1,0:T(8,128)(2,1)S(1)} %add_convert_fusion.39), channel_id=1, source_target_pairs={{0,1},{1,0},{2,3},{3,2},{4,5},{5,4},{6,7},{7,6},{8,9},{9,8},{10,11... | collective-permute-start | bytes 497672 | tf_op jit(solution)/shard_map/while/body/ppermute | solution.py:309
  554.9 15.4 %collective-permute-start.6 = (bf16[144,1152]{1,0:T(8,128)(2,1)S(1)}, bf16[144,1152]{1,0:T(8,128)(2,1)S(1)}, u32[]{:S(2)}, u32[]{:S(2)}) collective-permute-start(bf16[144,1152]{1,0:T(8,128)(2,1)S(1)} %maximum_select_fusion.24), channel_id=1, source_target_pairs={{0,8},{4,12},{8,0},{12,4},{1,9},{5,13},{9,1},{13,5},{2,10},{6,14},... | collective-permute-start | bytes 995336 | tf_op jit(solution)/shard_map/while/body/ppermute | solution.py:309
  563.7 34.2 %collective-permute-start.13 = (bf16[144,1152]{1,0:T(8,128)(2,1)S(1)}, bf16[144,1152]{1,0:T(8,128)(2,1)}, u32[]{:S(2)}, u32[]{:S(2)}) collective-permute-start(bf16[144,1152]{1,0:T(8,128)(2,1)S(1)} %maximum_select_fusion.27), channel_id=1, source_target_pairs={{0,8},{4,12},{8,0},{12,4},{1,9},{5,13},{9,1},{13,5},{2,10},{6,14},... | collective-permute-start | bytes 995336 | tf_op jit(solution)/shard_map/while/body/ppermute | solution.py:309
  570.5 54.7 %collective-permute-start.7 = (bf16[288,1152]{1,0:T(8,128)(2,1)S(1)}, bf16[288,1152]{1,0:T(8,128)(2,1)}, u32[]{:S(2)}, u32[]{:S(2)}) collective-permute-start(bf16[288,1152]{1,0:T(8,128)(2,1)S(1)} %maximum_select_fusion.25), channel_id=1, source_target_pairs={{0,4},{4,0},{8,12},{12,8},{1,5},{5,1},{9,13},{13,9},{2,6},{6,2},{1... | collective-permute-start | bytes 1990664 | tf_op jit(solution)/shard_map/while/body/ppermute | solution.py:309
  581.2 15.9 %collective-permute-start.23 = (f32[16,576]{1,0:T(8,128)}, f32[16,576]{1,0:T(8,128)S(1)}, u32[]{:S(2)}, u32[]{:S(2)}) collective-permute-start(f32[16,576]{1,0:T(8,128)} %slice.352), channel_id=1, source_target_pairs={{0,16},{16,0},{1,17},{17,1},{2,18},{18,2},{3,19},{19,3},{4,20},{20... | collective-permute-start | bytes 110600 | tf_op jit(solution)/shard_map/while/body/ppermute | solution.py:58
  599.2 28.7 %collective-permute-start.14 = (bf16[288,1152]{1,0:T(8,128)(2,1)S(1)}, bf16[288,1152]{1,0:T(8,128)(2,1)S(1)}, u32[]{:S(2)}, u32[]{:S(2)}) collective-permute-start(bf16[288,1152]{1,0:T(8,128)(2,1)S(1)} %maximum_select_fusion.28), channel_id=1, source_target_pairs={{0,4},{4,0},{8,12},{12,8},{1,5},{5,1},{9,13},{13,9},{2,6},{6,2},{1... | collective-permute-start | bytes 1990664 | tf_op jit(solution)/shard_map/while/body/ppermute | solution.py:309
  599.5 16.0 %collective-permute-start.27 = (bf16[72,1152]{1,0:T(8,128)(2,1)S(1)}, bf16[72,1152]{1,0:T(8,128)(2,1)S(1)}, u32[]{:S(2)}, u32[]{:S(2)}) collective-permute-start(bf16[72,1152]{1,0:T(8,128)(2,1)S(1)} %copy-done.9), channel_id=1, source_target_pairs={{0,1},{1,0},{2,3},{3,2},{4,5},{5,4},{6,7},{7,6},{8,9},{9,8},{10,11... | collective-permute-start | bytes 497672 | tf_op jit(solution)/shard_map/while/body/ppermute | solution.py:309
  (92 other events, 538.8 us)
Sparse Core Ops, SparseCore 0:
  19.3 53.0 all-gather.5
  74.6 51.6 all-gather.7
  128.6 68.3 all-gather.9
  199.1 40.1 all-gather.11
  280.0 98.9 reduce-scatter.1
  386.5 54.0 all-gather.13
  447.4 177.5 all-reduce.4

commit v4 on v3

--- a/solution.py
+++ b/solution.py
@@ -602,7 +602,7 @@
     g_down = lax.all_gather(g_down, RC, axis=0, tiled=True)
     dqkv = dqkv.transpose(2, 0, 1, 3, 4).reshape(3 * width, rows)
     dqkv_all = jnp.concatenate(swap_full(dqkv), 1)
-    dqkv_all, g_up, g_down = lax.optimization_barrier((dqkv_all, g_up, g_down))
+    g_up, g_down = lax.optimization_barrier((g_up, g_down))
     g_up = lax.psum(g_up, RC)
     da1 = [dotd(dqkv, w_qkv, 0, 1)]
     for other in o_qkv:

time: 669 us -> 662 us (0.990)
    unnamed x162 -> x164, local copies, waits for them, and re-layouts: 22.6 us -> 22.6 us
  transfers between devices with their start and end apart: 64 -> 64, of which waited for: 34 -> 33; matrix products, arithmetic and copies ran while one was open for 36% -> 36% of each run, Pallas kernels for 6% -> 6%
where the time goes in v4:
time: 662 us; the launch traced here: 652 us
  waiting for transfers between devices  243 us (37%)
  matrix products  103 us (16%)
  other arithmetic  78.1 us (12%)
  starting transfers between devices  76.9 us (12%)
  local copies, waits for them, and re-layouts  71.1 us (11%)
  Pallas kernels  40.9 us (6%)
  blocking collectives  23.1 us (3%)
  between operations  15.7 us (2%)
    ppermute x18, waiting for transfers between devices, send_down(): lax.ppermute(value, 'img', [(j, (j - k) % size) for j in range(size)])  109 us
    dot_general x34, matrix products, dotd(): lax.dot_general(left, right, (((ldim,), (rdim,)), ((), ())), preferred_el...  103 us
    ppermute x28, waiting for transfers between devices, swapped(): lax.ppermute(value, axis, [(j, j ^ bit) for j in range(lax.axis_size(axis...  85.2 us
    all_to_all x5, waiting for transfers between devices, exchange(): return lax.all_to_all(x, RC, split_axis=0, concat_axis=0, tiled=True)  29.3 us
    ppermute x28, starting transfers between devices, swapped(): lax.ppermute(value, axis, [(j, j ^ bit) for j in range(lax.axis_size(axis...  25.5 us
    all_to_all x1, blocking collectives, exchange(): return lax.all_to_all(x, RC, split_axis=0, concat_axis=0, tiled=True)  23.1 us
    all_to_all x5, starting transfers between devices, exchange(): return lax.all_to_all(x, RC, split_axis=0, concat_axis=0, tiled=True)  23 us
    unnamed x164, local copies, waits for them, and re-layouts  22.6 us
  transfers between devices with their start and end apart: 64, of which 33 were waited for; matrix products, arithmetic and copies ran while one was open for 36% of the time, Pallas kernels for 6%

profile of v4, /device:TPU:0, one launch (start us, length us, event | category | flops | bytes accessed | tf_op | source)
XLA Modules:
  0.0 651.7 jit_solution(12942538996331849674)
XLA Ops:
  13.5 5.0 collective-permute-done.35
  23.9 4.0 collective-permute-done.31
  35.2 4.6 collective-permute-done.34
  41.5 4.2 collective-permute-done.41
  47.9 7.0 %collective-permute-done.36 = bf16[40,4608]{1,0:T(8,128)(2,1)} collective-permute-done((bf16[40,4608]{1,0:T(8,128)(2,1)S(1)}, bf16[40,4608]{1,0:T(8,128)(2,1)}, u32[]{:S(2)}, u32[]{:S(2)}) %collective-permute-start.36) | collective-permute-done | bytes 368672 | tf_op jit(solution)/shard_map/ppermute | solution.py:53
  60.7 5.6 convolution_bitcast_fusion
  66.3 6.1 all-gather.6.cloned.1.call-done
  72.4 6.2 fusion.5
  78.6 3.9 copy.117
  85.3 4.6 all-to-all-start.2
  89.9 4.7 fusion.82
  96.1 39.6 %collective-permute-done.37 = bf16[768,1152]{1,0:T(8,128)(2,1)} collective-permute-done((bf16[768,1152]{1,0:T(8,128)(2,1)S(1)}, bf16[768,1152]{1,0:T(8,128)(2,1)}, u32[]{:S(2)}, u32[]{:S(2)}) %collective-permute-start.37) | collective-permute-done | bytes 1769504 | tf_op jit(solution)/shard_map/ppermute | solution.py:53
  138.1 13.4 %attend.1 = (bf16[16,1,72,256]{3,2,1,0:T(8,128)(2,1)}, f32[1,4,1,1024]{3,2,1,0:T(1,128)}) custom-call(s32[4]{0:T(128)} %refs_0_.3, bf16[16,1,3,72,256]{4,3,2,1,0:T(8,128)(2,1)} %all-to-all-done.2.refs_1_), custom_call_target="tpu_custom_call" | custom-call | flops 10000000000 | bytes 40000000 | tf_op jit(solution)/shard_map/attend/pallas_call | solution.py:247
  151.5 4.9 all-to-all-start.3
  163.4 14.9 %collective-permute-done.38 = bf16[576,32]{0,1:T(8,128)(2,1)} collective-permute-done((bf16[576,32]{0,1:T(8,128)(2,1)S(1)}, bf16[576,32]{0,1:T(8,128)(2,1)}, u32[]{:S(2)}, u32[]{:S(2)}) %collective-permute-start.38) | collective-permute-done | bytes 36896 | tf_op jit(solution)/shard_map/ppermute | solution.py:53
  179.1 6.5 collective-permute-done.44
  206.9 6.7 %fusion.88 = f32[256,4608]{1,0:T(8,128)} fusion(bf16[256,576]{0,1:T(8,128)(2,1)S(1)} %get-tuple-element.497, bf16[576,4608]{1,0:T(8,128)(2,1)} %param.21), kind=kOutput, calls=%fused_computation.298 | convolution fusion | flops 1358954496 | bytes 10321920 | tf_op jit(solution)/shard_map/dot_general | solution.py:46
  214.2 9.7 %multiply_convert_fusion = (bf16[256,4608]{1,0:T(8,128)(2,1)S(1)}, f32[256,4608]{1,0:T(8,128)}) fusion(f32[256,4608]{1,0:T(8,128)} %fusion.88, bf16[640,4608]{1,0:T(8,128)(2,1)} %all-gather.10.cloned.1.call-done, bf16[256,576]{0,1:T(8,128)(2,1)} %get-tuple-element.496), kind=kOutput, calls=%fused_computation.72 | convolution fusion | flops 1521745920 | bytes 17989632 | tf_op jit(solution)/shard_map/dot_general | solution.py:46
  232.3 4.3 fusion.89
  253.6 4.2 fusion.12
  272.6 7.4 %convolution_convert_fusion = bf16[2304,1152]{1,0:T(8,128)(2,1)} fusion(bf16[256,2304]{1,0:T(8,128)(2,1)} %collective-permute-done.45, bf16[256,2304]{1,0:T(8,128)(2,1)} %copy-done.32, bf16[256,1152]{1,0:T(8,128)(2,1)} %collective-permute-done.46, bf16[256,1152]{1,0:T(8,128)(2,1)S(1)} %bitcast.177), kind=kOutput, calls=%fused_computation.51 | convolution fusion | flops 2727641088 | bytes 8847360 | tf_op jit(solution)/shard_map/dot_general | solution.py:46
  287.8 23.1 %all_to_all.40.refs_2_ = bf16[16,1,72,256]{3,2,1,0:T(8,128)(2,1)} all-to-all(bf16[16,1,72,256]{3,2,1,0:T(8,128)(2,1)S(1)} %bitcast.190), channel_id=1, replica_groups=mesh['img'=2,'row'=4,'col'=4] {'row','col'}, dimensions={0} | all-to-all | bytes 1179648 | tf_op jit(solution)/shard_map/all_to_all | solution.py:352
  310.9 15.7 %attend_back.1 = bf16[16,1,3,72,256]{4,3,2,1,0:T(8,128)(2,1)} custom-call(s32[4]{0:T(128)} %refs_0_.3, bf16[16,1,3,72,256]{4,3,2,1,0:T(8,128)(2,1)} %all-to-all-done.2.refs_1_, bf16[16,1,72,256]{3,2,1,0:T(8,128)(2,1)} %all_to_all.40.refs_2_, bf16[16,1,72,256]{3,2,1,0:T(8,128)(2,1)} %get-tuple-element.312.refs_3_, f32[1,4,1,1024]{3,2,1,0:T(1,128)} %get-tuple-element.326.refs_4_), custom_call_target="tpu_custom_call" | custom-call | flops 10000000000 | bytes 40000000 | tf_op jit(solution)/shard_map/attend_back/pallas_call | solution.py:279
  326.5 4.6 all-to-all-start.5
  334.4 13.1 %collective-permute-done.48 = bf16[256,1152]{1,0:T(8,128)(2,1)} collective-permute-done((bf16[256,1152]{1,0:T(8,128)(2,1)}, bf16[256,1152]{1,0:T(8,128)(2,1)}, u32[]{:S(2)}, u32[]{:S(2)}) %collective-permute-start.48) | collective-permute-done | bytes 589856 | tf_op jit(solution)/shard_map/ppermute | solution.py:53
  350.6 7.7 %convolution_convert_fusion.1 = bf16[576,4608]{1,0:T(8,128)(2,1)} fusion(bf16[512,576]{0,1:T(8,128)(2,1)S(1)} %copy-done.39, bf16[256,4608]{1,0:T(8,128)(2,1)} %collective-permute-done.47, bf16[256,4608]{1,0:T(8,128)(2,1)} %fusion.12), kind=kOutput, calls=%fused_computation.52 | convolution fusion | flops 2730000384 | bytes 10616832 | tf_op jit(solution)/shard_map/dot_general | solution.py:46
  358.3 28.3 %all-to-all-done.5 = bf16[16,1,3,72,256]{4,3,2,1,0:T(8,128)(2,1)} async-done(((bf16[16,1,3,72,256]{4,3,2,1,0:T(8,128)(2,1)}), bf16[16,1,3,72,256]{4,3,2,1,0:T(8,128)(2,1)}, u32[]{:S(2)}, u32[]{:S(2)}) %all-to-all-start.5) | async-done | bytes 1769504 | tf_op jit(solution)/shard_map/all_to_all | solution.py:352
  393.0 4.0 fusion.94
  417.6 14.8 %collective-permute-done.51 = bf16[3456,256]{1,0:T(8,128)(2,1)} collective-permute-done((bf16[3456,256]{1,0:T(8,128)(2,1)}, bf16[3456,256]{1,0:T(8,128)(2,1)}, u32[]{:S(2)}, u32[]{:S(2)}) %collective-permute-start.51) | collective-permute-done | bytes 1769504 | tf_op jit(solution)/shard_map/ppermute | solution.py:53
  440.7 186.2 %while.31 = (s32[]{:T(128)}, bf16[16,11,1152]{2,0,1:T(8,128)(2,1)S(1)}, bf16[576,1152]{1,0:T(8,128)(2,1)S(1)}, bf16[576,1152]{1,0:T(8,128)(2,1)}, bf16[576,1152]...) while((s32[]{:T(128)}, ...), condition=%wide.region_25.26_spmd, body=%wide.region_22.25_spmd.sunk | while | flops 395250112 | bytes 176232400 | solution.py:382
  441.9 4.3 all-to-all-start
  450.6 7.3 %convert_element_type.653 = f32[2304,1152]{1,0:T(8,128)} convert(bf16[2304,1152]{1,0:T(8,128)(2,1)} %get-tuple-element.716) | non-fusion elementwise | flops 2654208 | bytes 15925248 | tf_op jit(solution)/shard_map/while/body/convert_element_type | solution.py:647
  474.9 4.7 all-to-all-start.1
  482.7 4.0 collective-permute-done.9
  490.3 7.7 %collective-permute-done.16 = bf16[144,1152]{1,0:T(8,128)(2,1)} collective-permute-done((bf16[144,1152]{1,0:T(8,128)(2,1)}, bf16[144,1152]{1,0:T(8,128)(2,1)}, u32[]{:S(2)}, u32[]{:S(2)}) %collective-permute-start.16) | collective-permute-done | bytes 331808 | tf_op jit(solution)/shard_map/while/body/ppermute | solution.py:309
  499.1 6.5 collective-permute-done.20
  511.4 6.8 %collective-permute-done.10 = bf16[72,1152]{1,0:T(8,128)(2,1)S(1)} collective-permute-done((bf16[72,1152]{1,0:T(8,128)(2,1)S(1)}, bf16[72,1152]{1,0:T(8,128)(2,1)S(1)}, u32[]{:S(2)}, u32[]{:S(2)}) %collective-permute-start.10) | collective-permute-done | bytes 165920 | tf_op jit(solution)/shard_map/while/body/ppermute | solution.py:309
  518.3 3.9 collective-permute-done.17
  528.3 16.8 %collective-permute-done.11 = bf16[72,1152]{1,0:T(8,128)(2,1)S(1)} collective-permute-done((bf16[72,1152]{1,0:T(8,128)(2,1)S(1)}, bf16[72,1152]{1,0:T(8,128)(2,1)S(1)}, u32[]{:S(2)}, u32[]{:S(2)}) %collective-permute-start.11) | collective-permute-done | bytes 165920 | tf_op jit(solution)/shard_map/while/body/ppermute | solution.py:309
  545.2 4.8 collective-permute-done.18
  564.6 5.8 fusion.148
  575.9 8.0 %outer.10 = f32[576,6912]{1,0:T(8,128)} custom-call(bf16[32,576]{1,0:T(8,128)(2,1)S(1)} %get-tuple-element.715.left_ref, bf16[32,6912]{1,0:T(8,128)(2,1)} %slice.367.right_ref), custom_call_target="tpu_custom_call" | custom-call | tf_op jit(solution)/shard_map/while/body/outer/pallas_call | solution.py:392
  583.9 3.8 outer.11
  592.0 7.2 %collective-permute-done.24 = bf16[72,1152]{1,0:T(8,128)(2,1)S(1)} collective-permute-done((bf16[72,1152]{1,0:T(8,128)(2,1)S(1)}, bf16[72,1152]{1,0:T(8,128)(2,1)S(1)}, u32[]{:S(2)}, u32[]{:S(2)}) %collective-permute-start.24) | collective-permute-done | bytes 165920 | tf_op jit(solution)/shard_map/while/body/ppermute | solution.py:309
  600.6 5.5 collective-permute-done.27
  607.5 6.8 %collective-permute-done.25 = bf16[144,1152]{1,0:T(8,128)(2,1)S(1)} collective-permute-done((bf16[144,1152]{1,0:T(8,128)(2,1)S(1)}, bf16[144,1152]{1,0:T(8,128)(2,1)S(1)}, u32[]{:S(2)}, u32[]{:S(2)}) %collective-permute-start.25) | collective-permute-done | bytes 331808 | tf_op jit(solution)/shard_map/while/body/ppermute | solution.py:309
  614.6 5.6 collective-permute-done.28
  636.5 8.2 %convert_element_type.482 = f32[576,4608]{1,0:T(8,128)} convert(bf16[576,4608]{1,0:T(8,128)(2,1)} %all-reduce.5.cloned.1.call-done) | non-fusion elementwise | flops 2654208 | bytes 15925248 | tf_op jit(solution)/shard_map/convert_element_type | solution.py:672
  (496 shorter events, 239.2 us)
Async XLA Ops:
  7.2 65.2 %all-gather.6.cloned.1.call-start = ((), (), s32[]{:S(2)}) async-start(), calls=%async_computation.7 | async-start | bytes 4700160 | tf_op jit(solution)/shard_map/all_gather | solution.py:116
  13.4 15.9 %collective-permute-start.32 = (bf16[8,1152]{1,0:T(8,128)(2,1)S(1)}, bf16[8,1152]{1,0:T(8,128)(2,1)S(1)}, u32[]{:S(2)}, u32[]{:S(2)}) collective-permute-start(bf16[8,1152]{1,0:T(8,128)(2,1)S(1)} %copy-done.73), channel_id=1, source_target_pairs={{0,16},{16,0},{1,17},{17,1},{2,18},{18,2},{3,19},{19,3},{4,20},{20... | collective-permute-start | bytes 55304 | tf_op jit(solution)/shard_map/ppermute | solution.py:53
  19.2 176.5 %all-gather.8.cloned.1.call-start = ((), (), s32[]{:S(2)}) async-start(), calls=%async_computation.8 | async-start | bytes 1566720 | tf_op jit(solution)/shard_map/all_gather | solution.py:116
  45.8 168.4 %all-gather.10.cloned.1.call-start = ((), (), s32[]{:S(2)}) async-start(), calls=%async_computation.9 | async-start | bytes 6266880 | tf_op jit(solution)/shard_map/all_gather | solution.py:116
  85.3 52.8 %all-to-all-start.2 = ((bf16[16,1,3,72,256]{4,3,2,1,0:T(8,128)(2,1)}), bf16[16,1,3,72,256]{4,3,2,1,0:T(8,128)(2,1)}, u32[]{:S(2)}, u32[]{:S(2)}) async-start(bf16[16,1,3,72,256]{4,3,2,1,0:T(8,128)(2,1)} %bitcast.171), calls=%async_computation.2 | async-start | bytes 3538944 | tf_op jit(solution)/shard_map/all_to_all | solution.py:352
  94.6 41.0 %collective-permute-start.37 = (bf16[768,1152]{1,0:T(8,128)(2,1)S(1)}, bf16[768,1152]{1,0:T(8,128)(2,1)}, u32[]{:S(2)}, u32[]{:S(2)}) collective-permute-start(bf16[768,1152]{1,0:T(8,128)(2,1)S(1)} %get-tuple-element.310), channel_id=1, source_target_pairs={{0,16},{16,0},{1,17},{17,1},{2,18},{18,2},{3,19},{19,3},{4,20},{20... | collective-permute-start | bytes 5308424 | tf_op jit(solution)/shard_map/ppermute | solution.py:53
  135.7 55.1 %collective-permute-start.40 = (bf16[768,1152]{1,0:T(8,128)(2,1)}, bf16[768,1152]{1,0:T(8,128)(2,1)}, u32[]{:S(2)}, u32[]{:S(2)}) collective-permute-start(bf16[768,1152]{1,0:T(8,128)(2,1)} %get-tuple-element.313), channel_id=1, source_target_pairs={{0,16},{16,0},{1,17},{17,1},{2,18},{18,2},{3,19},{19,3},{4,20},{20... | collective-permute-start | bytes 5308424 | tf_op jit(solution)/shard_map/ppermute | solution.py:53
  151.5 39.3 %all-to-all-start.3 = ((bf16[16,1,72,256]{3,2,1,0:T(8,128)(2,1)}), bf16[16,1,72,256]{3,2,1,0:T(8,128)(2,1)}, u32[]{:S(2)}, u32[]{:S(2)}) async-start(bf16[16,1,72,256]{3,2,1,0:T(8,128)(2,1)} %get-tuple-element.312.refs_3_), calls=%async_computation.3 | async-start | bytes 1179648 | tf_op jit(solution)/shard_map/all_to_all | solution.py:352
  156.3 83.6 %all-gather.12.cloned.1.call-start = ((), (), s32[]{:S(2)}) async-start(), calls=%async_computation.10 | async-start | bytes 1880064 | tf_op jit(solution)/shard_map/all_gather | solution.py:116
  156.4 21.9 %collective-permute-start.38 = (bf16[576,32]{0,1:T(8,128)(2,1)S(1)}, bf16[576,32]{0,1:T(8,128)(2,1)}, u32[]{:S(2)}, u32[]{:S(2)}) collective-permute-start(bf16[576,32]{0,1:T(8,128)(2,1)S(1)} %copy-done.60), channel_id=1, source_target_pairs={{0,16},{16,0},{1,17},{17,1},{2,18},{18,2},{3,19},{19,3},{4,20},{20... | collective-permute-start | bytes 110600 | tf_op jit(solution)/shard_map/ppermute | solution.py:53
  160.4 25.7 %collective-permute-start.39 = (bf16[256,576]{0,1:T(8,128)(2,1)}, bf16[256,576]{0,1:T(8,128)(2,1)}, u32[]{:S(2)}, u32[]{:S(2)}) collective-permute-start(bf16[256,576]{0,1:T(8,128)(2,1)} %copy-done.33), channel_id=1, source_target_pairs={{0,16},{16,0},{1,17},{17,1},{2,18},{18,2},{3,19},{19,3},{4,20},{20... | collective-permute-start | bytes 884744 | tf_op jit(solution)/shard_map/ppermute | solution.py:53
  162.5 23.1 %collective-permute-start.44 = (bf16[48,1152]{1,0:T(8,128)(2,1)S(1)}, bf16[48,1152]{1,0:T(8,128)(2,1)}, u32[]{:S(2)}, u32[]{:S(2)}) collective-permute-start(bf16[48,1152]{1,0:T(8,128)(2,1)S(1)} %constant_dynamic-slice_fusion.12), channel_id=1, source_target_pairs={{0,16},{16,0},{1,17},{17,1},{2,18},{18,2},{3,19},{19,3},{4,20},{20... | collective-permute-start | bytes 331784 | tf_op jit(solution)/shard_map/ppermute | solution.py:53
  185.6 200.9 %reduce-scatter.2.cloned.1.call-start = ((), (), s32[]{:S(2)}) async-start(), calls=%async_computation.11 | async-start | bytes 5640192 | tf_op jit(solution)/shard_map/reduce_scatter | solution.py:582
  194.3 31.4 %collective-permute-start.42 = (bf16[576,256]{1,0:T(8,128)(2,1)}, bf16[576,256]{1,0:T(8,128)(2,1)}, u32[]{:S(2)}, u32[]{:S(2)}) collective-permute-start(bf16[576,256]{1,0:T(8,128)(2,1)} %get-tuple-element.500), channel_id=1, source_target_pairs={{0,16},{16,0},{1,17},{17,1},{2,18},{18,2},{3,19},{19,3},{4,20},{20... | collective-permute-start | bytes 884744 | tf_op jit(solution)/shard_map/ppermute | solution.py:53
  213.6 14.2 %collective-permute-start.43 = (bf16[256,576]{0,1:T(8,128)(2,1)}, bf16[256,576]{0,1:T(8,128)(2,1)}, u32[]{:S(2)}, u32[]{:S(2)}) collective-permute-start(bf16[256,576]{0,1:T(8,128)(2,1)} %get-tuple-element.496), channel_id=1, source_target_pairs={{0,16},{16,0},{1,17},{17,1},{2,18},{18,2},{3,19},{19,3},{4,20},{20... | collective-permute-start | bytes 884744 | tf_op jit(solution)/shard_map/ppermute | solution.py:53
  230.8 41.8 %collective-permute-start.45 = (bf16[256,2304]{1,0:T(8,128)(2,1)}, bf16[256,2304]{1,0:T(8,128)(2,1)}, u32[]{:S(2)}, u32[]{:S(2)}) collective-permute-start(bf16[256,2304]{1,0:T(8,128)(2,1)} %get-tuple-element.485), channel_id=1, source_target_pairs={{0,16},{16,0},{1,17},{17,1},{2,18},{18,2},{3,19},{19,3},{4,20},{20... | collective-permute-start | bytes 3538952 | tf_op jit(solution)/shard_map/ppermute | solution.py:53
  249.2 23.4 %collective-permute-start.46 = (bf16[256,1152]{1,0:T(8,128)(2,1)S(1)}, bf16[256,1152]{1,0:T(8,128)(2,1)}, u32[]{:S(2)}, u32[]{:S(2)}) collective-permute-start(bf16[256,1152]{1,0:T(8,128)(2,1)S(1)} %bitcast.174), channel_id=1, source_target_pairs={{0,16},{16,0},{1,17},{17,1},{2,18},{18,2},{3,19},{19,3},{4,20},{20... | collective-permute-start | bytes 1769480 | tf_op jit(solution)/shard_map/ppermute | solution.py:53
  261.2 65.4 %collective-permute-start.47 = (bf16[256,4608]{1,0:T(8,128)(2,1)}, bf16[256,4608]{1,0:T(8,128)(2,1)}, u32[]{:S(2)}, u32[]{:S(2)}) collective-permute-start(bf16[256,4608]{1,0:T(8,128)(2,1)} %fusion.12), channel_id=1, source_target_pairs={{0,16},{16,0},{1,17},{17,1},{2,18},{18,2},{3,19},{19,3},{4,20},{20... | collective-permute-start | bytes 7077896 | tf_op jit(solution)/shard_map/ppermute | solution.py:53
  326.5 60.0 %all-to-all-start.5 = ((bf16[16,1,3,72,256]{4,3,2,1,0:T(8,128)(2,1)}), bf16[16,1,3,72,256]{4,3,2,1,0:T(8,128)(2,1)}, u32[]{:S(2)}, u32[]{:S(2)}) async-start(bf16[16,1,3,72,256]{4,3,2,1,0:T(8,128)(2,1)} %attend_back.1), calls=%async_computation.5 | async-start | bytes 3538944 | tf_op jit(solution)/shard_map/all_to_all | solution.py:352
  331.1 109.6 %all-gather.14.cloned.1.call-start = ((), (), s32[]{:S(2)}) async-start(), calls=%async_computation.12 | async-start | bytes 5640192 | tf_op jit(solution)/shard_map/all_gather | solution.py:602
  331.6 15.9 %collective-permute-start.48 = (bf16[256,1152]{1,0:T(8,128)(2,1)}, bf16[256,1152]{1,0:T(8,128)(2,1)}, u32[]{:S(2)}, u32[]{:S(2)}) collective-permute-start(bf16[256,1152]{1,0:T(8,128)(2,1)} %bitcast.196), channel_id=1, source_target_pairs={{0,16},{16,0},{1,17},{17,1},{2,18},{18,2},{3,19},{19,3},{4,20},{20... | collective-permute-start | bytes 1769480 | tf_op jit(solution)/shard_map/ppermute | solution.py:53
  386.6 249.9 %all-reduce.5.cloned.1.call-start = ((), (), s32[]{:S(2)}) async-start(), calls=%async_computation.13 | async-start | bytes 10616832 | tf_op jit(solution)/shard_map/psum | solution.py:606
  391.5 40.9 %collective-permute-start.51 = (bf16[3456,256]{1,0:T(8,128)(2,1)}, bf16[3456,256]{1,0:T(8,128)(2,1)}, u32[]{:S(2)}, u32[]{:S(2)}) collective-permute-start(bf16[3456,256]{1,0:T(8,128)(2,1)} %bitcast.30), channel_id=1, source_target_pairs={{0,16},{16,0},{1,17},{17,1},{2,18},{18,2},{3,19},{19,3},{4,20},{20... | collective-permute-start | bytes 5308424 | tf_op jit(solution)/shard_map/ppermute | solution.py:53
  441.9 27.4 %all-to-all-start = ((bf16[16,11,1152]{2,1,0:T(8,128)(2,1)}), bf16[16,11,1152]{2,1,0:T(8,128)(2,1)S(1)}, u32[]{:S(2)}, u32[]{:S(2)}) async-start(bf16[16,11,1152]{2,1,0:T(8,128)(2,1)} %copy.153), calls=%async_computation | async-start | bytes 1179648 | tf_op jit(solution)/shard_map/while/body/all_to_all | solution.py:352
  447.9 14.0 %collective-permute-start.8 = (bf16[288,1152]{1,0:T(8,128)(2,1)S(1)}, bf16[288,1152]{1,0:T(8,128)(2,1)}, u32[]{:S(2)}, u32[]{:S(2)}) collective-permute-start(bf16[288,1152]{1,0:T(8,128)(2,1)S(1)} %constant_dynamic-slice_fusion.31), channel_id=1, source_target_pairs={{0,4},{4,0},{8,12},{12,8},{1,5},{5,1},{9,13},{13,9},{2,6},{6,2},{1... | collective-permute-start | bytes 1990664 | tf_op jit(solution)/shard_map/while/body/ppermute | solution.py:309
  449.2 15.1 %collective-permute-start.15 = (bf16[288,1152]{1,0:T(8,128)(2,1)}, bf16[288,1152]{1,0:T(8,128)(2,1)}, u32[]{:S(2)}, u32[]{:S(2)}) collective-permute-start(bf16[288,1152]{1,0:T(8,128)(2,1)} %constant_dynamic-slice_fusion.34), channel_id=1, source_target_pairs={{0,4},{4,0},{8,12},{12,8},{1,5},{5,1},{9,13},{13,9},{2,6},{6,2},{1... | collective-permute-start | bytes 1990664 | tf_op jit(solution)/shard_map/while/body/ppermute | solution.py:309
  450.2 17.8 %collective-permute-start.19 = (bf16[288,1152]{1,0:T(8,128)(2,1)}, bf16[288,1152]{1,0:T(8,128)(2,1)}, u32[]{:S(2)}, u32[]{:S(2)}) collective-permute-start(bf16[288,1152]{1,0:T(8,128)(2,1)} %constant_dynamic-slice_fusion.37), channel_id=1, source_target_pairs={{0,4},{4,0},{8,12},{12,8},{1,5},{5,1},{9,13},{13,9},{2,6},{6,2},{1... | collective-permute-start | bytes 1990664 | tf_op jit(solution)/shard_map/while/body/ppermute | solution.py:309
  460.2 19.3 %collective-permute-start.2 = (bf16[144,1152]{1,0:T(8,128)(2,1)}, bf16[144,1152]{1,0:T(8,128)(2,1)}, u32[]{:S(2)}, u32[]{:S(2)}) collective-permute-start(bf16[144,1152]{1,0:T(8,128)(2,1)} %constant_dynamic-slice_fusion.29), channel_id=1, source_target_pairs={{0,8},{4,12},{8,0},{12,4},{1,9},{5,13},{9,1},{13,5},{2,10},{6,14},... | collective-permute-start | bytes 995336 | tf_op jit(solution)/shard_map/while/body/ppermute | solution.py:309
  463.9 22.8 %collective-permute-start.9 = (bf16[144,1152]{1,0:T(8,128)(2,1)}, bf16[144,1152]{1,0:T(8,128)(2,1)}, u32[]{:S(2)}, u32[]{:S(2)}) collective-permute-start(bf16[144,1152]{1,0:T(8,128)(2,1)} %constant_dynamic-slice_fusion.32), channel_id=1, source_target_pairs={{0,8},{4,12},{8,0},{12,4},{1,9},{5,13},{9,1},{13,5},{2,10},{6,14},... | collective-permute-start | bytes 995336 | tf_op jit(solution)/shard_map/while/body/ppermute | solution.py:309
  466.4 31.5 %collective-permute-start.16 = (bf16[144,1152]{1,0:T(8,128)(2,1)}, bf16[144,1152]{1,0:T(8,128)(2,1)}, u32[]{:S(2)}, u32[]{:S(2)}) collective-permute-start(bf16[144,1152]{1,0:T(8,128)(2,1)} %constant_dynamic-slice_fusion.35), channel_id=1, source_target_pairs={{0,8},{4,12},{8,0},{12,4},{1,9},{5,13},{9,1},{13,5},{2,10},{6,14},... | collective-permute-start | bytes 995336 | tf_op jit(solution)/shard_map/while/body/ppermute | solution.py:309
  471.6 34.0 %collective-permute-start.20 = (bf16[144,1152]{1,0:T(8,128)(2,1)}, bf16[144,1152]{1,0:T(8,128)(2,1)}, u32[]{:S(2)}, u32[]{:S(2)}) collective-permute-start(bf16[144,1152]{1,0:T(8,128)(2,1)} %constant_dynamic-slice_fusion.38), channel_id=1, source_target_pairs={{0,8},{4,12},{8,0},{12,4},{1,9},{5,13},{9,1},{13,5},{2,10},{6,14},... | collective-permute-start | bytes 995336 | tf_op jit(solution)/shard_map/while/body/ppermute | solution.py:309
  474.9 86.3 %all-to-all-start.1 = ((bf16[16,2,11,1152]{3,1,2,0:T(2,128)(2,1)}), bf16[16,2,11,1152]{3,1,2,0:T(2,128)(2,1)S(1)}, u32[]{:S(2)}, u32[]{:S(2)}) async-start(bf16[16,2,11,1152]{3,1,2,0:T(2,128)(2,1)} %broadcast_in_dim.51), calls=%async_computation.1 | async-start | bytes 1622016 | tf_op jit(solution)/shard_map/while/body/all_to_all | solution.py:352
  480.7 29.1 %collective-permute-start.3 = (bf16[72,1152]{1,0:T(8,128)(2,1)S(1)}, bf16[72,1152]{1,0:T(8,128)(2,1)S(1)}, u32[]{:S(2)}, u32[]{:S(2)}) collective-permute-start(bf16[72,1152]{1,0:T(8,128)(2,1)S(1)} %constant_dynamic-slice_fusion.30), channel_id=1, source_target_pairs={{0,1},{1,0},{2,3},{3,2},{4,5},{5,4},{6,7},{7,6},{8,9},{9,8},{10,11... | collective-permute-start | bytes 497672 | tf_op jit(solution)/shard_map/while/body/ppermute | solution.py:309
  487.8 30.4 %collective-permute-start.10 = (bf16[72,1152]{1,0:T(8,128)(2,1)S(1)}, bf16[72,1152]{1,0:T(8,128)(2,1)S(1)}, u32[]{:S(2)}, u32[]{:S(2)}) collective-permute-start(bf16[72,1152]{1,0:T(8,128)(2,1)S(1)} %constant_dynamic-slice_fusion.33), channel_id=1, source_target_pairs={{0,1},{1,0},{2,3},{3,2},{4,5},{5,4},{6,7},{7,6},{8,9},{9,8},{10,11... | collective-permute-start | bytes 497672 | tf_op jit(solution)/shard_map/while/body/ppermute | solution.py:309
  499.0 23.1 %collective-permute-start.17 = (bf16[72,1152]{1,0:T(8,128)(2,1)S(1)}, bf16[72,1152]{1,0:T(8,128)(2,1)S(1)}, u32[]{:S(2)}, u32[]{:S(2)}) collective-permute-start(bf16[72,1152]{1,0:T(8,128)(2,1)S(1)} %constant_dynamic-slice_fusion.36), channel_id=1, source_target_pairs={{0,1},{1,0},{2,3},{3,2},{4,5},{5,4},{6,7},{7,6},{8,9},{9,8},{10,11... | collective-permute-start | bytes 497672 | tf_op jit(solution)/shard_map/while/body/ppermute | solution.py:309
  506.7 18.9 %collective-permute-start.21 = (bf16[72,1152]{1,0:T(8,128)(2,1)S(1)}, bf16[72,1152]{1,0:T(8,128)(2,1)S(1)}, u32[]{:S(2)}, u32[]{:S(2)}) collective-permute-start(bf16[72,1152]{1,0:T(8,128)(2,1)S(1)} %constant_dynamic-slice_fusion.39), channel_id=1, source_target_pairs={{0,1},{1,0},{2,3},{3,2},{4,5},{5,4},{6,7},{7,6},{8,9},{9,8},{10,11... | collective-permute-start | bytes 497672 | tf_op jit(solution)/shard_map/while/body/ppermute | solution.py:309
  509.9 15.8 %collective-permute-start.4 = (bf16[72,1152]{1,0:T(8,128)(2,1)S(1)}, bf16[72,1152]{1,0:T(8,128)(2,1)S(1)}, u32[]{:S(2)}, u32[]{:S(2)}) collective-permute-start(bf16[72,1152]{1,0:T(8,128)(2,1)S(1)} %add_convert_fusion.38), channel_id=1, source_target_pairs={{0,2},{1,3},{2,0},{3,1},{4,6},{5,7},{6,4},{7,5},{8,10},{9,11},{10,... | collective-permute-start | bytes 497672 | tf_op jit(solution)/shard_map/while/body/ppermute | solution.py:309
  518.2 26.8 %collective-permute-start.11 = (bf16[72,1152]{1,0:T(8,128)(2,1)S(1)}, bf16[72,1152]{1,0:T(8,128)(2,1)S(1)}, u32[]{:S(2)}, u32[]{:S(2)}) collective-permute-start(bf16[72,1152]{1,0:T(8,128)(2,1)S(1)} %add_convert_fusion.42), channel_id=1, source_target_pairs={{0,2},{1,3},{2,0},{3,1},{4,6},{5,7},{6,4},{7,5},{8,10},{9,11},{10,... | collective-permute-start | bytes 497672 | tf_op jit(solution)/shard_map/while/body/ppermute | solution.py:309
  522.2 27.7 %collective-permute-start.18 = (bf16[72,1152]{1,0:T(8,128)(2,1)S(1)}, bf16[72,1152]{1,0:T(8,128)(2,1)S(1)}, u32[]{:S(2)}, u32[]{:S(2)}) collective-permute-start(bf16[72,1152]{1,0:T(8,128)(2,1)S(1)} %add_convert_fusion.46), channel_id=1, source_target_pairs={{0,2},{1,3},{2,0},{3,1},{4,6},{5,7},{6,4},{7,5},{8,10},{9,11},{10,... | collective-permute-start | bytes 497672 | tf_op jit(solution)/shard_map/while/body/ppermute | solution.py:309
  525.6 27.8 %collective-permute-start.22 = (bf16[72,1152]{1,0:T(8,128)(2,1)S(1)}, bf16[72,1152]{1,0:T(8,128)(2,1)S(1)}, u32[]{:S(2)}, u32[]{:S(2)}) collective-permute-start(bf16[72,1152]{1,0:T(8,128)(2,1)S(1)} %add_convert_fusion.50), channel_id=1, source_target_pairs={{0,2},{1,3},{2,0},{3,1},{4,6},{5,7},{6,4},{7,5},{8,10},{9,11},{10,... | collective-permute-start | bytes 497672 | tf_op jit(solution)/shard_map/while/body/ppermute | solution.py:309
  525.8 24.9 %collective-permute-start.5 = (bf16[72,1152]{1,0:T(8,128)(2,1)S(1)}, bf16[72,1152]{1,0:T(8,128)(2,1)S(1)}, u32[]{:S(2)}, u32[]{:S(2)}) collective-permute-start(bf16[72,1152]{1,0:T(8,128)(2,1)S(1)} %add_convert_fusion.39), channel_id=1, source_target_pairs={{0,1},{1,0},{2,3},{3,2},{4,5},{5,4},{6,7},{7,6},{8,9},{9,8},{10,11... | collective-permute-start | bytes 497672 | tf_op jit(solution)/shard_map/while/body/ppermute | solution.py:309
  557.0 31.5 %collective-permute-start.13 = (bf16[144,1152]{1,0:T(8,128)(2,1)S(1)}, bf16[144,1152]{1,0:T(8,128)(2,1)}, u32[]{:S(2)}, u32[]{:S(2)}) collective-permute-start(bf16[144,1152]{1,0:T(8,128)(2,1)S(1)} %maximum_select_fusion.27), channel_id=1, source_target_pairs={{0,8},{4,12},{8,0},{12,4},{1,9},{5,13},{9,1},{13,5},{2,10},{6,14},... | collective-permute-start | bytes 995336 | tf_op jit(solution)/shard_map/while/body/ppermute | solution.py:309
  561.1 59.3 %collective-permute-start.7 = (bf16[288,1152]{1,0:T(8,128)(2,1)S(1)}, bf16[288,1152]{1,0:T(8,128)(2,1)}, u32[]{:S(2)}, u32[]{:S(2)}) collective-permute-start(bf16[288,1152]{1,0:T(8,128)(2,1)S(1)} %maximum_select_fusion.25), channel_id=1, source_target_pairs={{0,4},{4,0},{8,12},{12,8},{1,5},{5,1},{9,13},{13,9},{2,6},{6,2},{1... | collective-permute-start | bytes 1990664 | tf_op jit(solution)/shard_map/while/body/ppermute | solution.py:309
  571.9 15.9 %collective-permute-start.23 = (f32[16,576]{1,0:T(8,128)}, f32[16,576]{1,0:T(8,128)S(1)}, u32[]{:S(2)}, u32[]{:S(2)}) collective-permute-start(f32[16,576]{1,0:T(8,128)} %slice.366), channel_id=1, source_target_pairs={{0,16},{16,0},{1,17},{17,1},{2,18},{18,2},{3,19},{19,3},{4,20},{20... | collective-permute-start | bytes 110600 | tf_op jit(solution)/shard_map/while/body/ppermute | solution.py:58
  589.8 33.4 %collective-permute-start.14 = (bf16[288,1152]{1,0:T(8,128)(2,1)S(1)}, bf16[288,1152]{1,0:T(8,128)(2,1)S(1)}, u32[]{:S(2)}, u32[]{:S(2)}) collective-permute-start(bf16[288,1152]{1,0:T(8,128)(2,1)S(1)} %maximum_select_fusion.28), channel_id=1, source_target_pairs={{0,4},{4,0},{8,12},{12,8},{1,5},{5,1},{9,13},{13,9},{2,6},{6,2},{1... | collective-permute-start | bytes 1990664 | tf_op jit(solution)/shard_map/while/body/ppermute | solution.py:309
  590.1 16.0 %collective-permute-start.27 = (bf16[72,1152]{1,0:T(8,128)(2,1)S(1)}, bf16[72,1152]{1,0:T(8,128)(2,1)S(1)}, u32[]{:S(2)}, u32[]{:S(2)}) collective-permute-start(bf16[72,1152]{1,0:T(8,128)(2,1)S(1)} %copy-done.18), channel_id=1, source_target_pairs={{0,1},{1,0},{2,3},{3,2},{4,5},{5,4},{6,7},{7,6},{8,9},{9,8},{10,11... | collective-permute-start | bytes 497672 | tf_op jit(solution)/shard_map/while/body/ppermute | solution.py:309
  599.2 15.1 %collective-permute-start.25 = (bf16[144,1152]{1,0:T(8,128)(2,1)S(1)}, bf16[144,1152]{1,0:T(8,128)(2,1)S(1)}, u32[]{:S(2)}, u32[]{:S(2)}) collective-permute-start(bf16[144,1152]{1,0:T(8,128)(2,1)S(1)} %maximum_select_fusion.30), channel_id=1, source_target_pairs={{0,8},{4,12},{8,0},{12,4},{1,9},{5,13},{9,1},{13,5},{2,10},{6,14},... | collective-permute-start | bytes 995336 | tf_op jit(solution)/shard_map/while/body/ppermute | solution.py:309
  606.1 14.1 %collective-permute-start.28 = (bf16[144,1152]{1,0:T(8,128)(2,1)S(1)}, bf16[144,1152]{1,0:T(8,128)(2,1)S(1)}, u32[]{:S(2)}, u32[]{:S(2)}) collective-permute-start(bf16[144,1152]{1,0:T(8,128)(2,1)S(1)} %maximum_select_fusion.33), channel_id=1, source_target_pairs={{0,8},{4,12},{8,0},{12,4},{1,9},{5,13},{9,1},{13,5},{2,10},{6,14},... | collective-permute-start | bytes 995336 | tf_op jit(solution)/shard_map/while/body/ppermute | solution.py:309
  (101 other events, 575.2 us)
Sparse Core Ops, SparseCore 0:
  19.3 53.0 all-gather.5
  74.6 51.6 all-gather.7
  128.6 69.3 all-gather.9
  200.1 39.0 all-gather.11
  280.2 99.4 reduce-scatter.1
  386.7 53.9 all-gather.13
  444.9 182.3 all-reduce.4
